TPU v7x, 32 devices: a whole 2x2x4 slice. The times are simulated.
32 devices in a mesh: section: 2 (over core), dp: 16 (over z, y, x).
Axes of the slice: x: 2, y: 2, z: 4, core: 2. Of those that a mesh axis runs over, the one named last changes fastest.
Arguments:
- pixels: bfloat16 [32, 196, 768], P('dp'), may hold values from -6 to 6
- ctx_idx: int32 [32, 128], P('dp'), may hold values from 0 to 195, as said below
- ctx_len: int32 [32], P('dp'), may hold values from 64 to 128
- tgt_idx: int32 [32, 4, 36], P('dp'), may hold values from 0 to 195, as said below
- tgt_len: int32 [32, 4], P('dp'), may hold values from 4 to 36, as said below
- slot_of: int32 [68], replicated, may hold values from 0 to 79, as said below
- weights: float32 [2, 80, 384, 384], P('section', 'dp')
- first_moment: float32 [2, 80, 384, 384], P('section', 'dp'), may hold values from -0.001953125 to 0.001953125
- second_moment: float32 [2, 80, 384, 384], P('section', 'dp'), may hold values from 4.9773828e-08 to 7.9638124e-07
- left_basis: float32 [2, 80, 384, 384], P('section', 'dp'), as said below
- right_basis: float32 [2, 80, 384, 384], P('section', 'dp'), as said below
- left_stats: float32 [2, 80, 384, 384], P('section', 'dp'), as said below
- right_stats: float32 [2, 80, 384, 384], P('section', 'dp'), as said below
- vectors: float32 [2, 18432], P('section')
- vector_first: float32 [2, 18432], P('section'), may hold values from -0.005859375 to 0.005859375
- vector_second: float32 [2, 18432], P('section'), may hold values from 9.9547655e-08 to 6.37105e-06
Outputs:
- loss_sum: float32 [], replicated
- loss_count: float32 [], replicated
- grad_norm: float32 [], replicated
- new_weights: float32 [2, 80, 384, 384], P('section', 'dp')
- new_first: float32 [2, 80, 384, 384], P('section', 'dp')
- new_second: float32 [2, 80, 384, 384], P('section', 'dp')
- new_left: float32 [2, 80, 384, 384], P('section', 'dp')
- new_right: float32 [2, 80, 384, 384], P('section', 'dp')
- new_left_stats: float32 [2, 80, 384, 384], P('section', 'dp')
- new_right_stats: float32 [2, 80, 384, 384], P('section', 'dp')
- new_vectors: float32 [2, 18432], P('section')
- new_vector_first: float32 [2, 18432], P('section')
- new_vector_second: float32 [2, 18432], P('section')
Inputs may be any that keep to these rules, and one draw needn't show every extreme that they name: `ctx_idx`: each image's 128 context patch numbers are distinct; the first ctx_len of them count. `tgt_idx`: each target block is a rectangle of the 14 x 14 patch grid, listed row by row; entries past its length are 0. `tgt_len`: A block's height times its width, with heights 2 to 6 and widths 2 to 6. `slot_of`: distinct slot numbers. `left_basis`: each block is orthogonal. `right_basis`: each block is orthogonal. `left_stats`: each block is symmetric positive definite. `right_stats`: each block is symmetric positive definite.
All inputs are finite; a program needn't handle non-finite values.
Results may differ from a plain program's by a relative error of at most 0.00065.
The roundings to bfloat16 on the way count: a program that leaves them out, or rounds other values in their place, can miss the bound.
Values may be sent and summed in bfloat16 or wider, within the bound.
No kernel may reach another device: no remote copies, remote signals or barrier semaphores. Data moves between devices by JAX's collectives and lax.ppermute only.
A program may use at most 384 MiB of HBM per device.

v0:
```python
import functools
import math

import jax
import jax.numpy as jnp
from jax import lax
from jax.experimental import pallas as pl
from jax.experimental.pallas import tpu as pltpu
from jax.sharding import PartitionSpec as P

D = 768
FF = 3072
H = 12
PD = 384
PFF = 1536
PH = 12
PIX = 768
GRID = 14
NT = 4
LC = 128
STEP = 10
P_SIZE = 196
LT = 36
NBE = 52
NBP = 16
VE = 11520
VP = 6912
VW = 18432


NORM_EPS = 1e-06
ADAM_EPS = 1e-08
BETA_FIRST = 0.5
BETA_SECOND = 0.5
BETA_STATS = 0.95
RATE_MATRIX = 0.02
RATE_VECTOR = 0.05
DECAY_MATRIX = 0.04
EMA_KEEP = 0.996
CLIP_LIMIT = 1.0
NEG_FILL = -1000000000.0
WIRE = jnp.float16
WIRE_TOP = 16384.0
f32 = jnp.float32
bf = jnp.bfloat16


def from_behind(shard, axis, by):
    size = lax.axis_size(axis)
    pairs = [(i, i + by) for i in range(size) if 0 <= i + by < size]
    return lax.ppermute(shard, axis, pairs)


def enc_shapes():
    return [(PIX, D), (D, 3 * D), (D, D), (D, FF), (FF, D)]


def pred_shapes():
    return [(D, PD), (PD, 3 * PD), (PD, PD), (PD, PFF), (PFF, PD), (PD, D)]


def enc_lengths():
    return [D] * 8 + [FF, D, D, D]


def pred_lengths():
    return [PD] * 8 + [PFF, PD, PD, PD, D, PD]


def sincos(width):
    quarter = width // 4
    frequency = 1.0 / 10000.0 ** (jnp.arange(quarter, dtype=jnp.float32) / quarter)
    cell_ids = jnp.arange(P_SIZE)
    row_pos = (cell_ids // GRID).astype(jnp.float32)[:, None] * frequency
    column_pos = (cell_ids % GRID).astype(jnp.float32)[:, None] * frequency
    return jnp.concatenate(
        [jnp.sin(row_pos), jnp.cos(row_pos), jnp.sin(column_pos), jnp.cos(column_pos)], 1
    )


DIMS = {"nn": (1, 0), "nt": (1, 1), "tn": (0, 0)}

def parts_of(a, count):
    found = []
    for index in range(count):
        piece = a.astype(bf)
        found.append(piece)
        if index + 1 < count:
            a = a - piece.astype(f32)
    return found

def product(left, right, form, pairs):
    ld, rd = DIMS[form]
    lhs = jnp.concatenate([left[i] for i, _ in pairs], ld)
    rhs = jnp.concatenate([right[j] for _, j in pairs], rd)
    return lax.dot_general(lhs, rhs, (((ld,), (rd,)), ((), ())), preferred_element_type=f32)

THREE = ((0, 1), (1, 0), (0, 0))
SIX = ((0, 2), (2, 0), (1, 1), (0, 1), (1, 0), (0, 0))
def mul3(left, right, form="nn"):
    return product(left, right, form, THREE)
def mul6(left, right, form="nn"):
    return product(left, right, form, SIX)

def invert_factors(mats):
    n = mats[0].shape[0]
    lane = lax.broadcasted_iota(jnp.int32, (8, n), 1)
    sub = lax.broadcasted_iota(jnp.int32, (8, n), 0)
    groups = [[a[8 * t : 8 * t + 8, :] for t in range(n // 8)] for a in mats]
    for j in range(n):
        top, at_row = divmod(j, 8)
        here = lane == j
        pick = jnp.full((8, n), j, jnp.int32)
        for tiles in groups:
            column = jnp.take_along_axis(tiles[top], pick, axis=1)
            pivot = jnp.broadcast_to(column[at_row : at_row + 1, :], (8, n))
            row = jnp.broadcast_to(tiles[top][at_row : at_row + 1, :], (8, n))
            scaled = jnp.where(here, 1.0, row) * (1.0 / pivot)
            for t in range(top, n // 8):
                if t > top:
                    column = jnp.take_along_axis(tiles[t], pick, axis=1)
                fresh = jnp.where(here, 0.0, tiles[t]) - column * scaled
                tiles[t] = jnp.where(sub > at_row, fresh, tiles[t]) if t == top else fresh
    results = []
    for tiles in groups:
        rows = []
        for t in range(n // 8):
            at = sub + 8 * t
            pivots = jnp.sum(jnp.where(lane == at, tiles[t], 0.0), axis=1, keepdims=True)
            unit = jnp.where(lane < at, tiles[t], jnp.where(lane == at, 1.0, 0.0))
            rows.append(unit * lax.rsqrt(pivots))
        results.append(jnp.concatenate(rows, 0))
    return results

def first_kernel(flag, factor, g_ref, w_ref, m_ref, v_ref, l_ref, r_ref, e_ref, f_ref,
                 w_out, m_out, v_out, e_out, f_out, base_out, gram_out):
    on = flag[pl.program_id(0)] != 0

    @pl.when(jnp.logical_not(on))
    def keep():
        for source, target in ((w_ref, w_out), (m_ref, m_out), (v_ref, v_out), (e_ref, e_out), (f_ref, f_out)):
            target[...] = source[...]

    @pl.when(on)
    def update():
        correct_one = 1.0 - BETA_FIRST**STEP
        correct_two = 1.0 - BETA_SECOND**STEP
        grad = parts_of(g_ref[0] * factor[0], 3)
        left = parts_of(l_ref[0], 3)
        right = parts_of(r_ref[0], 3)
        rotated = mul3(left, parts_of(mul3(grad, right), 2), "tn")
        moment = BETA_FIRST * m_ref[0] + (1.0 - BETA_FIRST) * rotated
        second = BETA_SECOND * v_ref[0] + (1.0 - BETA_SECOND) * rotated * rotated
        m_out[0] = moment
        v_out[0] = second
        normed = moment / correct_one / (jnp.sqrt(second / correct_two) + ADAM_EPS)
        weight = w_ref[0]
        step = mul3(left, parts_of(mul3(parts_of(normed, 2), right, "nt"), 2))
        w_out[0] = weight - RATE_MATRIX * (step + DECAY_MATRIX * weight)
        for index, (stat, target, basis, form) in enumerate(
            ((e_ref, e_out, left, "nt"), (f_ref, f_out, right, "tn"))
        ):
            fresh = BETA_STATS * stat[0] + (1.0 - BETA_STATS) * mul6(grad, grad, form)
            target[0] = fresh
            moved = mul6(parts_of(fresh, 3), basis)
            base_out[0, index] = moved
            pieces = parts_of(moved, 3)
            gram_out[0, index] = mul6(pieces, pieces, "tn")

def factor_kernel(flag, base_ref, gram_ref, q_out, base, gram, inverse):
    blocks, edge = base_ref.shape[0], base_ref.shape[-1]
    panel = 128
    count = edge // panel
    base[...] = base_ref[...]
    gram[...] = gram_ref[...]

    def stage(k):
        at = pl.ds(panel * k, panel)
        start = panel * k
        spot = slice(start, start + panel)
        rest = slice(start + panel, edge)

        def block(b, carry):
            @pl.when(flag[b] != 0)
            def run():
                for side in range(2):
                    inv = parts_of(inverse[b, side], 3)
                    q = mul6(parts_of(base[b, side, :, spot], 3), inv, "nt")
                    q_out[b, side, :, spot] = q
                    if k + 1 < count:
                        p = parts_of(mul6(inv, parts_of(gram[b, side, spot, rest], 3)), 3)
                        gram[b, side, rest, rest] = gram[b, side, rest, rest] - mul6(p, p, "tn")
                        base[b, side, :, rest] = base[b, side, :, rest] - mul6(parts_of(q, 3), p)
            return carry

        lax.fori_loop(0, blocks, block, 0)

    def turn(k, carry):
        for which in range(count):
            @pl.when(k == which)
            def load():
                spot = slice(panel * which, panel * which + panel)
                for b in range(blocks):
                    for side in range(2):
                        inverse[b, side] = gram[b, side, spot, spot]
        mats = invert_factors([inverse[b, side] for b in range(blocks) for side in range(2)])
        for b in range(blocks):
            for side in range(2):
                inverse[b, side] = mats[2 * b + side]
        for which in range(count):
            @pl.when(k == which)
            def run():
                stage(which)
        return carry

    lax.fori_loop(0, count, turn, 0)

def last_kernel(flag, l_ref, r_ref, m_ref, q_ref, l_out, r_out, m_out):
    on = flag[pl.program_id(0)] != 0

    @pl.when(jnp.logical_not(on))
    def keep():
        l_out[...] = l_ref[...]
        r_out[...] = r_ref[...]
        m_out[...] = m_ref[...]

    @pl.when(on)
    def update():
        l_out[0] = q_ref[0, 0]
        r_out[0] = q_ref[0, 1]
        turn_left = mul3(parts_of(q_ref[0, 0], 2), parts_of(l_ref[0], 2), "tn")
        turn_right = mul3(parts_of(r_ref[0], 2), parts_of(q_ref[0, 1], 2), "tn")
        half = mul3(parts_of(turn_left, 2), parts_of(m_ref[0], 2))
        m_out[0] = mul3(parts_of(half, 2), parts_of(turn_right, 2))

PLAIN = (((1,), (0,)), ((), ()))
RIGHT_T = (((1,), (1,)), ((), ()))
LEFT_T = (((0,), (0,)), ((), ()))
ROOT_HALF = 0.7071067811865476
ROOT_TWO_PI = 2.5066282746310002


def mm(left, right, dims=PLAIN):
    return lax.dot_general(left, right, dims, preferred_element_type=f32)


def norm_parts(x):
    center = x - jnp.mean(x, -1, keepdims=True)
    inverse = lax.rsqrt(jnp.mean(center * center, -1, keepdims=True) + NORM_EPS)
    return center * inverse, inverse


def norm(x, gain, shift):
    return norm_parts(x)[0] * gain + shift


def norm_back(x, gain, grad):
    unit, inverse = norm_parts(x)
    grad_unit = grad * gain
    mean_one = jnp.mean(grad_unit, -1, keepdims=True)
    mean_two = jnp.mean(grad_unit * unit, -1, keepdims=True)
    back = inverse * (grad_unit - mean_one - unit * mean_two)
    return back, col_sum(grad * unit), col_sum(grad)


def col_sum(x):
    return jnp.sum(x, 0, keepdims=True)


def gelu(x):
    return 0.5 * x * (1.0 + lax.erf(x * ROOT_HALF))


def gelu_slope(x):
    return 0.5 * (1.0 + lax.erf(x * ROOT_HALF)) + x * jnp.exp(-0.5 * x * x) * (1.0 / ROOT_TWO_PI)


def offsets(lengths):
    result = [0]
    for length in lengths:
        result.append(result[-1] + length)
    return result


class Vec:
    def __init__(self, ref, lengths):
        self.ref, self.at = ref, offsets(lengths)

    def __getitem__(self, k):
        return self.ref[:, self.at[k] : self.at[k + 1]]

    def __setitem__(self, k, value):
        self.ref[:, self.at[k] : self.at[k + 1]] = value

    def part(self, k, start, size):
        return self.ref[:, pl.ds(pl.multiple_of(self.at[k] + start, 128), size)]

    def put_part(self, k, start, size, value):
        self.ref[:, pl.ds(pl.multiple_of(self.at[k] + start, 128), size)] = value


class Fetch:
    def __init__(self, pieces, places, j, spot, sem):
        self.pieces, self.spot, self.sem = pieces, spot, sem
        self.which, self.index = places[j], places[NBE + NBP + j]

    def copy(self, piece, index):
        return pltpu.make_async_copy(piece.at[index], self.spot, self.sem)

    def start(self):
        if len(self.pieces) == 1:
            self.copy(self.pieces[0], self.index).start()
        else:
            self.start_among(0, len(self.pieces))

    def start_among(self, low, high):
        if high - low == 1:
            self.copy(self.pieces[low], self.index).start()
            return
        middle = (low + high) // 2

        @pl.when(self.which < middle)
        def below():
            self.start_among(low, middle)

        @pl.when(self.which >= middle)
        def above():
            self.start_among(middle, high)

    def wait(self):
        self.copy(self.pieces[0], 0).wait()


def load_blocks(pieces, places, sems, first, shapes, targets):
    edge = pieces[0].shape[-1]
    groups = []
    j = first
    for (height, breadth), target in zip(shapes, targets):
        group = []
        for row in range(height // edge):
            for column in range(breadth // edge):
                if target is not None:
                    spot = target.at[pl.ds(row * edge, edge), pl.ds(column * edge, edge)]
                    group.append(Fetch(pieces, places, j, spot, sems.at[j]))
                j += 1
        groups.append(group)
    return groups


def start_all(groups):
    for group in groups:
        for copy in group:
            copy.start()


def wait_group(group):
    for copy in group:
        copy.wait()


def head_masks(rows, heads, width):
    lane = lax.broadcasted_iota(jnp.int32, (rows, 128), 1)
    size = width // heads
    return [(lane >= size * h) & (lane < size * h + size) for h in range(128 // size)]


def as_factors(masks):
    return [jnp.where(mask, 1.0, 0.0).astype(bf) for mask in masks]


def soft(scores, allowed):
    scores = jnp.where(allowed, scores, NEG_FILL)
    top = jnp.max(scores, -1, keepdims=True)
    raised = jnp.exp(scores - top)
    return raised * (1.0 / jnp.sum(raised, -1, keepdims=True))


def attend(q_ref, k_ref, v_ref, valid_ref, out_ref, heads):
    images, rows, width = q_ref.shape
    keys = k_ref.shape[1]
    masks = head_masks(rows, heads, width)
    factors = as_factors(masks)

    def group(p, carry):
        lanes = pl.ds(pl.multiple_of(128 * p, 128), 128)
        for i in range(images):
            q, k, v = q_ref[i, :, lanes], k_ref[i, :, lanes], v_ref[i, :, lanes]
            allowed = jnp.broadcast_to(valid_ref[i], (rows, keys)) > 0.0
            result = jnp.zeros((rows, 128), f32)
            for mask, factor in zip(masks, factors):
                probs = soft(mm(q * factor, k, RIGHT_T), allowed)
                result = jnp.where(mask, mm(probs.astype(bf), v), result)
            out_ref[i, :, lanes] = result.astype(bf)
        return carry

    lax.fori_loop(0, width // 128, group, 0)


def attend_back(q_ref, k_ref, v_ref, valid_ref, go_ref, dq_ref, dk_ref, dv_ref, heads):
    images, rows, width = q_ref.shape
    keys = k_ref.shape[1]
    masks = head_masks(rows, heads, width)
    key_masks = head_masks(keys, heads, width)
    factors = as_factors(masks)
    scale = 1.0 / math.sqrt(width // heads)

    def group(p, carry):
        lanes = pl.ds(pl.multiple_of(128 * p, 128), 128)
        for i in range(images):
            q, k, v = q_ref[i, :, lanes], k_ref[i, :, lanes], v_ref[i, :, lanes]
            go = go_ref[i, :, lanes]
            allowed = jnp.broadcast_to(valid_ref[i], (rows, keys)) > 0.0
            dq = jnp.zeros((rows, 128), f32)
            dk = jnp.zeros((keys, 128), f32)
            dv = jnp.zeros((keys, 128), f32)
            for mask, key_mask, factor in zip(masks, key_masks, factors):
                probs = soft(mm(q * factor, k, RIGHT_T), allowed)
                dv = jnp.where(key_mask, mm(probs.astype(bf), go, LEFT_T), dv)
                dprobs = mm(go * factor, v, RIGHT_T)
                dscores = probs * (dprobs - jnp.sum(dprobs * probs, -1, keepdims=True))
                low = dscores.astype(bf)
                dq = jnp.where(mask, mm(low, k) * scale, dq)
                dk = jnp.where(key_mask, mm(low, q, LEFT_T), dk)
            dq_ref[i, :, lanes] = dq
            dk_ref[i, :, lanes] = dk
            dv_ref[i, :, lanes] = dv
        return carry

    lax.fori_loop(0, width // 128, group, 0)


def split_rows(ref, value):
    images, rows, _ = ref.shape
    for i in range(images):
        ref[i] = value[rows * i : rows * i + rows].astype(ref.dtype)


def flat(ref):
    return jnp.concatenate([ref[i] for i in range(ref.shape[0])], 0)


STRIP = 384


def feed_forward(normed, mid, up, down, vec, pre_ref, acc_ref):
    acc_ref[...] = mid

    def strip(c, carry):
        lanes = pl.ds(pl.multiple_of(c * STRIP, 128), STRIP)
        pre = mm(normed, up[:, lanes]) + vec.part(8, c * STRIP, STRIP)
        if pre_ref is not None:
            pre_ref[:, lanes] = pre
        acc_ref[...] += mm(gelu(pre).astype(bf), down[lanes, :])
        return carry

    lax.fori_loop(0, up.shape[1] // STRIP, strip, 0)
    return acc_ref[...] + vec[9]


def encoder_kernel(
    slots, table, rows_ref, pos_ref, valid_ref, vec_ref,
    z_out, e_out, q_out, k_out, v_out, att_out, mid_out, pre_out, hid_out,
    wp, wqkv, wo, w1, w2, acc, sems,
):
    vec = Vec(vec_ref, enc_lengths())
    groups = load_blocks(table, slots, sems, 0, enc_shapes(), (wp, wqkv, wo, w1, w2))
    start_all(groups)
    wait_group(groups[0])
    e = mm(rows_ref[...], wp[...]) + vec[0] + pos_ref[...]
    e_out[...] = e
    normed = norm(e, vec[1], vec[2]).astype(bf)
    wait_group(groups[1])
    split_rows(q_out, (mm(normed, wqkv[:, :D]) + vec[3]) * (1.0 / math.sqrt(D // H)))
    split_rows(k_out, mm(normed, wqkv[:, D : 2 * D]))
    split_rows(v_out, mm(normed, wqkv[:, 2 * D :]) + vec[4])
    attend(q_out, k_out, v_out, valid_ref, att_out, H)
    wait_group(groups[2])
    mid = e + mm(flat(att_out), wo[...]) + vec[5]
    mid_out[...] = mid
    hidden = norm(mid, vec[6], vec[7]).astype(bf)
    wait_group(groups[3])
    wait_group(groups[4])
    hid = feed_forward(hidden, mid, w1, w2, vec, pre_out, acc)
    hid_out[...] = hid
    z_out[...] = norm(hid, vec[10], vec[11]).astype(bf)


def target_kernel(
    slots, table, all_ref, pos_all_ref, some_ref, pos_some_ref, valid_ref, vec_ref,
    out_ref, wp, wqkv, wo, w1, w2, q, k, v, att, acc, sems,
):
    vec = Vec(vec_ref, enc_lengths())
    groups = load_blocks(table, slots, sems, 0, enc_shapes(), (wp, wqkv, wo, w1, w2))
    start_all(groups)
    wait_group(groups[0])
    e = mm(all_ref[...], wp[...]) + vec[0] + pos_all_ref[...]
    normed = norm(e, vec[1], vec[2]).astype(bf)
    wait_group(groups[1])
    split_rows(k, mm(normed, wqkv[:, D : 2 * D]))
    split_rows(v, mm(normed, wqkv[:, 2 * D :]) + vec[4])
    e = mm(some_ref[...], wp[...]) + vec[0] + pos_some_ref[...]
    normed = norm(e, vec[1], vec[2]).astype(bf)
    split_rows(q, (mm(normed, wqkv[:, :D]) + vec[3]) * (1.0 / math.sqrt(D // H)))
    attend(q, k, v, valid_ref, att, H)
    wait_group(groups[2])
    mid = e + mm(flat(att), wo[...]) + vec[5]
    hidden = norm(mid, vec[6], vec[7]).astype(bf)
    wait_group(groups[3])
    wait_group(groups[4])
    hid = feed_forward(hidden, mid, w1, w2, vec, None, acc)
    out_ref[...] = norm_parts(norm(hid, vec[10], vec[11]))[0]


def put_block(ref, value, j, depth):
    edge = value.shape[-1]
    if depth % 8:
        ref[j] = value
    else:
        ref[:, depth * j : depth * j + depth, :] = value.reshape(edge // depth, depth, edge)


def raise_top(top_ref, value):
    top_ref[...] = jnp.maximum(top_ref[...], jnp.max(jnp.abs(value), 0, keepdims=True))


def predictor_kernel(
    depth, slots, table, z_ref, pos_c_ref, pos_t_ref, valid_ref, tgt_ref, tmask_ref, vec_ref,
    dz_out, flow_a, flow_b, vec_out, loss_out, top_out,
    win, wqkv, wo, w1, w2, wout, q, k, v, att, go, dq, dk, dv, pre_ref, act_ref, dpre_ref, acc, sems,
):
    vec, grads = Vec(vec_ref, pred_lengths()), Vec(vec_out, pred_lengths())
    edge = table[0].shape[-1]
    half = flow_split(NBP)
    images = z_ref.shape[0] // LC
    groups = load_blocks(table, slots, sems, NBE, pred_shapes(), (win, wqkv, wo, w1, w2, wout))
    start_all(groups)
    for group in groups:
        wait_group(group)
    firsts = offsets([h * b // (edge * edge) for h, b in pred_shapes()])

    def store(index, matrix):
        for row in range(matrix.shape[0] // edge):
            for column in range(matrix.shape[1] // edge):
                j = firsts[index] + row * (pred_shapes()[index][1] // edge) + column
                value = matrix[row * edge : row * edge + edge, column * edge : column * edge + edge]
                raise_top(top_out, value)
                if j < half:
                    put_block(flow_a, value, j, depth)
                else:
                    put_block(flow_b, value, j - half, depth)

    top_out[...] = jnp.zeros_like(top_out)
    z = z_ref[...]
    x_c = mm(z, win[...]) + vec[0] + pos_c_ref[...]
    x_t = vec[13] + pos_t_ref[...]
    n_c = norm(x_c, vec[1], vec[2]).astype(bf)
    n_t = norm(x_t, vec[1], vec[2]).astype(bf)
    split_rows(q, (mm(n_t, wqkv[:, :PD]) + vec[3]) * (1.0 / math.sqrt(PD // PH)))
    for ref, start, bias in ((k, PD, 0.0), (v, 2 * PD, vec[4])):
        of_c = mm(n_c, wqkv[:, start : start + PD]) + bias
        of_t = mm(n_t, wqkv[:, start : start + PD]) + bias
        count = NT * LT
        for i in range(images):
            ref[i, :LC, :] = of_c[LC * i : LC * i + LC].astype(bf)
            ref[i, LC:, :] = of_t[count * i : count * i + count].astype(bf)
    attend(q, k, v, valid_ref, att, PH)
    mid = x_t + mm(flat(att), wo[...]) + vec[5]
    n_two = norm(mid, vec[6], vec[7]).astype(bf)
    y = feed_forward(n_two, mid, w1, w2, vec, pre_ref, acc)
    n_three = norm(y, vec[10], vec[11]).astype(bf)
    difference = mm(n_three, wout[...]) + vec[12] - tgt_ref[...]
    tmask = tmask_ref[...]
    magnitude = jnp.abs(difference)
    loss = jnp.where(magnitude < 1.0, 0.5 * difference * difference, magnitude - 0.5) * tmask
    loss_out[...] = col_sum(loss)
    grad = jnp.clip(difference, -1.0, 1.0) * tmask

    grads[12] = col_sum(grad)
    low = grad.astype(bf)
    store(5, mm(n_three.T, low))
    dy, grads[10], grads[11] = norm_back(y, vec[10], mm(low, wout[...], RIGHT_T))
    grads[9] = col_sum(dy)
    low = dy.astype(bf)
    acc[...] = jnp.zeros_like(acc)

    def strip(c, carry):
        lanes = pl.ds(pl.multiple_of(c * STRIP, 128), STRIP)
        pre = pre_ref[:, lanes]
        act_ref[:, lanes] = gelu(pre).astype(bf)
        dpre = mm(low, w2[lanes, :], RIGHT_T) * gelu_slope(pre)
        grads.put_part(8, c * STRIP, STRIP, col_sum(dpre))
        dpre = dpre.astype(bf)
        dpre_ref[:, lanes] = dpre
        acc[...] += mm(dpre, w1[:, lanes], RIGHT_T)
        return carry

    lax.fori_loop(0, PFF // STRIP, strip, 0)
    store(4, mm(act_ref[...].T, low))
    store(3, mm(n_two.T, dpre_ref[...]))
    dmid, grads[6], grads[7] = norm_back(mid, vec[6], acc[...])
    dmid = dmid + dy
    grads[5] = col_sum(dmid)
    low = dmid.astype(bf)
    split_rows(go, mm(low, wo[...], RIGHT_T))
    store(2, mm(flat(att).T, low))
    attend_back(q, k, v, valid_ref, go, dq, dk, dv, PH)
    d_q, d_k, d_v = flat(dq), [dk[i] for i in range(images)], [dv[i] for i in range(images)]
    grads[3] = col_sum(d_q)
    grads[4] = sum(col_sum(part) for part in d_v)
    q_low = d_q.astype(bf)
    k_c = jnp.concatenate([part[:LC] for part in d_k], 0).astype(bf)
    k_t = jnp.concatenate([part[LC:] for part in d_k], 0).astype(bf)
    v_c = jnp.concatenate([part[:LC] for part in d_v], 0).astype(bf)
    v_t = jnp.concatenate([part[LC:] for part in d_v], 0).astype(bf)
    n_c_t, n_t_t = n_c.T, n_t.T
    store(
        1,
        jnp.concatenate(
            [mm(n_t_t, q_low), mm(n_c_t, k_c) + mm(n_t_t, k_t), mm(n_c_t, v_c) + mm(n_t_t, v_t)], 1
        ),
    )
    wq, wk, wv = wqkv[:, :PD], wqkv[:, PD : 2 * PD], wqkv[:, 2 * PD :]
    dn_t = mm(q_low, wq, RIGHT_T) + mm(k_t, wk, RIGHT_T) + mm(v_t, wv, RIGHT_T)
    dn_c = mm(k_c, wk, RIGHT_T) + mm(v_c, wv, RIGHT_T)
    dx_t, gain_t, shift_t = norm_back(x_t, vec[1], dn_t)
    dx_c, gain_c, shift_c = norm_back(x_c, vec[1], dn_c)
    grads[1] = gain_t + gain_c
    grads[2] = shift_t + shift_c
    dx_t = dx_t + dmid
    grads[13] = col_sum(dx_t)
    grads[0] = col_sum(dx_c)
    low = dx_c.astype(bf)
    dz_out[...] = mm(low, win[...], RIGHT_T).astype(bf)
    store(0, mm(z.T, low))


def flow_split(count):
    return (count // 2 + 3) // 4 * 4


def encoder_back_kernel(
    depth, slots, table, dz_ref, rows_ref, e_ref, q, k, v, att_ref, mid_ref, pre_ref, hid_ref, valid_ref, vec_ref,
    flow_a, flow_b, vec_out, top_out,
    wqkv, wo, w1, w2, go, dq, dk, dv, act_t, dpre_ref, x_t, dqkv, acc, stage, sems, out_sems,
):
    vec, grads = Vec(vec_ref, enc_lengths()), Vec(vec_out, enc_lengths())
    edge = table[0].shape[-1]
    half = flow_split(NBE)
    groups = load_blocks(table, slots, sems, 0, enc_shapes(), (None, wqkv, wo, w1, w2))
    start_all(groups[::-1])
    firsts = offsets([h * b // (edge * edge) for h, b in enc_shapes()])
    sent = []

    def store(index, left_t, right):
        columns = enc_shapes()[index][1] // edge
        rows = enc_shapes()[index][0] // edge
        for first in range(0, rows * columns, 4):
            turn = len(sent)
            slot = turn % 2
            if turn >= 2:
                sent[turn - 2].wait()
            for b in range(4):
                row, column = divmod(first + b, columns)
                value = mm(
                    left_t[row * edge : row * edge + edge, :],
                    right[:, column * edge : column * edge + edge],
                )
                raise_top(top_out, value)
                put_block(stage.at[slot], value, b, depth)
            j = firsts[index] + first
            target, start = (flow_a, j) if j < half else (flow_b, j - half)
            if depth % 8:
                spot = target.at[pl.ds(start, 4)]
            else:
                spot = target.at[:, pl.ds(depth * start, 4 * depth), :]
            copy = pltpu.make_async_copy(stage.at[slot], spot, out_sems.at[turn])
            copy.start()
            sent.append(copy)

    top_out[...] = jnp.zeros_like(top_out)
    hid = hid_ref[...]
    dy, grads[10], grads[11] = norm_back(hid, vec[10], dz_ref[...].astype(f32))
    grads[9] = col_sum(dy)
    low = dy.astype(bf)
    wait_group(groups[4])
    wait_group(groups[3])
    acc[...] = jnp.zeros_like(acc)

    def strip(c, carry):
        lanes = pl.ds(pl.multiple_of(c * STRIP, 128), STRIP)
        pre = pre_ref[:, lanes]
        act_t[lanes, :] = gelu(pre).astype(bf).T
        dpre = mm(low, w2[lanes, :], RIGHT_T) * gelu_slope(pre)
        grads.put_part(8, c * STRIP, STRIP, col_sum(dpre))
        dpre = dpre.astype(bf)
        dpre_ref[:, lanes] = dpre
        acc[...] += mm(dpre, w1[:, lanes], RIGHT_T)
        return carry

    lax.fori_loop(0, FF // STRIP, strip, 0)
    dqkv[:, :D] = low
    store(4, act_t, dqkv)
    mid = mid_ref[...]
    unit, _ = norm_parts(mid)
    x_t[...] = (unit * vec[6] + vec[7]).astype(bf).T
    store(3, x_t, dpre_ref)
    dmid, grads[6], grads[7] = norm_back(mid, vec[6], acc[...])
    dmid = dmid + dy
    acc[...] = dmid
    grads[5] = col_sum(dmid)
    low = dmid.astype(bf)
    wait_group(groups[2])
    wait_group(groups[1])
    split_rows(go, mm(low, wo[...], RIGHT_T))
    x_t[...] = flat(att_ref).T
    dqkv[:, :D] = low
    store(2, x_t, dqkv)
    attend_back(q, k, v, valid_ref, go, dq, dk, dv, H)
    d_q, d_v = flat(dq), flat(dv)
    grads[3] = col_sum(d_q)
    grads[4] = col_sum(d_v)
    dqkv[:, :D] = d_q.astype(bf)
    dqkv[:, D : 2 * D] = flat(dk).astype(bf)
    dqkv[:, 2 * D :] = d_v.astype(bf)
    e = e_ref[...]
    x_t[...] = norm(e, vec[1], vec[2]).astype(bf).T
    store(1, x_t, dqkv)
    back, grads[1], grads[2] = norm_back(e, vec[1], mm(dqkv[...], wqkv[...], RIGHT_T))
    de = acc[...] + back
    grads[0] = col_sum(de)
    dqkv[:, :D] = de.astype(bf)
    x_t[...] = rows_ref[...].T
    store(0, x_t, dqkv)
    for copy in sent[-2:]:
        copy.wait()


def spaces(count):
    return [pl.BlockSpec(memory_space=pltpu.VMEM)] * count


ANYWHERE = pl.BlockSpec(memory_space=pl.ANY)


def weight_scratch(shapes):
    return [pltpu.VMEM(shape, bf) for shape in shapes]


def call_kernel(body, section, places, table, args, outs, any_outs, scratch, name):
    count = len(table)

    def guarded(places_ref, *refs):
        @pl.when(places_ref[2 * (NBE + NBP)] == section)
        def run():
            body(places_ref, refs[:count], *refs[count:])

    specs = [ANYWHERE] * count + spaces(len(args))
    out_specs = [ANYWHERE if i in any_outs else spaces(1)[0] for i in range(len(outs))]
    return pl.pallas_call(
        guarded,
        grid_spec=pltpu.PrefetchScalarGridSpec(
            num_scalar_prefetch=1, grid=(), in_specs=specs, out_specs=out_specs, scratch_shapes=scratch
        ),
        out_shape=[jax.ShapeDtypeStruct(shape, kind) for shape, kind in outs],
        compiler_params=pltpu.CompilerParams(vmem_limit_bytes=58 << 20),
        name=name,
    )(places, *table, *args)


MARKS = 16


def flow_shapes(count, edge, ranks):
    half = flow_split(count)
    if (edge // ranks) % 8:
        return [((n, edge, edge), f32) for n in (half, count - half)]
    return [((ranks, edge // ranks * n + MARKS, edge), f32) for n in (half, count - half)]


def encoder_call(slots, table, rows, pos, valid, vec):
    n = rows.shape[0]
    images = n // LC
    per = (images, LC, D)
    outs = [((n, D), bf), ((n, D), f32), (per, bf), (per, bf), (per, bf), (per, bf)]
    outs += [((n, D), f32), ((n, FF), f32), ((n, D), f32)]
    scratch = weight_scratch(enc_shapes()) + [pltpu.VMEM((n, D), f32), pltpu.SemaphoreType.DMA((NBE,))]
    args = (rows, pos, valid, vec)
    return call_kernel(encoder_kernel, 0, slots, table, args, outs, (), scratch, "encoder_forward")


def target_call(slots, table, rows, pos, some, pos_some, valid, vec, images):
    n = some.shape[0]
    keys = rows.shape[0] // images
    per, wide = (images, n // images, D), (images, keys, D)
    scratch = weight_scratch(enc_shapes()) + [
        pltpu.VMEM(per, bf),
        pltpu.VMEM(wide, bf),
        pltpu.VMEM(wide, bf),
        pltpu.VMEM(per, bf),
        pltpu.VMEM((n, D), f32),
        pltpu.SemaphoreType.DMA((NBE,)),
    ]
    args = (rows, pos, some, pos_some, valid, vec)
    outs = [((n, D), f32)]
    return call_kernel(target_kernel, 1, slots, table, args, outs, (), scratch, "target_forward")[0]


def predictor_call(slots, table, z, pos_c, pos_t, valid, tgt, tmask, vec, ranks):
    n, m = z.shape[0], pos_t.shape[0]
    images = n // LC
    rows, keys = m // images, valid.shape[-1]
    edge = table[0].shape[-1]
    per, wide = (images, rows, PD), (images, keys, PD)
    outs = [((n, D), bf)] + flow_shapes(NBP, edge, ranks) + [((1, VP), f32), ((1, D), f32), ((1, edge), f32)]
    scratch = weight_scratch(pred_shapes()) + [
        pltpu.VMEM(per, bf),
        pltpu.VMEM(wide, bf),
        pltpu.VMEM(wide, bf),
        pltpu.VMEM(per, bf),
        pltpu.VMEM(per, bf),
        pltpu.VMEM(per, f32),
        pltpu.VMEM(wide, f32),
        pltpu.VMEM(wide, f32),
        pltpu.VMEM((m, PFF), f32),
        pltpu.VMEM((m, PFF), bf),
        pltpu.VMEM((m, PFF), bf),
        pltpu.VMEM((m, PD), f32),
        pltpu.SemaphoreType.DMA((NBE + NBP,)),
    ]
    args = (z, pos_c, pos_t, valid, tgt, tmask, vec)
    body = functools.partial(predictor_kernel, edge // ranks)
    return call_kernel(body, 1, slots, table, args, outs, (), scratch, "predictor_step")


def encoder_back_call(slots, table, dz, rows, kept, valid, vec, ranks):
    n = rows.shape[0]
    images = n // LC
    edge = table[0].shape[-1]
    per = (images, LC, D)
    e, q, k, v, att, mid, pre, hid = kept
    depth = edge // ranks
    stage = (2, ranks, 4 * depth, edge) if depth % 8 == 0 else (2, 4, edge, edge)
    scratch = weight_scratch(enc_shapes()[1:]) + [
        pltpu.VMEM(per, bf),
        pltpu.VMEM(per, f32),
        pltpu.VMEM(per, f32),
        pltpu.VMEM(per, f32),
        pltpu.VMEM((FF, n), bf),
        pltpu.VMEM((n, FF), bf),
        pltpu.VMEM((D, n), bf),
        pltpu.VMEM((n, 3 * D), bf),
        pltpu.VMEM((n, D), f32),
        pltpu.VMEM(stage, f32),
        pltpu.SemaphoreType.DMA((NBE,)),
        pltpu.SemaphoreType.DMA((NBE // 4,)),
    ]
    outs = flow_shapes(NBE, edge, ranks) + [((1, VE), f32), ((1, edge), f32)]
    args = (dz, rows, e, q, k, v, att, mid, pre, hid, valid, vec)
    body = functools.partial(encoder_back_kernel, edge // ranks)
    return call_kernel(body, 0, slots, table, args, outs, (0, 1), scratch, "encoder_backward")


def soap_first(flags, factor, *arrays):
    n, e = arrays[0].shape[:2]
    one = pl.BlockSpec((1, e, e), lambda i, *_: (i, 0, 0))
    two = pl.BlockSpec((1, 2, e, e), lambda i, *_: (i, 0, 0, 0))
    single = jax.ShapeDtypeStruct((n, e, e), f32)
    double = jax.ShapeDtypeStruct((n, 2, e, e), f32)
    return pl.pallas_call(
        first_kernel,
        grid_spec=pltpu.PrefetchScalarGridSpec(
            num_scalar_prefetch=2, grid=(n,), in_specs=[one] * 8, out_specs=[one] * 5 + [two] * 2
        ),
        out_shape=[single] * 5 + [double] * 2,
        compiler_params=pltpu.CompilerParams(vmem_limit_bytes=56 << 20),
        name="soap_first",
    )(flags, factor, *arrays)


def soap_factor(flags, base, gram):
    n, _, e, _ = base.shape
    whole = pl.BlockSpec(memory_space=pltpu.VMEM)
    return pl.pallas_call(
        factor_kernel,
        grid_spec=pltpu.PrefetchScalarGridSpec(
            num_scalar_prefetch=1,
            grid=(),
            in_specs=[whole] * 2,
            out_specs=whole,
            scratch_shapes=[
                pltpu.VMEM((n, 2, e, e), f32),
                pltpu.VMEM((n, 2, e, e), f32),
                pltpu.VMEM((n, 2, 128, 128), f32),
            ],
        ),
        out_shape=jax.ShapeDtypeStruct(base.shape, f32),
        compiler_params=pltpu.CompilerParams(vmem_limit_bytes=56 << 20),
        name="soap_factor",
    )(flags, base, gram)


def soap_last(flags, left, right, moment, fresh):
    n, e = left.shape[:2]
    one = pl.BlockSpec((1, e, e), lambda i, *_: (i, 0, 0))
    two = pl.BlockSpec((1, 2, e, e), lambda i, *_: (i, 0, 0, 0))
    return pl.pallas_call(
        last_kernel,
        grid_spec=pltpu.PrefetchScalarGridSpec(
            num_scalar_prefetch=1, grid=(n,), in_specs=[one] * 3 + [two], out_specs=[one] * 3
        ),
        out_shape=[jax.ShapeDtypeStruct((n, e, e), f32)] * 3,
        compiler_params=pltpu.CompilerParams(vmem_limit_bytes=56 << 20),
        name="soap_last",
    )(flags, left, right, moment, fresh)


def place_shares(slots, second, enc_share, pred_share, ranks, slot_count):
    depth, edge = enc_share.shape[1:]

    def body(slots_ref, second_ref, enc_ref, pred_ref, out_ref):
        def run(source, first, count):
            def copy(j, carry):
                slot = slots_ref[first + j]
                rows = pl.ds(pl.multiple_of(slot % slot_count * depth, depth), depth)
                out_ref[slot // slot_count, rows, :] = source[j]
                return carry

            lax.fori_loop(0, count, copy, 0)

        @pl.when(second_ref[0] == 0)
        def enc():
            run(enc_ref, 0, NBE)

        @pl.when(second_ref[0] != 0)
        def pred():
            run(pred_ref, NBE, NBP)

    return pl.pallas_call(
        body,
        grid_spec=pltpu.PrefetchScalarGridSpec(
            num_scalar_prefetch=2, grid=(), in_specs=spaces(2), out_specs=spaces(1)[0]
        ),
        out_shape=jax.ShapeDtypeStruct((ranks, slot_count * depth + MARKS, edge), f32),
        compiler_params=pltpu.CompilerParams(vmem_limit_bytes=40 << 20),
        name="place_shares",
    )(slots, second, enc_share, pred_share)


ROUNDS = (
    (((1, 0), (2, 1), (4, 2)), ()),
    (((5, 0), (6, 1), (8, 3)), (1, 2, 4)),
    (((3, 0), (7, 1)), (5, 6)),
    (((9, 0), (10, 1), (12, 2)), (3, 7, 8)),
    (((13, 0), (14, 1)), (9, 10, 12)),
    (((11, 0), (15, 1)), (13, 14)),
)


def gather_pieces(own):
    both = Exchange((0, 1))
    if both.ranks != 16:
        return None
    held = {0: own}
    for moves, awaited in ROUNDS:
        names = sorted({piece ^ (1 << bit) for piece, bit in moves} | set(awaited))
        values = [held[name] for name in names]
        if awaited:
            values = lax.optimization_barrier(values)
        source = dict(zip(names, values))
        for piece, bit in moves:
            held[piece] = both.swap(source[piece ^ (1 << bit)], bit)
    return [held[piece] for piece in range(both.ranks)]


class Exchange:
    def __init__(self, sections):
        self.ranks = lax.axis_size("dp")
        self.bits = self.ranks.bit_length() - 1
        self.sections = sections

    def swap(self, value, bit):
        pairs = [
            (s * self.ranks + i, s * self.ranks + (i ^ (1 << bit)))
            for s in self.sections
            for i in range(self.ranks)
        ]
        return lax.ppermute(value, ("section", "dp"), pairs)

    def total(self, value):
        for bit in range(self.bits):
            value = value + self.swap(value, bit)
        return value


def wire_exponent(bound):
    return jnp.floor(jnp.log2(WIRE_TOP / jnp.maximum(bound, 1e-30)))


def pack(values, exponent):
    row = lax.broadcasted_iota(jnp.int32, values.shape, values.ndim - 2)
    marked = jnp.where(row < values.shape[-2] - MARKS, values * jnp.exp2(exponent), exponent)
    return marked.astype(WIRE)


def halve(exchange, flows, orders, bound):
    bits = exchange.bits
    me = lax.axis_index("dp")
    parts = [f.reshape((2,) * bits + f.shape[1:]) for f in flows]
    bounds = [bound for _ in flows]
    left = [list(range(bits - 1, -1, -1)) for _ in flows]
    for stage in range(bits):
        for k, part in enumerate(parts):
            bit = orders[k][stage]
            axis = left[k].index(bit)
            mine = (me >> bit) & 1
            give = lax.dynamic_index_in_dim(part, 1 - mine, axis, keepdims=False)
            arrived = exchange.swap(pack(give, wire_exponent(bounds[k])), bit)
            keep = lax.dynamic_index_in_dim(part, mine, axis, keepdims=False)
            unscale = jnp.exp2(-arrived[..., -1, 0].reshape(-1)[0].astype(f32))
            parts[k] = keep + arrived.astype(f32) * unscale
            bounds[k] = bounds[k] + WIRE_TOP * unscale
            left[k].remove(bit)
    return [part[:-MARKS] for part in parts], sum(bounds)


def by_share(flow, ranks):
    if flow.shape[0] == ranks and flow.shape[1] != flow.shape[2]:
        return flow
    blocks, edge = flow.shape[:2]
    cut = flow.reshape(blocks, ranks, edge // ranks, edge)
    cut = cut.transpose(1, 0, 2, 3).reshape(ranks, -1, edge)
    return jnp.pad(cut, ((0, 0), (0, MARKS), (0, 0)))


def on_device(
    pixels,
    ctx_idx,
    ctx_len,
    tgt_idx,
    tgt_len,
    slot_of,
    weights,
    first_moment,
    second_moment,
    left_basis,
    right_basis,
    left_stats,
    right_stats,
    vectors,
    vector_first,
    vector_second,
):
    section_index = lax.axis_index("section")
    owner_index = lax.axis_index("dp")
    ranks = lax.axis_size("dp")
    is_first = section_index == 0
    second = section_index.astype(jnp.int32).reshape(1)
    slot_count = weights.shape[1]
    edge = weights.shape[-1]
    own = weights[0].astype(bf)
    table = gather_pieces(own)
    if table is None:
        table = [lax.all_gather(own, "dp", axis=0, tiled=True)]
        places = jnp.concatenate([jnp.zeros_like(slot_of), slot_of, second])
    else:
        places = [jnp.bitwise_xor(slot_of // slot_count, owner_index), slot_of % slot_count, second]
        places = jnp.concatenate(places)
    enc_slots = slot_of[:NBE]
    pred_slots = slot_of[NBE:]
    row_now = vectors[0]
    enc_vec_now = lax.dynamic_slice_in_dim(row_now, section_index * VP, VE)[None]
    pred_vec_now = row_now[None, :VP]
    pos_enc = sincos(D)
    pos_pred = sincos(PD)
    images = ctx_idx.shape[0]
    rows_all = -(-P_SIZE // 16) * 16
    tgt_flat = tgt_idx.reshape(images, NT * LT)
    ctx_valid = (jnp.arange(LC)[None, :] < ctx_len[:, None]).astype(f32)
    tgt_valid = (jnp.arange(LT)[None, None, :] < tgt_len[:, :, None]).astype(f32)
    tgt_valid = tgt_valid.reshape(images, NT * LT)
    joined_valid = jnp.concatenate([ctx_valid, tgt_valid], 1)[:, None, :]
    all_valid = (jnp.arange(rows_all) < P_SIZE).astype(f32)
    all_valid = jnp.broadcast_to(all_valid, (images, 1, rows_all))

    def pick(index):
        return (index[..., None] == jnp.arange(P_SIZE)).astype(f32)

    ctx_hot = pick(ctx_idx)
    tgt_hot = pick(tgt_flat)

    def choose(hot, values):
        return jnp.einsum(
            "njp,pd->njd", hot, values, precision=lax.Precision.HIGHEST, preferred_element_type=f32
        ).reshape(-1, values.shape[-1])

    def choose_pixels(hot):
        picked = jnp.einsum("njp,npd->njd", hot.astype(bf), pixels, preferred_element_type=f32)
        return picked.astype(bf).reshape(-1, PIX)

    pixel_rows = choose_pixels(ctx_hot)
    enc_pos_ctx = choose(ctx_hot, pos_enc)
    padding = ((0, 0), (0, rows_all - P_SIZE), (0, 0))
    pixel_all = jnp.pad(pixels, padding).reshape(-1, PIX)
    pos_all = jnp.broadcast_to(jnp.pad(pos_enc[None], padding), (images, rows_all, D)).reshape(-1, D)
    pixel_tgt = choose_pixels(tgt_hot)
    enc_pos_tgt = choose(tgt_hot, pos_enc)
    pred_pos_ctx = choose(ctx_hot, pos_pred)
    pred_pos_tgt = choose(tgt_hot, pos_pred)

    ctx_keys = ctx_valid[:, None, :]
    encoded = encoder_call(places, table, pixel_rows, enc_pos_ctx, ctx_keys, enc_vec_now)
    context = from_behind(encoded[0], "section", 1)
    target = target_call(
        places, table, pixel_all, pos_all, pixel_tgt, enc_pos_tgt, all_valid, enc_vec_now, images
    )
    back_send, pred_a, pred_b, pred_vec, loss_lanes, pred_top = predictor_call(
        places,
        table,
        context,
        pred_pos_ctx,
        pred_pos_tgt,
        joined_valid,
        target,
        tgt_valid.reshape(-1, 1),
        pred_vec_now,
        ranks,
    )
    incoming = from_behind(back_send, "section", -1)
    loss_local = jnp.where(is_first, 0.0, jnp.sum(loss_lanes))

    low_order = list(range(Exchange((0,)).bits))
    orders = [low_order, low_order]
    if len(low_order) > 2:
        orders = [[0, 2, 1] + low_order[3:], [1, 0, 2] + low_order[3:]]
    pred_flows = [by_share(flow, ranks) for flow in (pred_a, pred_b)]
    pred_parts, pred_bound = halve(Exchange((1,)), pred_flows, orders, jnp.max(pred_top))

    enc_a, enc_b, enc_vec, enc_top = encoder_back_call(
        places, table, incoming, pixel_rows, encoded[1:], ctx_keys, enc_vec_now, ranks
    )
    enc_flows = [by_share(flow, ranks) for flow in (enc_a, enc_b)]
    enc_parts, enc_bound = halve(Exchange((0,)), enc_flows, orders, jnp.max(enc_top))
    depth = edge // ranks
    enc_share = jnp.concatenate(enc_parts, 0).reshape(NBE, depth, edge)
    pred_share = jnp.concatenate(pred_parts, 0).reshape(NBP, depth, edge)

    both = Exchange((0, 1))
    vec_local = jnp.where(is_first, enc_vec[0], jnp.pad(pred_vec[0], (0, VE - VP)))
    count_local = jnp.where(is_first, 0, jnp.sum(tgt_len)).astype(f32)
    scalars = jnp.pad(jnp.stack([loss_local, count_local]), (0, 126))
    summed = both.total(jnp.concatenate([vec_local, scalars]))
    vec_total = jnp.pad(summed[:VE], (0, VW - VE))
    share_squares = jnp.where(
        is_first, jnp.sum(enc_share * enc_share), jnp.sum(pred_share * pred_share)
    )
    squares = both.total(jnp.full((128,), share_squares))
    facts = jnp.stack([squares[0] + jnp.sum(summed[:VE] ** 2), summed[VE], summed[VE + 1]])
    facts = jnp.pad(facts, (0, 125))
    swap_sections = [(i, 1 - i) for i in range(2)]
    facts = facts + lax.ppermute(facts, "section", swap_sections)
    square_total, loss_total, count_total = facts[0], facts[1], facts[2]

    placed = place_shares(slot_of, second, enc_share, pred_share, ranks, slot_count)
    exponent = wire_exponent(jnp.where(is_first, enc_bound, pred_bound))
    payload = pack(placed, exponent)
    owned = lax.all_to_all(payload, "dp", split_axis=0, concat_axis=0, tiled=True).astype(f32)
    unscale = jnp.exp2(-owned[:, -1:, :1])
    owned = (owned[:, : slot_count * depth] * unscale).reshape(ranks, slot_count, depth, edge)
    owned_sum = owned.transpose(1, 0, 2, 3).reshape(slot_count, edge, edge)

    own_ids = owner_index * slot_count + jnp.arange(slot_count)
    enc_here = jnp.any(own_ids[:, None] == enc_slots[None, :], 1)
    pred_here = jnp.any(own_ids[:, None] == pred_slots[None, :], 1)
    trained = jnp.where(is_first, enc_here, pred_here)
    ema_here = jnp.logical_and(jnp.logical_not(is_first), enc_here)
    positions = jnp.arange(VW)
    vec_trained = positions < jnp.where(is_first, VE, VP)
    vec_ema = jnp.logical_and(jnp.logical_not(is_first), positions >= VP)
    grad_norm = jnp.sqrt(square_total) / count_total
    factor = jnp.minimum(1.0, CLIP_LIMIT / (grad_norm + 1e-06)) / count_total

    flags = trained.astype(jnp.int32)
    new_weight, moment, new_second, new_estat, new_fstat, base, gram = soap_first(
        flags,
        factor.reshape(1),
        owned_sum,
        weights[0],
        first_moment[0],
        second_moment[0],
        left_basis[0],
        right_basis[0],
        left_stats[0],
        right_stats[0],
    )
    fresh_bases = soap_factor(flags, base, gram)
    new_left, new_right, new_first = soap_last(
        flags, left_basis[0], right_basis[0], moment, fresh_bases
    )

    correct_one = 1.0 - BETA_FIRST**STEP
    correct_two = 1.0 - BETA_SECOND**STEP
    vec_clipped = vec_total * factor
    fresh_first = BETA_FIRST * vector_first[0] + (1.0 - BETA_FIRST) * vec_clipped
    fresh_second = BETA_SECOND * vector_second[0] + (1.0 - BETA_SECOND) * vec_clipped * vec_clipped
    stepped = row_now - RATE_VECTOR * (fresh_first / correct_one) / (
        jnp.sqrt(fresh_second / correct_two) + ADAM_EPS
    )
    new_vec = jnp.where(vec_trained, stepped, row_now)
    new_vec_first = jnp.where(vec_trained, fresh_first, vector_first[0])
    new_vec_second = jnp.where(vec_trained, fresh_second, vector_second[0])
    from_encoder = from_behind(new_weight.astype(bf), "section", 1).astype(f32)
    vec_from_encoder = from_behind(new_vec.astype(bf), "section", 1).astype(f32)
    new_weight = jnp.where(
        ema_here[:, None, None], EMA_KEEP * weights[0] + (1.0 - EMA_KEEP) * from_encoder, new_weight
    )
    aligned = jnp.concatenate([jnp.zeros((VP,), f32), vec_from_encoder[:VE]])
    new_vec = jnp.where(vec_ema, EMA_KEEP * row_now + (1.0 - EMA_KEEP) * aligned, new_vec)
    return (
        loss_total,
        count_total,
        grad_norm,
        new_weight[None],
        new_first[None],
        new_second[None],
        new_left[None],
        new_right[None],
        new_estat[None],
        new_fstat[None],
        new_vec[None],
        new_vec_first[None],
        new_vec_second[None],
    )


def solution(mesh):
    in_specs = (
        P("dp", None, None),
        P("dp", None),
        P("dp"),
        P("dp", None, None),
        P("dp", None),
        P(),
        P("section", "dp", None, None),
        P("section", "dp", None, None),
        P("section", "dp", None, None),
        P("section", "dp", None, None),
        P("section", "dp", None, None),
        P("section", "dp", None, None),
        P("section", "dp", None, None),
        P("section", None),
        P("section", None),
        P("section", None),
    )
    out_specs = (
        P(),
        P(),
        P(),
        P("section", "dp", None, None),
        P("section", "dp", None, None),
        P("section", "dp", None, None),
        P("section", "dp", None, None),
        P("section", "dp", None, None),
        P("section", "dp", None, None),
        P("section", "dp", None, None),
        P("section", None),
        P("section", None),
        P("section", None),
    )
    return jax.shard_map(
        on_device, mesh=mesh, in_specs=in_specs, out_specs=out_specs, check_vma=False
    )
```

profile of v0, /device:TPU:20, one launch (start us, length us, event | category | flops | bytes accessed | tf_op | source)
XLA Modules:
  0.0 734.3 jit_solution(10903074704027790600)
XLA Ops:
  0.7 2.0 bitcast_convert_fusion.refs_0_
  6.4 30.5 %collective-permute-done.1.refs_2_ = bf16[5,384,384]{2,1,0:T(8,128)(2,1)S(1)} collective-permute-done((bf16[5,384,384]{2,1,0:T(8,128)(2,1)S(1)}, bf16[5,384,384]{2,1,0:T(8,128)(2,1)S(1)}, u32[]{:S(2)}, u32[]{:S(2)}) %collective-permute-start.1) | collective-permute-done | bytes 1474592 | tf_op jit(solution)/shard_map/ppermute | solution.py:987
  40.7 30.1 %collective-permute-done.3.refs_5_ = bf16[5,384,384]{2,1,0:T(8,128)(2,1)S(1)} collective-permute-done((bf16[5,384,384]{2,1,0:T(8,128)(2,1)S(1)}, bf16[5,384,384]{2,1,0:T(8,128)(2,1)S(1)}, u32[]{:S(2)}, u32[]{:S(2)}) %collective-permute-start.3) | collective-permute-done | bytes 1474592 | tf_op jit(solution)/shard_map/ppermute | solution.py:987
  75.2 26.6 %collective-permute-done.7.refs_8_ = bf16[5,384,384]{2,1,0:T(8,128)(2,1)} collective-permute-done((bf16[5,384,384]{2,1,0:T(8,128)(2,1)S(1)}, bf16[5,384,384]{2,1,0:T(8,128)(2,1)}, u32[]{:S(2)}, u32[]{:S(2)}) %collective-permute-start.7) | collective-permute-done | bytes 1474592 | tf_op jit(solution)/shard_map/ppermute | solution.py:987
  105.8 2.9 collective-permute-start.10
  113.1 23.3 %collective-permute-done.9.refs_10_ = bf16[5,384,384]{2,1,0:T(8,128)(2,1)} collective-permute-done((bf16[5,384,384]{2,1,0:T(8,128)(2,1)}, bf16[5,384,384]{2,1,0:T(8,128)(2,1)}, u32[]{:S(2)}, u32[]{:S(2)}) %collective-permute-start.9) | collective-permute-done | bytes 1474592 | tf_op jit(solution)/shard_map/ppermute | solution.py:987
  136.4 5.1 collective-permute-done.10.refs_12_
  154.2 22.1 %collective-permute-done.11.refs_13_ = bf16[5,384,384]{2,1,0:T(8,128)(2,1)} collective-permute-done((bf16[5,384,384]{2,1,0:T(8,128)(2,1)}, bf16[5,384,384]{2,1,0:T(8,128)(2,1)}, u32[]{:S(2)}, u32[]{:S(2)}) %collective-permute-start.11) | collective-permute-done | bytes 1474592 | tf_op jit(solution)/shard_map/ppermute | solution.py:987
  179.1 2.1 fusion.53
  181.8 27.7 %collective-permute-done.13.refs_11_ = bf16[5,384,384]{2,1,0:T(8,128)(2,1)S(1)} collective-permute-done((bf16[5,384,384]{2,1,0:T(8,128)(2,1)}, bf16[5,384,384]{2,1,0:T(8,128)(2,1)S(1)}, u32[]{:S(2)}, u32[]{:S(2)}) %collective-permute-start.13) | collective-permute-done | bytes 1474592 | tf_op jit(solution)/shard_map/ppermute | solution.py:987
  211.1 24.9 %encoder_forward.1 = (bf16[256,768]{1,0:T(8,128)(2,1)}, f32[256,768]{1,0:T(8,128)}, bf16[2,128,768]{2,1,0:T(8,128)(2,1)}, bf16[2,128,768]{2,1,0:T(8,128)(2,1)}, ...) custom-call(s32[137]{0:T(256)} %pad_add_fusion.places_ref, ...), custom_call_target="tpu_custom_call" | custom-call | tf_op jit(solution)/shard_map/encoder_forward/pallas_call | solution.py:759
  245.4 4.3 target_forward.1.refs_20_
  250.5 7.2 predictor_step.1
  261.1 3.0 constant_dynamic-slice_fusion.2
  265.1 1.8 constant_dynamic-slice_fusion
  266.9 2.3 fusion.13
  270.9 1.8 collective-permute-start.25
  272.6 32.2 %collective-permute-done.16.refs_16_ = bf16[256,768]{1,0:T(8,128)(2,1)S(1)} collective-permute-done((bf16[256,768]{1,0:T(8,128)(2,1)}, bf16[256,768]{1,0:T(8,128)(2,1)S(1)}, u32[]{:S(2)}, u32[]{:S(2)}) %collective-permute-start.16) | collective-permute-done | bytes 393248 | tf_op jit(solution)/shard_map/ppermute | solution.py:51
  305.6 43.6 %encoder_backward.1 = (f32[16,688,384]{2,1,0:T(8,128)}, f32[16,592,384]{2,1,0:T(8,128)}, f32[1,11520]{1,0:T(1,128)}, f32[1,384]{1,0:T(1,128)}) custom-call(s32[137]{0:T(256)} %pad_add_fusion.places_ref, bf16[5,384,384]{2,1,0:T(8,128)(2,1)} %copy-done.1, bf16[5,384,384]{2,1,0:T(8,128)(2,1)} %copy-done.6, bf16[5,384,384]{2,1,0:T(8,128)(2,1)} %copy-done.5, ...), custom_call_target="tpu_custom_call" | custom-call | tf_op jit(solution)/shard_map/encoder_backward/pallas_call | solution.py:759
  349.2 11.6 %constant_dynamic-slice_fusion.6 = (f32[2,2,2,1,688,384]{5,4,3,2,1,0:T(8,128)}, f32[2,2,2,1,688,384]{5,4,3,2,1,0:T(8,128)}) fusion(f32[2,2,2,2,688,384]{5,4,3,2,1,0:T(8,128)} %bitcast.213, s32[]{:T(128)S(6)} %select_n.233, s32[]{:T(128)S(6)} %select_n.232), kind=kLoop, calls=%fused_computation.116 | loop fusion | bytes 33816584 | tf_op jit(solution)/shard_map/jit(dynamic_index_in_dim)/dynamic_slice | solution.py:1016
  362.2 11.3 %constant_dynamic-slice_fusion.4 = (f32[2,2,1,2,592,384]{5,4,3,2,1,0:T(8,128)}, f32[2,2,1,2,592,384]{5,4,3,2,1,0:T(8,128)}) fusion(f32[2,2,2,2,592,384]{5,4,3,2,1,0:T(8,128)} %bitcast.214, s32[]{:T(128)S(6)} %select_n.239, s32[]{:T(128)S(6)} %select_n.238), kind=kLoop, calls=%fused_computation.114 | loop fusion | bytes 29097992 | tf_op jit(solution)/shard_map/jit(dynamic_index_in_dim)/dynamic_slice | solution.py:1016
  373.5 6.0 fusion.5
  379.5 1.9 collective-permute-start.21
  381.5 3.3 fusion.2
  384.8 3.1 collective-permute-start.17
  391.6 2.3 bitcast_add_fusion.4
  393.9 2.6 bitcast_add_fusion.5
  396.5 1.8 fusion.17
  402.4 2.5 bitcast_add_fusion.8
  405.0 2.3 bitcast_add_fusion.9
  407.3 17.0 %collective-permute-done.21 = f16[2,2,2,592,384]{4,3,0,1,2:T(8,128)(2,1)} collective-permute-done((f16[2,2,2,592,384]{4,3,0,1,2:T(8,128)(2,1)}, f16[2,2,2,592,384]{4,3,0,1,2:T(8,128)(2,1)}, u32[]{:S(2)}, u32[]{:S(2)}) %collective-permute-start.21) | collective-permute-done | bytes 3637280 | tf_op jit(solution)/shard_map/ppermute | solution.py:987
  426.1 4.8 bitcast_add_fusion.1
  430.9 2.9 copy-done.3
  435.5 2.9 collective-permute-start.22
  439.5 8.8 %bitcast_add_fusion = f32[2,2,2,688,384]{4,3,0,2,1:T(8,128)} fusion(f32[2,2,2,1,688,384]{5,4,3,2,1,0:T(8,128)} %get-tuple-element.90, f16[2,2,2,688,384]{4,3,0,2,1:T(8,128)(2,1)} %collective-permute-done.17, f32[]{:T(128)} %bitcast.17), kind=kLoop, calls=%fused_computation.4 | loop fusion | flops 6340608 | bytes 21135364 | tf_op jit(solution)/shard_map/add | solution.py:1020
  449.1 4.2 fusion.6
  453.3 3.2 collective-permute-start.18
  466.9 2.9 bitcast_add_fusion.3
  472.8 2.8 collective-permute-start.23
  475.6 6.1 collective-permute-done.18
  482.7 5.3 bitcast_add_fusion.2
  488.2 1.9 fusion.14
  490.1 2.1 collective-permute-start.19
  495.1 2.1 bitcast_add_fusion.7
  498.3 1.9 collective-permute-start.24
  500.2 6.7 collective-permute-done.19
  510.0 1.9 collective-permute-start.20
  512.0 2.2 dynamic-slice_bitcast_fusion.1
  514.1 13.6 %collective-permute-done.24 = f16[592,384]{1,0:T(8,128)(2,1)} collective-permute-done((f16[592,384]{1,0:T(8,128)(2,1)}, f16[592,384]{1,0:T(8,128)(2,1)}, u32[]{:S(2)}, u32[]{:S(2)}) %collective-permute-start.24) | collective-permute-done | bytes 454688 | tf_op jit(solution)/shard_map/ppermute | solution.py:987
  529.6 2.3 slice_add_fusion.1
  532.9 7.6 %collective-permute-done.20 = f16[688,384]{1,0:T(8,128)(2,1)} collective-permute-done((f16[688,384]{1,0:T(8,128)(2,1)S(1)}, f16[688,384]{1,0:T(8,128)(2,1)}, u32[]{:S(2)}, u32[]{:S(2)}) %collective-permute-start.20) | collective-permute-done | bytes 528416 | tf_op jit(solution)/shard_map/ppermute | solution.py:987
  546.6 1.8 select_convert_fusion
  548.4 11.2 %all-to-all-start = ((f16[16,136,384]{2,1,0:T(8,128)(2,1)}), f16[16,136,384]{2,1,0:T(8,128)(2,1)S(1)}, u32[]{:S(2)}, u32[]{:S(2)}) async-start(f16[16,136,384]{2,1,0:T(8,128)(2,1)} %select_convert_fusion), calls=%async_computation | async-start | bytes 3342336 | tf_op jit(solution)/shard_map/all_to_all | solution.py:1166
  564.1 2.6 collective-permute-done.37
  570.9 2.8 collective-permute-start.39
  574.6 4.2 collective-permute-done.39
  579.2 4.7 collective-permute-done.40
  586.0 2.4 collective-permute-done.36
  593.8 1.8 copy.98
  595.6 45.9 %soap_first.1 = (f32[5,384,384]{2,1,0:T(8,128)}, f32[5,384,384]{2,1,0:T(8,128)}, f32[5,384,384]{2,1,0:T(8,128)}, f32[5,384,384]{2,1,0:T(8,128)}, f32[5,384,384]{...) custom-call(s32[5]{0:T(128)} %get-tuple-element.116.flag, f32[1]{0:T(128)} %bitcast.73.factor, ...), custom_call_target="tpu_custom_call" | custom-call | tf_op jit(solution)/shard_map/soap_first/pallas_call | solution.py:869
  641.5 3.2 convert_element_type.335
  649.7 64.2 %soap_factor.1.q_ref = f32[5,2,384,384]{3,2,1,0:T(8,128)} custom-call(s32[5]{0:T(128)} %get-tuple-element.116.flag, f32[5,2,384,384]{3,2,1,0:T(8,128)} %get-tuple-element.79.base_ref, f32[5,2,384,384]{3,2,1,0:T(8,128)} %get-tuple-element.80.gram_ref), custom_call_target="tpu_custom_call" | custom-call | tf_op jit(solution)/shard_map/soap_factor/pallas_call | solution.py:883
  713.9 16.7 %soap_last.1 = (f32[5,384,384]{2,1,0:T(8,128)}, f32[5,384,384]{2,1,0:T(8,128)}, f32[5,384,384]{2,1,0:T(8,128)}) custom-call(s32[5]{0:T(128)} %get-tuple-element.116.flag, f32[5,384,384]{2,1,0:T(8,128)} %bitcast.216, f32[5,384,384]{2,1,0:T(8,128)} %bitcast.218, f32[5,384,384]{2,1,0:T(8,128)} %get-tuple-element.78.m_ref, f32[5,2,384,384]{3,2,1,0:T(8,128)} %soap_factor.1.q_ref), custom_call_target="tpu_custom_call" | custom-call | tf_op jit(solution)/shard_map/soap_last/pallas_call | solution.py:906
  730.6 2.2 select_bitcast_fusion
  (290 shorter events, 104.2 us)
Async XLA Ops:
  0.6 109.5 %copy-start.42 = (s32[2,4]{1,0:T(2,128)S(1)}, s32[2,4]{1,0:T(2,128)}, u32[]{:S(2)}) copy-start(s32[2,4]{1,0:T(2,128)} %param.20) | copy-start | bytes 100
  0.7 109.7 %copy-start.51 = (s32[2]{0:T(128)S(1)}, s32[2]{0:T(128)}, u32[]{:S(2)}) copy-start(s32[2]{0:T(128)} %param.18) | copy-start | bytes 28
  0.7 111.0 %copy-start = (s32[68]{0:T(128)S(1)}, s32[68]{0:T(128)}, u32[]{:S(2)}) copy-start(s32[68]{0:T(128)} %slots_ref.1) | copy-start | bytes 820
  0.7 144.9 %copy-start.47 = (s32[2,4,36]{2,1,0:T(4,128)S(1)}, s32[2,4,36]{2,1,0:T(4,128)}, u32[]{:S(2)}) copy-start(s32[2,4,36]{2,1,0:T(4,128)} %param.19) | copy-start | bytes 3460
  0.7 145.0 %copy-start.44 = (s32[2,128]{1,0:T(2,128)S(1)}, s32[2,128]{1,0:T(2,128)}, u32[]{:S(2)}) copy-start(s32[2,128]{1,0:T(2,128)} %param.17) | copy-start | bytes 3076
  2.7 150.4 %copy-start.1 = (bf16[5,384,384]{2,1,0:T(8,128)(2,1)}, bf16[5,384,384]{2,1,0:T(8,128)(2,1)S(1)}, u32[]{:S(2)}) copy-start(bf16[5,384,384]{2,1,0:T(8,128)(2,1)S(1)} %bitcast_convert_fusion.refs_0_) | copy-start | bytes 4423684
  2.7 34.1 %collective-permute-start.1 = (bf16[5,384,384]{2,1,0:T(8,128)(2,1)S(1)}, bf16[5,384,384]{2,1,0:T(8,128)(2,1)S(1)}, u32[]{:S(2)}, u32[]{:S(2)}) collective-permute-start(bf16[5,384,384]{2,1,0:T(8,128)(2,1)S(1)} %bitcast_convert_fusion.refs_0_), channel_id=1, source_target_pairs={{0,2},{1,3},{2,0},{3,1},{4,6},{5,7},{6,4},{7,5},{8,10},{9,11},{10,... | collective-permute-start | bytes 4423688 | tf_op jit(solution)/shard_map/ppermute | solution.py:987
  3.3 33.7 %collective-permute-start = (bf16[5,384,384]{2,1,0:T(8,128)(2,1)S(1)}, bf16[5,384,384]{2,1,0:T(8,128)(2,1)S(1)}, u32[]{:S(2)}, u32[]{:S(2)}) collective-permute-start(bf16[5,384,384]{2,1,0:T(8,128)(2,1)S(1)} %bitcast_convert_fusion.refs_0_), channel_id=1, source_target_pairs={{0,1},{1,0},{2,3},{3,2},{4,5},{5,4},{6,7},{7,6},{8,9},{9,8},{10,11... | collective-permute-start | bytes 4423688 | tf_op jit(solution)/shard_map/ppermute | solution.py:987
  4.8 33.5 %collective-permute-start.2 = (bf16[5,384,384]{2,1,0:T(8,128)(2,1)S(1)}, bf16[5,384,384]{2,1,0:T(8,128)(2,1)S(1)}, u32[]{:S(2)}, u32[]{:S(2)}) collective-permute-start(bf16[5,384,384]{2,1,0:T(8,128)(2,1)S(1)} %bitcast_convert_fusion.refs_0_), channel_id=1, source_target_pairs={{0,4},{1,5},{2,6},{3,7},{4,0},{5,1},{6,2},{7,3},{8,12},{9,13},{10,... | collective-permute-start | bytes 4423688 | tf_op jit(solution)/shard_map/ppermute | solution.py:987
  36.8 116.3 %copy-start.5 = (bf16[5,384,384]{2,1,0:T(8,128)(2,1)}, bf16[5,384,384]{2,1,0:T(8,128)(2,1)S(1)}, u32[]{:S(2)}) copy-start(bf16[5,384,384]{2,1,0:T(8,128)(2,1)S(1)} %collective-permute-done.1.refs_2_) | copy-start | bytes 4423684
  37.1 33.8 %copy-start.6 = (bf16[5,384,384]{2,1,0:T(8,128)(2,1)}, bf16[5,384,384]{2,1,0:T(8,128)(2,1)S(1)}, u32[]{:S(2)}) copy-start(bf16[5,384,384]{2,1,0:T(8,128)(2,1)S(1)} %collective-permute-done.refs_1_) | copy-start | bytes 4423684
  38.3 33.0 %copy-start.7 = (bf16[5,384,384]{2,1,0:T(8,128)(2,1)}, bf16[5,384,384]{2,1,0:T(8,128)(2,1)S(1)}, u32[]{:S(2)}) copy-start(bf16[5,384,384]{2,1,0:T(8,128)(2,1)S(1)} %collective-permute-done.2.refs_4_) | copy-start | bytes 4423684
  38.3 32.5 %collective-permute-start.3 = (bf16[5,384,384]{2,1,0:T(8,128)(2,1)S(1)}, bf16[5,384,384]{2,1,0:T(8,128)(2,1)S(1)}, u32[]{:S(2)}, u32[]{:S(2)}) collective-permute-start(bf16[5,384,384]{2,1,0:T(8,128)(2,1)S(1)} %collective-permute-done.2.refs_4_), channel_id=1, source_target_pairs={{0,1},{1,0},{2,3},{3,2},{4,5},{5,4},{6,7},{7,6},{8,9},{9,8},{10,11... | collective-permute-start | bytes 4423688 | tf_op jit(solution)/shard_map/ppermute | solution.py:987
  38.8 32.5 %collective-permute-start.4 = (bf16[5,384,384]{2,1,0:T(8,128)(2,1)S(1)}, bf16[5,384,384]{2,1,0:T(8,128)(2,1)S(1)}, u32[]{:S(2)}, u32[]{:S(2)}) collective-permute-start(bf16[5,384,384]{2,1,0:T(8,128)(2,1)S(1)} %collective-permute-done.2.refs_4_), channel_id=1, source_target_pairs={{0,2},{1,3},{2,0},{3,1},{4,6},{5,7},{6,4},{7,5},{8,10},{9,11},{10,... | collective-permute-start | bytes 4423688 | tf_op jit(solution)/shard_map/ppermute | solution.py:987
  40.3 61.5 %collective-permute-start.7 = (bf16[5,384,384]{2,1,0:T(8,128)(2,1)S(1)}, bf16[5,384,384]{2,1,0:T(8,128)(2,1)}, u32[]{:S(2)}, u32[]{:S(2)}) collective-permute-start(bf16[5,384,384]{2,1,0:T(8,128)(2,1)S(1)} %bitcast_convert_fusion.refs_0_), channel_id=1, source_target_pairs={{0,8},{1,9},{2,10},{3,11},{4,12},{5,13},{6,14},{7,15},{8,0},{9,1},... | collective-permute-start | bytes 4423688 | tf_op jit(solution)/shard_map/ppermute | solution.py:987
  70.8 32.1 %copy-start.8 = (bf16[5,384,384]{2,1,0:T(8,128)(2,1)}, bf16[5,384,384]{2,1,0:T(8,128)(2,1)S(1)}, u32[]{:S(2)}) copy-start(bf16[5,384,384]{2,1,0:T(8,128)(2,1)S(1)} %collective-permute-done.3.refs_5_) | copy-start | bytes 4423684
  71.3 31.7 %collective-permute-start.5 = (bf16[5,384,384]{2,1,0:T(8,128)(2,1)S(1)}, bf16[5,384,384]{2,1,0:T(8,128)(2,1)S(1)}, u32[]{:S(2)}, u32[]{:S(2)}) collective-permute-start(bf16[5,384,384]{2,1,0:T(8,128)(2,1)S(1)} %collective-permute-done.1.refs_2_), channel_id=1, source_target_pairs={{0,1},{1,0},{2,3},{3,2},{4,5},{5,4},{6,7},{7,6},{8,9},{9,8},{10,11... | collective-permute-start | bytes 4423688 | tf_op jit(solution)/shard_map/ppermute | solution.py:987
  72.6 31.6 %collective-permute-start.6 = (bf16[5,384,384]{2,1,0:T(8,128)(2,1)S(1)}, bf16[5,384,384]{2,1,0:T(8,128)(2,1)S(1)}, u32[]{:S(2)}, u32[]{:S(2)}) collective-permute-start(bf16[5,384,384]{2,1,0:T(8,128)(2,1)S(1)} %collective-permute-done.3.refs_5_), channel_id=1, source_target_pairs={{0,2},{1,3},{2,0},{3,1},{4,6},{5,7},{6,4},{7,5},{8,10},{9,11},{10,... | collective-permute-start | bytes 4423688 | tf_op jit(solution)/shard_map/ppermute | solution.py:987
  104.2 32.2 %collective-permute-start.9 = (bf16[5,384,384]{2,1,0:T(8,128)(2,1)}, bf16[5,384,384]{2,1,0:T(8,128)(2,1)}, u32[]{:S(2)}, u32[]{:S(2)}) collective-permute-start(bf16[5,384,384]{2,1,0:T(8,128)(2,1)} %collective-permute-done.7.refs_8_), channel_id=1, source_target_pairs={{0,2},{1,3},{2,0},{3,1},{4,6},{5,7},{6,4},{7,5},{8,10},{9,11},{10,... | collective-permute-start | bytes 4423688 | tf_op jit(solution)/shard_map/ppermute | solution.py:987
  105.8 35.7 %collective-permute-start.10 = (bf16[5,384,384]{2,1,0:T(8,128)(2,1)}, bf16[5,384,384]{2,1,0:T(8,128)(2,1)}, u32[]{:S(2)}, u32[]{:S(2)}) collective-permute-start(bf16[5,384,384]{2,1,0:T(8,128)(2,1)} %collective-permute-done.7.refs_8_), channel_id=1, source_target_pairs={{0,4},{1,5},{2,6},{3,7},{4,0},{5,1},{6,2},{7,3},{8,12},{9,13},{10,... | collective-permute-start | bytes 4423688 | tf_op jit(solution)/shard_map/ppermute | solution.py:987
  108.7 34.2 %collective-permute-start.8 = (bf16[5,384,384]{2,1,0:T(8,128)(2,1)}, bf16[5,384,384]{2,1,0:T(8,128)(2,1)}, u32[]{:S(2)}, u32[]{:S(2)}) collective-permute-start(bf16[5,384,384]{2,1,0:T(8,128)(2,1)} %collective-permute-done.7.refs_8_), channel_id=1, source_target_pairs={{0,1},{1,0},{2,3},{3,2},{4,5},{5,4},{6,7},{7,6},{8,9},{9,8},{10,11... | collective-permute-start | bytes 4423688 | tf_op jit(solution)/shard_map/ppermute | solution.py:987
  143.0 33.4 %collective-permute-start.11 = (bf16[5,384,384]{2,1,0:T(8,128)(2,1)}, bf16[5,384,384]{2,1,0:T(8,128)(2,1)}, u32[]{:S(2)}, u32[]{:S(2)}) collective-permute-start(bf16[5,384,384]{2,1,0:T(8,128)(2,1)} %collective-permute-done.10.refs_12_), channel_id=1, source_target_pairs={{0,1},{1,0},{2,3},{3,2},{4,5},{5,4},{6,7},{7,6},{8,9},{9,8},{10,11... | collective-permute-start | bytes 4423688 | tf_op jit(solution)/shard_map/ppermute | solution.py:987
  144.3 33.1 %collective-permute-start.12 = (bf16[5,384,384]{2,1,0:T(8,128)(2,1)}, bf16[5,384,384]{2,1,0:T(8,128)(2,1)}, u32[]{:S(2)}, u32[]{:S(2)}) collective-permute-start(bf16[5,384,384]{2,1,0:T(8,128)(2,1)} %collective-permute-done.10.refs_12_), channel_id=1, source_target_pairs={{0,2},{1,3},{2,0},{3,1},{4,6},{5,7},{6,4},{7,5},{8,10},{9,11},{10,... | collective-permute-start | bytes 4423688 | tf_op jit(solution)/shard_map/ppermute | solution.py:987
  149.8 27.6 %copy-start.24 = (f32[196,192]{1,0:T(8,128)}, f32[196,192]{1,0:T(8,128)S(1)}, u32[]{:S(2)}) copy-start(f32[196,192]{1,0:T(8,128)S(1)} %get-tuple-element.113) | copy-start | bytes 451588
  149.8 28.2 %copy-start.25 = (f32[196,192]{1,0:T(8,128)}, f32[196,192]{1,0:T(8,128)S(1)}, u32[]{:S(2)}) copy-start(f32[196,192]{1,0:T(8,128)S(1)} %get-tuple-element.114) | copy-start | bytes 451588
  149.8 31.3 %copy-start.30 = (f32[1,18432]{1,0:T(1,128)S(1)}, f32[1,18432]{1,0:T(1,128)}, u32[]{:S(2)}) copy-start(f32[1,18432]{1,0:T(1,128)} %param.29) | copy-start | bytes 221188
  177.4 32.1 %collective-permute-start.13 = (bf16[5,384,384]{2,1,0:T(8,128)(2,1)}, bf16[5,384,384]{2,1,0:T(8,128)(2,1)S(1)}, u32[]{:S(2)}, u32[]{:S(2)}) collective-permute-start(bf16[5,384,384]{2,1,0:T(8,128)(2,1)} %collective-permute-done.9.refs_10_), channel_id=1, source_target_pairs={{0,1},{1,0},{2,3},{3,2},{4,5},{5,4},{6,7},{7,6},{8,9},{9,8},{10,11... | collective-permute-start | bytes 4423688 | tf_op jit(solution)/shard_map/ppermute | solution.py:987
  178.1 31.8 %collective-permute-start.14 = (bf16[5,384,384]{2,1,0:T(8,128)(2,1)}, bf16[5,384,384]{2,1,0:T(8,128)(2,1)S(1)}, u32[]{:S(2)}, u32[]{:S(2)}) collective-permute-start(bf16[5,384,384]{2,1,0:T(8,128)(2,1)} %collective-permute-done.11.refs_13_), channel_id=1, source_target_pairs={{0,2},{1,3},{2,0},{3,1},{4,6},{5,7},{6,4},{7,5},{8,10},{9,11},{10,... | collective-permute-start | bytes 4423688 | tf_op jit(solution)/shard_map/ppermute | solution.py:987
  211.1 26.4 %copy-start.27 = (bf16[2,196,768]{2,0,1:T(2,128)(2,1)S(1)}, bf16[2,196,768]{2,0,1:T(2,128)(2,1)}, u32[]{:S(2)}) copy-start(bf16[2,196,768]{2,0,1:T(2,128)(2,1)} %param.16) | copy-start | bytes 1806340
  236.0 13.7 %collective-permute-start.15 = (bf16[256,768]{1,0:T(8,128)(2,1)}, bf16[256,768]{1,0:T(8,128)(2,1)S(1)}, u32[]{:S(2)}, u32[]{:S(2)}) collective-permute-start(bf16[256,768]{1,0:T(8,128)(2,1)} %get-tuple-element.58), channel_id=1, source_target_pairs={{0,16},{1,17},{2,18},{3,19},{4,20},{5,21},{6,22},{7,23},{8,24},{9,... | collective-permute-start | bytes 1179656 | tf_op jit(solution)/shard_map/ppermute | solution.py:51
  237.5 159.0 %copy-start.45 = (pred[208]{0:T(512)(128)(4,1)}, pred[208]{0:T(512)(128)(4,1)S(1)}, u32[]{:S(2)}) copy-start(pred[208]{0:T(512)(128)(4,1)S(1)} %iota_compare_fusion.12) | copy-start | bytes 628
  259.8 45.1 %collective-permute-start.16 = (bf16[256,768]{1,0:T(8,128)(2,1)}, bf16[256,768]{1,0:T(8,128)(2,1)S(1)}, u32[]{:S(2)}, u32[]{:S(2)}) collective-permute-start(bf16[256,768]{1,0:T(8,128)(2,1)} %get-tuple-element.59), channel_id=1, source_target_pairs={{16,0},{17,1},{18,2},{19,3},{20,4},{21,5},{22,6},{23,7},{24,8},{25... | collective-permute-start | bytes 1179656 | tf_op jit(solution)/shard_map/ppermute | solution.py:51
  269.1 118.8 %collective-permute-start.29 = (f16[2,2,2,208,384]{4,3,0,2,1:T(8,128)(2,1)}, f16[2,2,2,208,384]{4,3,0,2,1:T(8,128)(2,1)}, u32[]{:S(2)}, u32[]{:S(2)}) collective-permute-start(f16[2,2,2,208,384]{4,3,0,2,1:T(8,128)(2,1)} %get-tuple-element.127), channel_id=1, source_target_pairs={{16,18},{17,19},{18,16},{19,17},{20,22},{21,23},{22,20},{23,21},{2... | collective-permute-start | bytes 3833864 | tf_op jit(solution)/shard_map/ppermute | solution.py:987
  270.9 118.9 %collective-permute-start.25 = (f16[2,2,2,208,384]{4,3,0,2,1:T(8,128)(2,1)}, f16[2,2,2,208,384]{4,3,0,2,1:T(8,128)(2,1)}, u32[]{:S(2)}, u32[]{:S(2)}) collective-permute-start(f16[2,2,2,208,384]{4,3,0,2,1:T(8,128)(2,1)} %get-tuple-element.126), channel_id=1, source_target_pairs={{16,17},{17,16},{18,19},{19,18},{20,21},{21,20},{22,23},{23,22},{2... | collective-permute-start | bytes 3833864 | tf_op jit(solution)/shard_map/ppermute | solution.py:987
  379.5 44.7 %collective-permute-start.21 = (f16[2,2,2,592,384]{4,3,0,1,2:T(8,128)(2,1)}, f16[2,2,2,592,384]{4,3,0,1,2:T(8,128)(2,1)}, u32[]{:S(2)}, u32[]{:S(2)}) collective-permute-start(f16[2,2,2,592,384]{4,3,0,1,2:T(8,128)(2,1)} %fusion.5), channel_id=1, source_target_pairs={{0,2},{1,3},{2,0},{3,1},{4,6},{5,7},{6,4},{7,5},{8,10},{9,11},{10,... | collective-permute-start | bytes 10911752 | tf_op jit(solution)/shard_map/ppermute | solution.py:987
  384.8 53.6 %collective-permute-start.17 = (f16[2,2,2,688,384]{4,3,0,2,1:T(8,128)(2,1)}, f16[2,2,2,688,384]{4,3,0,2,1:T(8,128)(2,1)}, u32[]{:S(2)}, u32[]{:S(2)}) collective-permute-start(f16[2,2,2,688,384]{4,3,0,2,1:T(8,128)(2,1)} %fusion.2), channel_id=1, source_target_pairs={{0,1},{1,0},{2,3},{3,2},{4,5},{5,4},{6,7},{7,6},{8,9},{9,8},{10,11... | collective-permute-start | bytes 12681224 | tf_op jit(solution)/shard_map/ppermute | solution.py:987
  398.4 2.4 collective-permute-start.30
  399.2 2.0 collective-permute-start.26
  435.5 30.3 %collective-permute-start.22 = (f16[2,2,592,384]{3,2,0,1:T(8,128)(2,1)}, f16[2,2,592,384]{3,2,0,1:T(8,128)(2,1)}, u32[]{:S(2)}, u32[]{:S(2)}) collective-permute-start(f16[2,2,592,384]{3,2,0,1:T(8,128)(2,1)} %fusion.7), channel_id=1, source_target_pairs={{0,1},{1,0},{2,3},{3,2},{4,5},{5,4},{6,7},{7,6},{8,9},{9,8},{10,11... | collective-permute-start | bytes 5455880 | tf_op jit(solution)/shard_map/ppermute | solution.py:987
  453.3 28.4 %collective-permute-start.18 = (f16[2,2,688,384]{3,2,0,1:T(8,128)(2,1)}, f16[2,2,688,384]{3,2,0,1:T(8,128)(2,1)}, u32[]{:S(2)}, u32[]{:S(2)}) collective-permute-start(f16[2,2,688,384]{3,2,0,1:T(8,128)(2,1)} %fusion.6), channel_id=1, source_target_pairs={{0,4},{1,5},{2,6},{3,7},{4,0},{5,1},{6,2},{7,3},{8,12},{9,13},{10,... | collective-permute-start | bytes 6340616 | tf_op jit(solution)/shard_map/ppermute | solution.py:987
  457.5 1.4 collective-permute-start.31
  458.1 2.1 collective-permute-start.27
  461.9 1.4 collective-permute-start.28
  462.6 2.0 collective-permute-start.32
  472.8 20.3 %collective-permute-start.23 = (f16[2,592,384]{2,1,0:T(8,128)(2,1)}, f16[2,592,384]{2,1,0:T(8,128)(2,1)}, u32[]{:S(2)}, u32[]{:S(2)}) collective-permute-start(f16[2,592,384]{2,1,0:T(8,128)(2,1)} %fusion.15), channel_id=1, source_target_pairs={{0,4},{1,5},{2,6},{3,7},{4,0},{5,1},{6,2},{7,3},{8,12},{9,13},{10,... | collective-permute-start | bytes 2727944 | tf_op jit(solution)/shard_map/ppermute | solution.py:987
  490.1 16.8 %collective-permute-start.19 = (f16[2,688,384]{2,1,0:T(8,128)(2,1)S(1)}, f16[2,688,384]{2,1,0:T(8,128)(2,1)S(1)}, u32[]{:S(2)}, u32[]{:S(2)}) collective-permute-start(f16[2,688,384]{2,1,0:T(8,128)(2,1)S(1)} %fusion.14), channel_id=1, source_target_pairs={{0,2},{1,3},{2,0},{3,1},{4,6},{5,7},{6,4},{7,5},{8,10},{9,11},{10,... | collective-permute-start | bytes 3170312 | tf_op jit(solution)/shard_map/ppermute | solution.py:987
  498.3 29.4 %collective-permute-start.24 = (f16[592,384]{1,0:T(8,128)(2,1)}, f16[592,384]{1,0:T(8,128)(2,1)}, u32[]{:S(2)}, u32[]{:S(2)}) collective-permute-start(f16[592,384]{1,0:T(8,128)(2,1)} %fusion.19), channel_id=1, source_target_pairs={{0,8},{1,9},{2,10},{3,11},{4,12},{5,13},{6,14},{7,15},{8,0},{9,1},... | collective-permute-start | bytes 1363976 | tf_op jit(solution)/shard_map/ppermute | solution.py:987
  510.0 30.5 %collective-permute-start.20 = (f16[688,384]{1,0:T(8,128)(2,1)S(1)}, f16[688,384]{1,0:T(8,128)(2,1)}, u32[]{:S(2)}, u32[]{:S(2)}) collective-permute-start(f16[688,384]{1,0:T(8,128)(2,1)S(1)} %fusion.18), channel_id=1, source_target_pairs={{0,8},{1,9},{2,10},{3,11},{4,12},{5,13},{6,14},{7,15},{8,0},{9,1},... | collective-permute-start | bytes 1585160 | tf_op jit(solution)/shard_map/ppermute | solution.py:987
  548.4 13.8 %copy-start.37 = (f32[1,6912]{1,0:T(1,128)S(1)}, f32[1,6912]{1,0:T(1,128)}, u32[]{:S(2)}) copy-start(f32[1,6912]{1,0:T(1,128)} %get-tuple-element.75) | copy-start | bytes 82948
  548.4 14.0 %copy-start.36 = (f32[1,11520]{1,0:T(1,128)S(1)}, f32[1,11520]{1,0:T(1,128)}, u32[]{:S(2)}) copy-start(f32[1,11520]{1,0:T(1,128)} %get-tuple-element.74) | copy-start | bytes 138244
  548.4 44.6 %all-to-all-start = ((f16[16,136,384]{2,1,0:T(8,128)(2,1)}), f16[16,136,384]{2,1,0:T(8,128)(2,1)S(1)}, u32[]{:S(2)}, u32[]{:S(2)}) async-start(f16[16,136,384]{2,1,0:T(8,128)(2,1)} %select_convert_fusion), calls=%async_computation | async-start | bytes 3342336 | tf_op jit(solution)/shard_map/all_to_all | solution.py:1166
  562.6 4.2 collective-permute-start.37
  566.7 4.2 collective-permute-start.38
  568.7 5.0 collective-permute-start.33
  570.9 7.9 %collective-permute-start.39 = (f32[11648]{0:T(1024)S(1)}, f32[11648]{0:T(1024)S(1)}, u32[]{:S(2)}, u32[]{:S(2)}) collective-permute-start(f32[11648]{0:T(1024)S(1)} %add.320), channel_id=1, source_target_pairs={{0,4},{1,5},{2,6},{3,7},{4,0},{5,1},{6,2},{7,3},{8,12},{9,13},{10,... | collective-permute-start | bytes 139784 | tf_op jit(solution)/shard_map/ppermute | solution.py:987
  573.6 5.2 collective-permute-start.34
  578.8 5.0 collective-permute-start.40
  578.9 5.0 collective-permute-start.35
  583.9 4.5 collective-permute-start.36
  589.2 1.1 collective-permute-start.41
  644.7 85.8 %collective-permute-start.42 = (bf16[5,384,384]{2,1,0:T(8,128)(2,1)}, bf16[5,384,384]{2,1,0:T(8,128)(2,1)S(1)}, u32[]{:S(2)}, u32[]{:S(2)}) collective-permute-start(bf16[5,384,384]{2,1,0:T(8,128)(2,1)} %convert_element_type.335), channel_id=1, source_target_pairs={{0,16},{1,17},{2,18},{3,19},{4,20},{5,21},{6,22},{7,23},{8,24},{9,... | collective-permute-start | bytes 4423688 | tf_op jit(solution)/shard_map/ppermute | solution.py:51
  646.9 2.1 collective-permute-start.43
  713.9 16.7 %copy-start.4 = (f32[1,5,384,384]{3,2,1,0:T(8,128)S(1)}, f32[1,5,384,384]{3,2,1,0:T(8,128)}, u32[]{:S(2)}) copy-start(f32[1,5,384,384]{3,2,1,0:T(8,128)} %param.22) | copy-start | bytes 8847364
  713.9 16.7 %copy-start.16 = (f32[5,384,384]{2,1,0:T(8,128)S(1)}, f32[5,384,384]{2,1,0:T(8,128)}, u32[]{:S(2)}) copy-start(f32[5,384,384]{2,1,0:T(8,128)} %get-tuple-element.77) | copy-start | bytes 8847364
  (35 other events, 196.4 us)
where the time goes:
time: 748 us; the launch traced here: 734 us
  waiting for transfers between devices  272 us (36%)
  Pallas kernels  208 us (28%)
  other arithmetic  91 us (12%)
  starting transfers between devices  71.7 us (10%)
  local copies, waits for them, and re-layouts  62.6 us (8%)
  between operations  20.8 us (3%)
  matrix products  8.08 us (1%)
    ppermute x39, waiting for transfers between devices, swap(): return lax.ppermute(value, ('section', 'dp'), pairs)  238 us
    pallas_call x4, Pallas kernels, call_kernel(): pl.pallas_call(guarded, grid_spec=pltpu.PrefetchScalarGridSpec(num_scalar...  80.1 us
    pallas_call x1, Pallas kernels, soap_factor(): pl.pallas_call(factor_kernel, grid_spec=pltpu.PrefetchScalarGridSpec(num_...  64.2 us
    ppermute x39, starting transfers between devices, swap(): return lax.ppermute(value, ('section', 'dp'), pairs)  55.1 us
    pallas_call x1, Pallas kernels, soap_first(): pl.pallas_call(first_kernel, grid_spec=pltpu.PrefetchScalarGridSpec(num_s...  45.9 us
    add x16, other arithmetic, halve(): parts[k] = keep + arrived.astype(f32) * unscale  39.3 us
    ppermute x4, waiting for transfers between devices, from_behind(): return lax.ppermute(shard, axis, pairs)  33.1 us
    dynamic_slice x4, local copies, waits for them, and re-layouts, halve(): give = lax.dynamic_index_in_dim(part, 1 - mine, axis, keepdims=False)  27.6 us
  transfers between devices with their start and end apart: 45, of which 28 were waited for; matrix products, arithmetic and copies ran while one was open for 19% of the time, Pallas kernels for 18%

commit v1 on v0

--- a/solution.py
+++ b/solution.py
@@ -511,12 +511,39 @@
     out_ref[...] = norm_parts(norm(hid, vec[10], vec[11]))[0]
 
 
-def put_block(ref, value, j, depth):
-    edge = value.shape[-1]
-    if depth % 8:
-        ref[j] = value
-    else:
-        ref[:, depth * j : depth * j + depth, :] = value.reshape(edge // depth, depth, edge)
+class Flow:
+    def __init__(self, outs, stage, depth, me):
+        self.outs, self.stage, self.depth, self.me = outs, stage, depth, me
+
+    def put(self, value, j):
+        edge, depth = value.shape[-1], self.depth
+        if depth % 8:
+            self.stage[j] = value
+        else:
+            cut = value.reshape(self.stage.shape[:2] + (depth, edge))
+            self.stage[:, :, depth * j : depth * j + depth, :] = cut
+
+    def copies(self, start, count, sems):
+        depth = self.depth
+        if depth % 8:
+            target = self.outs[0].at[pl.ds(start, count)]
+            return [pltpu.make_async_copy(self.stage.at[pl.ds(0, count)], target, sems[0])]
+        group = len(self.outs)
+        mine = self.me & (group - 1)
+        made = []
+        for p in range(group):
+            source = self.stage.at[:, mine ^ p, pl.ds(0, depth * count), :]
+            target = self.outs[p].at[:, pl.ds(depth * start, depth * count), :]
+            made.append(pltpu.make_async_copy(source, target, sems[p]))
+        return made
+
+
+GROUP_BITS = 2
+GROUP = 1 << GROUP_BITS
+
+
+def sems_of(ref, turn):
+    return [ref.at[turn, p] for p in range(GROUP)]
 
 
 def raise_top(top_ref, value):
@@ -525,12 +552,12 @@
 
 def predictor_kernel(
     depth, slots, table, z_ref, pos_c_ref, pos_t_ref, valid_ref, tgt_ref, tmask_ref, vec_ref,
-    dz_out, flow_a, flow_b, vec_out, loss_out, top_out,
-    win, wqkv, wo, w1, w2, wout, q, k, v, att, go, dq, dk, dv, pre_ref, act_ref, dpre_ref, acc, sems,
+    dz_out, out_0, out_1, out_2, out_3, vec_out, loss_out, top_out,
+    win, wqkv, wo, w1, w2, wout, q, k, v, att, go, dq, dk, dv, pre_ref, act_ref, dpre_ref, acc, stage, sems, flow_sems,
 ):
     vec, grads = Vec(vec_ref, pred_lengths()), Vec(vec_out, pred_lengths())
     edge = table[0].shape[-1]
-    half = flow_split(NBP)
+    flow = Flow((out_0, out_1, out_2, out_3), stage, depth, slots[2 * (NBE + NBP) + 1])
     images = z_ref.shape[0] // LC
     groups = load_blocks(table, slots, sems, NBE, pred_shapes(), (win, wqkv, wo, w1, w2, wout))
     start_all(groups)
@@ -544,10 +571,7 @@
                 j = firsts[index] + row * (pred_shapes()[index][1] // edge) + column
                 value = matrix[row * edge : row * edge + edge, column * edge : column * edge + edge]
                 raise_top(top_out, value)
-                if j < half:
-                    put_block(flow_a, value, j, depth)
-                else:
-                    put_block(flow_b, value, j - half, depth)
+                flow.put(value, j)
 
     top_out[...] = jnp.zeros_like(top_out)
     z = z_ref[...]
@@ -632,56 +656,60 @@
     low = dx_c.astype(bf)
     dz_out[...] = mm(low, win[...], RIGHT_T).astype(bf)
     store(0, mm(z.T, low))
-
-
-def flow_split(count):
-    return (count // 2 + 3) // 4 * 4
-
-
-def encoder_back_kernel(
-    depth, slots, table, dz_ref, rows_ref, e_ref, q, k, v, att_ref, mid_ref, pre_ref, hid_ref, valid_ref, vec_ref,
-    flow_a, flow_b, vec_out, top_out,
-    wqkv, wo, w1, w2, go, dq, dk, dv, act_t, dpre_ref, x_t, dqkv, acc, stage, sems, out_sems,
-):
-    vec, grads = Vec(vec_ref, enc_lengths()), Vec(vec_out, enc_lengths())
-    edge = table[0].shape[-1]
-    half = flow_split(NBE)
-    groups = load_blocks(table, slots, sems, 0, enc_shapes(), (None, wqkv, wo, w1, w2))
-    start_all(groups[::-1])
-    firsts = offsets([h * b // (edge * edge) for h, b in enc_shapes()])
-    sent = []
-
-    def store(index, left_t, right):
-        columns = enc_shapes()[index][1] // edge
-        rows = enc_shapes()[index][0] // edge
+    leaving = flow.copies(0, NBP, sems_of(flow_sems, 0))
+    for copy in leaving:
+        copy.start()
+    for copy in leaving:
+        copy.wait()
+
+
+class Store:
+    def __init__(self, top, sems):
+        self.top, self.sems, self.sent = top, sems, []
+
+    def run(self, flow, slots, start, shape, left_t, right):
+        edge = slots.shape[-1]
+        columns, rows = shape[1] // edge, shape[0] // edge
         for first in range(0, rows * columns, 4):
-            turn = len(sent)
-            slot = turn % 2
+            turn = len(self.sent)
             if turn >= 2:
-                sent[turn - 2].wait()
+                for copy in self.sent[turn - 2]:
+                    copy.wait()
+            flow.stage = slots.at[turn % 2]
             for b in range(4):
                 row, column = divmod(first + b, columns)
                 value = mm(
                     left_t[row * edge : row * edge + edge, :],
                     right[:, column * edge : column * edge + edge],
                 )
-                raise_top(top_out, value)
-                put_block(stage.at[slot], value, b, depth)
-            j = firsts[index] + first
-            target, start = (flow_a, j) if j < half else (flow_b, j - half)
-            if depth % 8:
-                spot = target.at[pl.ds(start, 4)]
-            else:
-                spot = target.at[:, pl.ds(depth * start, 4 * depth), :]
-            copy = pltpu.make_async_copy(stage.at[slot], spot, out_sems.at[turn])
-            copy.start()
-            sent.append(copy)
-
+                raise_top(self.top, value)
+                flow.put(value, b)
+            made = flow.copies(start + first, 4, sems_of(self.sems, turn))
+            for copy in made:
+                copy.start()
+            self.sent.append(made)
+
+    def finish(self):
+        for made in self.sent[-2:]:
+            for copy in made:
+                copy.wait()
+
+
+def feed_back_kernel(
+    depth, slots, table, dz_ref, mid_ref, pre_ref, hid_ref, vec_ref,
+    out_0, out_1, out_2, out_3, dmid_out, vec_out, top_out,
+    w1, w2, act_t, dpre_ref, x_t, low_ref, acc, stage, sems, out_sems,
+):
+    vec, grads = Vec(vec_ref, enc_lengths()), Vec(vec_out, enc_lengths())
+    flow = Flow((out_0, out_1, out_2, out_3), None, depth, slots[2 * (NBE + NBP) + 1])
+    groups = load_blocks(table, slots, sems, 0, enc_shapes(), (None, None, None, w1, w2))
+    start_all(groups)
     top_out[...] = jnp.zeros_like(top_out)
     hid = hid_ref[...]
     dy, grads[10], grads[11] = norm_back(hid, vec[10], dz_ref[...].astype(f32))
     grads[9] = col_sum(dy)
     low = dy.astype(bf)
+    low_ref[...] = low
     wait_group(groups[4])
     wait_group(groups[3])
     acc[...] = jnp.zeros_like(acc)
@@ -698,15 +726,28 @@
         return carry
 
     lax.fori_loop(0, FF // STRIP, strip, 0)
-    dqkv[:, :D] = low
-    store(4, act_t, dqkv)
     mid = mid_ref[...]
-    unit, _ = norm_parts(mid)
-    x_t[...] = (unit * vec[6] + vec[7]).astype(bf).T
-    store(3, x_t, dpre_ref)
     dmid, grads[6], grads[7] = norm_back(mid, vec[6], acc[...])
-    dmid = dmid + dy
-    acc[...] = dmid
+    dmid_out[...] = dmid + dy
+    x_t[...] = (norm_parts(mid)[0] * vec[6] + vec[7]).astype(bf).T
+    store = Store(top_out, out_sems)
+    store.run(flow, stage, 16, (FF, D), act_t, low_ref)
+    store.run(flow, stage, 0, (D, FF), x_t, dpre_ref)
+    store.finish()
+
+
+def attention_back_kernel(
+    depth, slots, table, dmid_ref, rows_ref, e_ref, q, k, v, att_ref, valid_ref, vec_ref,
+    out_0, out_1, out_2, out_3, vec_out, top_out,
+    wqkv, wo, go, dq, dk, dv, x_t, dqkv, stage, sems, out_sems,
+):
+    vec, grads = Vec(vec_ref, enc_lengths()), Vec(vec_out, enc_lengths())
+    flow = Flow((out_0, out_1, out_2, out_3), None, depth, slots[2 * (NBE + NBP) + 1])
+    groups = load_blocks(table, slots, sems, 0, enc_shapes(), (None, wqkv, wo, None, None))
+    start_all(groups[::-1])
+    top_out[...] = jnp.zeros_like(top_out)
+    store = Store(top_out, out_sems)
+    dmid = dmid_ref[...]
     grads[5] = col_sum(dmid)
     low = dmid.astype(bf)
     wait_group(groups[2])
@@ -714,7 +755,7 @@
     split_rows(go, mm(low, wo[...], RIGHT_T))
     x_t[...] = flat(att_ref).T
     dqkv[:, :D] = low
-    store(2, x_t, dqkv)
+    store.run(flow, stage, 16, (D, D), x_t, dqkv)
     attend_back(q, k, v, valid_ref, go, dq, dk, dv, H)
     d_q, d_v = flat(dq), flat(dv)
     grads[3] = col_sum(d_q)
@@ -724,15 +765,14 @@
     dqkv[:, 2 * D :] = d_v.astype(bf)
     e = e_ref[...]
     x_t[...] = norm(e, vec[1], vec[2]).astype(bf).T
-    store(1, x_t, dqkv)
+    store.run(flow, stage, 4, (D, 3 * D), x_t, dqkv)
     back, grads[1], grads[2] = norm_back(e, vec[1], mm(dqkv[...], wqkv[...], RIGHT_T))
-    de = acc[...] + back
+    de = dmid_ref[...] + back
     grads[0] = col_sum(de)
     dqkv[:, :D] = de.astype(bf)
     x_t[...] = rows_ref[...].T
-    store(0, x_t, dqkv)
-    for copy in sent[-2:]:
-        copy.wait()
+    store.run(flow, stage, 0, (PIX, D), x_t, dqkv)
+    store.finish()
 
 
 def spaces(count):
@@ -746,23 +786,54 @@
     return [pltpu.VMEM(shape, bf) for shape in shapes]
 
 
-def call_kernel(body, section, places, table, args, outs, any_outs, scratch, name):
-    count = len(table)
+def call_kernel(body, section, places, table, args, outs, any_outs, scratch, name, micros):
+    pieces, n_in, n_out = len(table), len(args), len(outs)
+    inside = [i for i in range(n_out) if i not in any_outs]
+    held = [pltpu.VMEM(a.shape, a.dtype) for a in args]
+    held += [pltpu.VMEM(outs[i][0], outs[i][1]) for i in inside]
+    n_held = len(held)
 
     def guarded(places_ref, *refs):
         @pl.when(places_ref[2 * (NBE + NBP)] == section)
         def run():
-            body(places_ref, refs[:count], *refs[count:])
-
-    specs = [ANYWHERE] * count + spaces(len(args))
-    out_specs = [ANYWHERE if i in any_outs else spaces(1)[0] for i in range(len(outs))]
+            sources = refs[:pieces]
+            given = refs[pieces : pieces + n_in]
+            results = list(refs[pieces + n_in : pieces + n_in + n_out])
+            local = refs[pieces + n_in + n_out :]
+            mine, rest, sems = local[:n_held], local[n_held:-1], local[-1]
+            loads = [
+                pltpu.make_async_copy(given[i], mine[i], sems.at[i]) for i in range(n_in)
+            ]
+            for copy in loads:
+                copy.start()
+            stores = []
+            for place, i in enumerate(inside):
+                stores.append(
+                    pltpu.make_async_copy(mine[n_in + place], results[i], sems.at[n_in + place])
+                )
+                results[i] = mine[n_in + place]
+            for copy in loads:
+                copy.wait()
+            body(places_ref, sources, *mine[:n_in], *results, *rest)
+            for copy in stores:
+                copy.start()
+            for copy in stores:
+                copy.wait()
+
     return pl.pallas_call(
         guarded,
         grid_spec=pltpu.PrefetchScalarGridSpec(
-            num_scalar_prefetch=1, grid=(), in_specs=specs, out_specs=out_specs, scratch_shapes=scratch
+            num_scalar_prefetch=1,
+            grid=(),
+            in_specs=[ANYWHERE] * (pieces + n_in),
+            out_specs=[ANYWHERE] * n_out,
+            scratch_shapes=held + scratch + [pltpu.SemaphoreType.DMA((n_held,))],
         ),
         out_shape=[jax.ShapeDtypeStruct(shape, kind) for shape, kind in outs],
         compiler_params=pltpu.CompilerParams(vmem_limit_bytes=58 << 20),
+        cost_estimate=pl.CostEstimate(
+            flops=0, transcendentals=0, bytes_accessed=int(micros * 3.0e6)
+        ),
         name=name,
     )(places, *table, *args)
 
@@ -770,11 +841,16 @@
 MARKS = 16
 
 
-def flow_shapes(count, edge, ranks):
-    half = flow_split(count)
-    if (edge // ranks) % 8:
-        return [((n, edge, edge), f32) for n in (half, count - half)]
-    return [((ranks, edge // ranks * n + MARKS, edge), f32) for n in (half, count - half)]
+def flow_outs(count, edge, ranks):
+    depth = edge // ranks
+    if depth % 8:
+        return [((count, edge, edge), f32)] + [((8, edge), f32)] * (GROUP - 1)
+    return [((ranks // GROUP, depth * count + MARKS, edge), f32)] * GROUP
+
+
+def stage_shape(count, edge, ranks):
+    depth = edge // ranks
+    return (count, edge, edge) if depth % 8 else (ranks // GROUP, GROUP, depth * count, edge)
 
 
 def encoder_call(slots, table, rows, pos, valid, vec):
@@ -785,7 +861,7 @@
     outs += [((n, D), f32), ((n, FF), f32), ((n, D), f32)]
     scratch = weight_scratch(enc_shapes()) + [pltpu.VMEM((n, D), f32), pltpu.SemaphoreType.DMA((NBE,))]
     args = (rows, pos, valid, vec)
-    return call_kernel(encoder_kernel, 0, slots, table, args, outs, (), scratch, "encoder_forward")
+    return call_kernel(encoder_kernel, 0, slots, table, args, outs, (), scratch, "encoder_forward", 25)
 
 
 def target_call(slots, table, rows, pos, some, pos_some, valid, vec, images):
@@ -802,7 +878,7 @@
     ]
     args = (rows, pos, some, pos_some, valid, vec)
     outs = [((n, D), f32)]
-    return call_kernel(target_kernel, 1, slots, table, args, outs, (), scratch, "target_forward")[0]
+    return call_kernel(target_kernel, 1, slots, table, args, outs, (), scratch, "target_forward", 25)[0]
 
 
 def predictor_call(slots, table, z, pos_c, pos_t, valid, tgt, tmask, vec, ranks):
@@ -811,7 +887,8 @@
     rows, keys = m // images, valid.shape[-1]
     edge = table[0].shape[-1]
     per, wide = (images, rows, PD), (images, keys, PD)
-    outs = [((n, D), bf)] + flow_shapes(NBP, edge, ranks) + [((1, VP), f32), ((1, D), f32), ((1, edge), f32)]
+    outs = [((n, D), bf)] + flow_outs(NBP, edge, ranks)
+    outs += [((1, VP), f32), ((1, D), f32), ((1, edge), f32)]
     scratch = weight_scratch(pred_shapes()) + [
         pltpu.VMEM(per, bf),
         pltpu.VMEM(wide, bf),
@@ -825,39 +902,57 @@
         pltpu.VMEM((m, PFF), bf),
         pltpu.VMEM((m, PFF), bf),
         pltpu.VMEM((m, PD), f32),
+        pltpu.VMEM(stage_shape(NBP, edge, ranks), f32),
         pltpu.SemaphoreType.DMA((NBE + NBP,)),
+        pltpu.SemaphoreType.DMA((1, GROUP)),
     ]
     args = (z, pos_c, pos_t, valid, tgt, tmask, vec)
     body = functools.partial(predictor_kernel, edge // ranks)
-    return call_kernel(body, 1, slots, table, args, outs, (), scratch, "predictor_step")
-
-
-def encoder_back_call(slots, table, dz, rows, kept, valid, vec, ranks):
+    return call_kernel(body, 1, slots, table, args, outs, (1, 2, 3, 4), scratch, "predictor_step", 50)
+
+
+def feed_back_call(slots, table, dz, kept, vec, ranks):
+    n = dz.shape[0]
+    edge = table[0].shape[-1]
+    mid, pre, hid = kept
+    scratch = weight_scratch(enc_shapes()[3:]) + [
+        pltpu.VMEM((FF, n), bf),
+        pltpu.VMEM((n, FF), bf),
+        pltpu.VMEM((D, n), bf),
+        pltpu.VMEM((n, D), bf),
+        pltpu.VMEM((n, D), f32),
+        pltpu.VMEM((2,) + stage_shape(4, edge, ranks), f32),
+        pltpu.SemaphoreType.DMA((NBE,)),
+        pltpu.SemaphoreType.DMA((8, GROUP)),
+    ]
+    outs = flow_outs(32, edge, ranks)
+    outs += [((n, D), f32), ((1, VE), f32), ((1, edge), f32)]
+    args = (dz, mid, pre, hid, vec)
+    body = functools.partial(feed_back_kernel, edge // ranks)
+    return call_kernel(body, 0, slots, table, args, outs, (0, 1, 2, 3), scratch, "feed_backward", 25)
+
+
+def attention_back_call(slots, table, dmid, rows, kept, valid, vec, ranks):
     n = rows.shape[0]
     images = n // LC
     edge = table[0].shape[-1]
     per = (images, LC, D)
-    e, q, k, v, att, mid, pre, hid = kept
-    depth = edge // ranks
-    stage = (2, ranks, 4 * depth, edge) if depth % 8 == 0 else (2, 4, edge, edge)
-    scratch = weight_scratch(enc_shapes()[1:]) + [
+    e, q, k, v, att = kept
+    scratch = weight_scratch(enc_shapes()[1:3]) + [
         pltpu.VMEM(per, bf),
         pltpu.VMEM(per, f32),
         pltpu.VMEM(per, f32),
         pltpu.VMEM(per, f32),
-        pltpu.VMEM((FF, n), bf),
-        pltpu.VMEM((n, FF), bf),
         pltpu.VMEM((D, n), bf),
         pltpu.VMEM((n, 3 * D), bf),
-        pltpu.VMEM((n, D), f32),
-        pltpu.VMEM(stage, f32),
+        pltpu.VMEM((2,) + stage_shape(4, edge, ranks), f32),
         pltpu.SemaphoreType.DMA((NBE,)),
-        pltpu.SemaphoreType.DMA((NBE // 4,)),
+        pltpu.SemaphoreType.DMA((5, GROUP)),
     ]
-    outs = flow_shapes(NBE, edge, ranks) + [((1, VE), f32), ((1, edge), f32)]
-    args = (dz, rows, e, q, k, v, att, mid, pre, hid, valid, vec)
-    body = functools.partial(encoder_back_kernel, edge // ranks)
-    return call_kernel(body, 0, slots, table, args, outs, (0, 1), scratch, "encoder_backward")
+    outs = flow_outs(20, edge, ranks) + [((1, VE), f32), ((1, edge), f32)]
+    args = (dmid, rows, e, q, k, v, att, valid, vec)
+    body = functools.partial(attention_back_kernel, edge // ranks)
+    return call_kernel(body, 0, slots, table, args, outs, (0, 1, 2, 3), scratch, "attention_backward", 25)
 
 
 def soap_first(flags, factor, *arrays):
@@ -956,20 +1051,22 @@
 )
 
 
-def gather_pieces(own):
+def gather_pieces(own, extra):
     both = Exchange((0, 1))
     if both.ranks != 16:
-        return None
+        return None, extra
     held = {0: own}
-    for moves, awaited in ROUNDS:
+    for number, (moves, awaited) in enumerate(ROUNDS):
         names = sorted({piece ^ (1 << bit) for piece, bit in moves} | set(awaited))
         values = [held[name] for name in names]
-        if awaited:
+        if number == 2:
+            values, extra = lax.optimization_barrier((values, extra))
+        elif awaited:
             values = lax.optimization_barrier(values)
         source = dict(zip(names, values))
         for piece, bit in moves:
             held[piece] = both.swap(source[piece ^ (1 << bit)], bit)
-    return [held[piece] for piece in range(both.ranks)]
+    return [held[piece] for piece in range(both.ranks)], extra
 
 
 class Exchange:
@@ -979,8 +1076,11 @@
         self.sections = sections
 
     def swap(self, value, bit):
+        return self.trade(value, 1 << bit)
+
+    def trade(self, value, flip):
         pairs = [
-            (s * self.ranks + i, s * self.ranks + (i ^ (1 << bit)))
+            (s * self.ranks + i, s * self.ranks + (i ^ flip))
             for s in self.sections
             for i in range(self.ranks)
         ]
@@ -1002,34 +1102,49 @@
     return marked.astype(WIRE)
 
 
-def halve(exchange, flows, orders, bound):
-    bits = exchange.bits
-    me = lax.axis_index("dp")
-    parts = [f.reshape((2,) * bits + f.shape[1:]) for f in flows]
-    bounds = [bound for _ in flows]
-    left = [list(range(bits - 1, -1, -1)) for _ in flows]
-    for stage in range(bits):
-        for k, part in enumerate(parts):
-            bit = orders[k][stage]
-            axis = left[k].index(bit)
-            mine = (me >> bit) & 1
-            give = lax.dynamic_index_in_dim(part, 1 - mine, axis, keepdims=False)
-            arrived = exchange.swap(pack(give, wire_exponent(bounds[k])), bit)
-            keep = lax.dynamic_index_in_dim(part, mine, axis, keepdims=False)
-            unscale = jnp.exp2(-arrived[..., -1, 0].reshape(-1)[0].astype(f32))
-            parts[k] = keep + arrived.astype(f32) * unscale
-            bounds[k] = bounds[k] + WIRE_TOP * unscale
-            left[k].remove(bit)
-    return [part[:-MARKS] for part in parts], sum(bounds)
-
-
-def by_share(flow, ranks):
-    if flow.shape[0] == ranks and flow.shape[1] != flow.shape[2]:
-        return flow
-    blocks, edge = flow.shape[:2]
-    cut = flow.reshape(blocks, ranks, edge // ranks, edge)
-    cut = cut.transpose(1, 0, 2, 3).reshape(ranks, -1, edge)
-    return jnp.pad(cut, ((0, 0), (0, MARKS), (0, 0)))
+def flow_pieces(arrays, ranks):
+    if arrays[1].ndim == 3:
+        return list(arrays)
+    blocks, edge = arrays[0].shape[:2]
+    cut = arrays[0].reshape(blocks, ranks, edge // ranks, edge).transpose(1, 0, 2, 3)
+    cut = jnp.pad(cut.reshape(ranks, -1, edge), ((0, 0), (0, MARKS), (0, 0)))
+    return cut_pieces(cut, 0, GROUP)
+
+
+def cut_pieces(shares, shift, size):
+    mine = (lax.axis_index("dp") >> shift) & (size - 1)
+    cut = shares.reshape((shares.shape[0] // size, size) + shares.shape[1:])
+    return [lax.dynamic_index_in_dim(cut, mine ^ p, 1, keepdims=False) for p in range(size)]
+
+
+def pack_pieces(pieces, bound):
+    return [pack(piece, wire_exponent(bound)) for piece in pieces[1:]]
+
+
+def send_packed(exchange, lows, shift):
+    return [exchange.trade(low, (p + 1) << shift) for p, low in enumerate(lows)]
+
+
+def send_pieces(exchange, pieces, shift, bound):
+    return send_packed(exchange, pack_pieces(pieces, bound), shift)
+
+
+def add_pieces(keep, arrived, bound):
+    for got in arrived:
+        unscale = jnp.exp2(-got[0, -1, 0].astype(f32))
+        keep = keep + got.astype(f32) * unscale
+        bound = bound + WIRE_TOP * unscale
+    return keep, bound
+
+
+def finish_sum(exchange, shares, bound):
+    shift = GROUP_BITS
+    while shares.shape[0] > 1:
+        pieces = cut_pieces(shares, shift, min(GROUP, shares.shape[0]))
+        arrived = send_pieces(exchange, pieces, shift, bound)
+        shares, bound = add_pieces(pieces[0], arrived, bound)
+        shift += GROUP_BITS
+    return shares[0, :-MARKS], bound
 
 
 def on_device(
@@ -1057,14 +1172,6 @@
     second = section_index.astype(jnp.int32).reshape(1)
     slot_count = weights.shape[1]
     edge = weights.shape[-1]
-    own = weights[0].astype(bf)
-    table = gather_pieces(own)
-    if table is None:
-        table = [lax.all_gather(own, "dp", axis=0, tiled=True)]
-        places = jnp.concatenate([jnp.zeros_like(slot_of), slot_of, second])
-    else:
-        places = [jnp.bitwise_xor(slot_of // slot_count, owner_index), slot_of % slot_count, second]
-        places = jnp.concatenate(places)
     enc_slots = slot_of[:NBE]
     pred_slots = slot_of[NBE:]
     row_now = vectors[0]
@@ -1108,41 +1215,75 @@
     pred_pos_tgt = choose(tgt_hot, pos_pred)
 
     ctx_keys = ctx_valid[:, None, :]
-    encoded = encoder_call(places, table, pixel_rows, enc_pos_ctx, ctx_keys, enc_vec_now)
-    context = from_behind(encoded[0], "section", 1)
+    tgt_mask = tgt_valid.reshape(-1, 1)
+    ready = (
+        pixel_rows, enc_pos_ctx, ctx_keys, enc_vec_now, pixel_all, pos_all, pixel_tgt, enc_pos_tgt,
+        all_valid, pred_pos_ctx, pred_pos_tgt, joined_valid, tgt_mask, pred_vec_now,
+    )
+    own = weights[0].astype(bf)
+    place = [second, owner_index.astype(jnp.int32).reshape(1)]
+    table, ready = gather_pieces(own, ready)
+    if table is None:
+        table = [lax.all_gather(own, "dp", axis=0, tiled=True)]
+        places = jnp.concatenate([jnp.zeros_like(slot_of), slot_of] + place)
+    else:
+        sources = jnp.bitwise_xor(slot_of // slot_count, owner_index)
+        places = jnp.concatenate([sources, slot_of % slot_count] + place)
+    (
+        pixel_rows, enc_pos_ctx, ctx_keys, enc_vec_now, pixel_all, pos_all, pixel_tgt, enc_pos_tgt,
+        all_valid, pred_pos_ctx, pred_pos_tgt, joined_valid, tgt_mask, pred_vec_now,
+    ) = ready
+
+    z, *kept = encoder_call(places, table, pixel_rows, enc_pos_ctx, ctx_keys, enc_vec_now)
+    context = from_behind(z, "section", 1)
     target = target_call(
         places, table, pixel_all, pos_all, pixel_tgt, enc_pos_tgt, all_valid, enc_vec_now, images
     )
-    back_send, pred_a, pred_b, pred_vec, loss_lanes, pred_top = predictor_call(
-        places,
-        table,
-        context,
-        pred_pos_ctx,
-        pred_pos_tgt,
-        joined_valid,
-        target,
-        tgt_valid.reshape(-1, 1),
-        pred_vec_now,
-        ranks,
+    back_send, *pred_flows, pred_vec, loss_lanes, pred_top = predictor_call(
+        places, table, context, pred_pos_ctx, pred_pos_tgt, joined_valid, target, tgt_mask, pred_vec_now, ranks
     )
     incoming = from_behind(back_send, "section", -1)
     loss_local = jnp.where(is_first, 0.0, jnp.sum(loss_lanes))
 
-    low_order = list(range(Exchange((0,)).bits))
-    orders = [low_order, low_order]
-    if len(low_order) > 2:
-        orders = [[0, 2, 1] + low_order[3:], [1, 0, 2] + low_order[3:]]
-    pred_flows = [by_share(flow, ranks) for flow in (pred_a, pred_b)]
-    pred_parts, pred_bound = halve(Exchange((1,)), pred_flows, orders, jnp.max(pred_top))
-
-    enc_a, enc_b, enc_vec, enc_top = encoder_back_call(
-        places, table, incoming, pixel_rows, encoded[1:], ctx_keys, enc_vec_now, ranks
-    )
-    enc_flows = [by_share(flow, ranks) for flow in (enc_a, enc_b)]
-    enc_parts, enc_bound = halve(Exchange((0,)), enc_flows, orders, jnp.max(enc_top))
+    behind = Exchange((1,))
+
+    def sum_predictor(flows, top):
+        bound = jnp.max(top)
+        pieces = flow_pieces(flows, ranks)
+        shares, bound = add_pieces(pieces[0], send_pieces(behind, pieces, 0, bound), bound)
+        return finish_sum(behind, shares, bound)
+
+    def skip_predictor(flows, top):
+        return jnp.zeros((edge // ranks * NBP, edge), f32), jnp.zeros((), f32)
+
+    incoming, pred_top = lax.optimization_barrier((incoming, pred_top))
+    pred_sum, pred_bound = lax.cond(is_first, skip_predictor, sum_predictor, pred_flows, pred_top)
+    incoming, pred_sum = lax.optimization_barrier((incoming, pred_sum))
+    *feed_flow, grad_mid, feed_vec, feed_top = feed_back_call(
+        places, table, incoming, kept[5:], enc_vec_now, ranks
+    )
+    ahead = Exchange((0,))
+    feed_bound = jnp.max(feed_top)
+    feed_pieces = flow_pieces(feed_flow, ranks)
+    lows, grad_mid = lax.optimization_barrier((pack_pieces(feed_pieces, feed_bound), grad_mid))
+    feed_arrived = send_packed(ahead, lows, 0)
+    *rest_flow, rest_vec, rest_top = attention_back_call(
+        places, table, grad_mid, pixel_rows, kept[:5], ctx_keys, enc_vec_now, ranks
+    )
+    rest_bound = jnp.max(rest_top)
+    rest_pieces = flow_pieces(rest_flow, ranks)
+    lows = pack_pieces(rest_pieces, rest_bound)
+    feed_arrived, lows = lax.optimization_barrier((feed_arrived, lows))
+    rest_arrived = send_packed(ahead, lows, 0)
+    feed_shares, feed_bound = add_pieces(feed_pieces[0], feed_arrived, feed_bound)
+    rest_shares, rest_bound = add_pieces(rest_pieces[0], rest_arrived, rest_bound)
+    enc_shares = jnp.concatenate([rest_shares[:, :-MARKS], feed_shares], 1)
+    enc_sum, enc_bound = finish_sum(ahead, enc_shares, jnp.maximum(rest_bound, feed_bound))
+    cut_at = 6 * D
+    enc_vec = jnp.concatenate([rest_vec[:, :cut_at], feed_vec[:, cut_at:]], 1)
     depth = edge // ranks
-    enc_share = jnp.concatenate(enc_parts, 0).reshape(NBE, depth, edge)
-    pred_share = jnp.concatenate(pred_parts, 0).reshape(NBP, depth, edge)
+    enc_share = enc_sum.reshape(NBE, depth, edge)
+    pred_share = pred_sum.reshape(NBP, depth, edge)
 
     both = Exchange((0, 1))
     vec_local = jnp.where(is_first, enc_vec[0], jnp.pad(pred_vec[0], (0, VE - VP)))

time: 748 us -> 721 us (0.964)
  the two profiles are of different devices: /device:TPU:20 before, /device:TPU:4 now
where the time goes in v1:
time: 721 us; the launch traced here: 716 us
  waiting for transfers between devices  310 us (43%)
  Pallas kernels  219 us (30%)
  starting transfers between devices  74.5 us (10%)
  other arithmetic  57.9 us (8%)
  local copies, waits for them, and re-layouts  26.1 us (4%)
  between operations  17.4 us (2%)
  matrix products  11.2 us (2%)
    ppermute x32, waiting for transfers between devices, trade(): return lax.ppermute(value, ('section', 'dp'), pairs)  257 us
    pallas_call x5, Pallas kernels, call_kernel(): pl.pallas_call(guarded, grid_spec=pltpu.PrefetchScalarGridSpec(num_scalar...  84.5 us
    pallas_call x1, Pallas kernels, soap_factor(): pl.pallas_call(factor_kernel, grid_spec=pltpu.PrefetchScalarGridSpec(num_...  67.6 us
    ppermute x32, starting transfers between devices, trade(): return lax.ppermute(value, ('section', 'dp'), pairs)  63.4 us
    ppermute x4, waiting for transfers between devices, from_behind(): return lax.ppermute(shard, axis, pairs)  52.5 us
    pallas_call x1, Pallas kernels, soap_first(): pl.pallas_call(first_kernel, grid_spec=pltpu.PrefetchScalarGridSpec(num_s...  48.9 us
    convert_element_type x4, other arithmetic, pack(): return marked.astype(WIRE)  19.3 us
    pallas_call x1, Pallas kernels, soap_last(): pl.pallas_call(last_kernel, grid_spec=pltpu.PrefetchScalarGridSpec(num_sc...  16 us
  transfers between devices with their start and end apart: 38, of which 27 were waited for; matrix products, arithmetic and copies ran while one was open for 8% of the time, Pallas kernels for 16%

profile of v1, /device:TPU:4, one launch (start us, length us, event | category | flops | bytes accessed | tf_op | source)
XLA Modules:
  0.0 715.8 jit_solution(10370925249790676110)
XLA Ops:
  0.7 2.0 bitcast_convert_fusion.refs_0_
  2.7 1.6 collective-permute-start.6
  4.8 1.6 collective-permute-start.8
  7.1 2.2 multiply_sine_fusion.1
  9.4 1.4 multiply_sine_fusion.3
  11.2 2.1 fusion.50
  13.2 2.0 copy.38
  15.3 2.4 fusion.26
  17.7 2.3 fusion.25
  20.0 2.7 fusion.23
  22.7 1.6 fusion.21
  26.5 10.3 %collective-permute-done.6.refs_1_ = bf16[5,384,384]{2,1,0:T(8,128)(2,1)S(1)} collective-permute-done((bf16[5,384,384]{2,1,0:T(8,128)(2,1)S(1)}, bf16[5,384,384]{2,1,0:T(8,128)(2,1)S(1)}, u32[]{:S(2)}, u32[]{:S(2)}) %collective-permute-start.6) | collective-permute-done | bytes 1474592 | tf_op jit(solution)/shard_map/ppermute | solution.py:1087
  38.7 1.7 collective-permute-start.10
  41.7 2.0 pad.26.clone
  45.4 2.6 collective-permute-start.13
  48.0 23.3 %collective-permute-done.9.refs_5_ = bf16[5,384,384]{2,1,0:T(8,128)(2,1)} collective-permute-done((bf16[5,384,384]{2,1,0:T(8,128)(2,1)}, bf16[5,384,384]{2,1,0:T(8,128)(2,1)}, u32[]{:S(2)}, u32[]{:S(2)}) %collective-permute-start.9) | collective-permute-done | bytes 1474592 | tf_op jit(solution)/shard_map/ppermute | solution.py:1087
  74.7 1.4 collective-permute-start.12
  76.2 33.7 %collective-permute-done.13.refs_8_ = bf16[5,384,384]{2,1,0:T(8,128)(2,1)S(1)} collective-permute-done((bf16[5,384,384]{2,1,0:T(8,128)(2,1)S(1)}, bf16[5,384,384]{2,1,0:T(8,128)(2,1)S(1)}, u32[]{:S(2)}, u32[]{:S(2)}) %collective-permute-start.13) | collective-permute-done | bytes 1474592 | tf_op jit(solution)/shard_map/ppermute | solution.py:1087
  109.9 1.6 collective-permute-start.14
  112.7 30.4 %collective-permute-done.14.refs_9_ = bf16[5,384,384]{2,1,0:T(8,128)(2,1)S(1)} collective-permute-done((bf16[5,384,384]{2,1,0:T(8,128)(2,1)S(1)}, bf16[5,384,384]{2,1,0:T(8,128)(2,1)S(1)}, u32[]{:S(2)}, u32[]{:S(2)}) %collective-permute-start.14) | collective-permute-done | bytes 1474592 | tf_op jit(solution)/shard_map/ppermute | solution.py:1087
  146.6 30.1 %collective-permute-done.17.refs_13_ = bf16[5,384,384]{2,1,0:T(8,128)(2,1)} collective-permute-done((bf16[5,384,384]{2,1,0:T(8,128)(2,1)S(1)}, bf16[5,384,384]{2,1,0:T(8,128)(2,1)}, u32[]{:S(2)}, u32[]{:S(2)}) %collective-permute-start.17) | collective-permute-done | bytes 1474592 | tf_op jit(solution)/shard_map/ppermute | solution.py:1087
  179.5 1.4 collective-permute-start.20
  181.7 28.8 %collective-permute-done.19.refs_11_ = bf16[5,384,384]{2,1,0:T(8,128)(2,1)} collective-permute-done((bf16[5,384,384]{2,1,0:T(8,128)(2,1)}, bf16[5,384,384]{2,1,0:T(8,128)(2,1)}, u32[]{:S(2)}, u32[]{:S(2)}) %collective-permute-start.19) | collective-permute-done | bytes 1474592 | tf_op jit(solution)/shard_map/ppermute | solution.py:1087
  210.7 24.9 %encoder_forward.1 = (bf16[256,768]{1,0:T(8,128)(2,1)}, f32[256,768]{1,0:T(8,128)}, bf16[2,128,768]{2,1,0:T(8,128)(2,1)}, bf16[2,128,768]{2,1,0:T(8,128)(2,1)}, ...) custom-call(s32[138]{0:T(256)} %pad_add_fusion.places_ref, ...), custom_call_target="tpu_custom_call" | custom-call | bytes 75000000 | tf_op jit(solution)/shard_map/encoder_forward/pallas_call | solution.py:823
  239.9 8.2 %predictor_step.1 = (bf16[256,768]{1,0:T(8,128)(2,1)}, f32[4,400,384]{2,1,0:T(8,128)}, f32[4,400,384]{2,1,0:T(8,128)S(1)}, f32[4,400,384]{2,1,0:T(8,128)}, f32[4...) custom-call(s32[138]{0:T(256)} %pad_add_fusion.places_ref, ...), custom_call_target="tpu_custom_call" | custom-call | bytes 150000000 | tf_op jit(solution)/shard_map/predictor_step/pallas_call | solution.py:823
  249.3 51.6 %collective-permute-done.22.refs_16_ = bf16[256,768]{1,0:T(8,128)(2,1)S(1)} collective-permute-done((bf16[256,768]{1,0:T(8,128)(2,1)}, bf16[256,768]{1,0:T(8,128)(2,1)S(1)}, u32[]{:S(2)}, u32[]{:S(2)}) %collective-permute-start.22) | collective-permute-done | bytes 393248 | tf_op jit(solution)/shard_map/ppermute | solution.py:51
  301.8 23.5 %feed_backward.1 = (f32[4,784,384]{2,1,0:T(8,128)}, f32[4,784,384]{2,1,0:T(8,128)}, f32[4,784,384]{2,1,0:T(8,128)}, f32[4,784,384]{2,1,0:T(8,128)}, f32[256,768]...) custom-call(s32[138]{0:T(256)} %pad_add_fusion.places_ref, bf16[5,384,384]{2,1,0:T(8,128)(2,1)} %copy-done.1, ...), custom_call_target="tpu_custom_call" | custom-call | bytes 75000000 | tf_op jit(solution)/shard_map/feed_backward/pallas_call | solution.py:823
  327.3 8.1 %select_convert_fusion.6 = (f16[4,784,384]{2,1,0:T(8,128)(2,1)}, f16[4,784,384]{2,1,0:T(8,128)(2,1)}, f16[4,784,384]{2,1,0:T(8,128)(2,1)}) fusion(f32[4,784,384]{2,1,0:T(8,128)} %get-tuple-element.145, f32[]{:T(128)S(6)} %floor.18, f32[]{:T(128)S(6)} %exp2.213, pred[784]{0:T(1024)(128)(4,1)S(1)} %iota_compare_fusion.10, ...), kind=kLoop, calls=%fused_computation.21 | loop fusion | flops 10838016 | bytes 21676824 | tf_op jit(solution)/shard_map/convert_element_type | solution.py:1102
  335.4 3.3 collective-permute-start.23
  338.8 1.9 collective-permute-start.24
  340.7 4.0 collective-permute-start.25
  344.7 26.6 %attention_backward.1 = (f32[4,496,384]{2,1,0:T(8,128)}, f32[4,496,384]{2,1,0:T(8,128)}, f32[4,496,384]{2,1,0:T(8,128)}, f32[4,496,384]{2,1,0:T(8,128)}, f32[1,11520]{1,0:T(1,128)}, /*index=5*/f32[1,384]{1,0:T(1,128)}) custom-call(s32[138]{0:T(256)} %pad_add_fusion.places_ref, bf16[5,384,384]{2,1,0:T(8,128)(2,1)} %copy-done.1, ...), custom_call_target="tpu_custom_call" | custom-call | bytes 75000000 | tf_op jit(solution)/shard_map/attention_backward/pallas_call | solution.py:823
  373.4 6.6 select_convert_fusion.10
  380.0 16.2 %collective-permute-done.24 = f16[4,784,384]{2,1,0:T(8,128)(2,1)} collective-permute-done((f16[4,784,384]{2,1,0:T(8,128)(2,1)}, f16[4,784,384]{2,1,0:T(8,128)(2,1)}, u32[]{:S(2)}, u32[]{:S(2)}) %collective-permute-start.24) | collective-permute-done | bytes 2408480 | tf_op jit(solution)/shard_map/ppermute | solution.py:1087
  396.1 2.8 collective-permute-start.28
  398.9 3.1 collective-permute-start.27
  402.0 3.3 collective-permute-start.26
  411.0 7.8 %multiply_add_fusion.1 = f32[4,784,384]{2,1,0:T(8,128)} fusion(f16[4,784,384]{2,1,0:T(8,128)(2,1)} %collective-permute-done.25, f16[4,784,384]{2,1,0:T(8,128)(2,1)} %collective-permute-done.24, f32[4,784,384]{2,1,0:T(8,128)} %get-tuple-element.164, f16[4,784,384]{2,1,0:T(8,128)(2,1)S(1)} %collective-permute-done.23, f32[]{:T(128)} %bitcast.27, f32[]{:T(128)} %bitcast.26, ...), kind=kLoop, calls=%fused_computation.20 | loop fusion | flops 10838016 | bytes 16859148 | tf_op jit(solution)/shard_map/add | solution.py:1135
  421.1 14.3 %collective-permute-done.27 = f16[4,496,384]{2,1,0:T(8,128)(2,1)} collective-permute-done((f16[4,496,384]{2,1,0:T(8,128)(2,1)}, f16[4,496,384]{2,1,0:T(8,128)(2,1)}, u32[]{:S(2)}, u32[]{:S(2)}) %collective-permute-start.27) | collective-permute-done | bytes 1523744 | tf_op jit(solution)/shard_map/ppermute | solution.py:1087
  440.0 4.2 fusion.4
  444.5 2.8 fusion.12
  447.3 8.9 %collective-permute-start.31 = (f16[1,1264,384]{2,1,0:T(8,128)(2,1)}, f16[1,1264,384]{2,1,0:T(8,128)(2,1)}, u32[]{:S(2)}, u32[]{:S(2)}) collective-permute-start(f16[1,1264,384]{2,1,0:T(8,128)(2,1)} %get-tuple-element.196), channel_id=1, source_target_pairs={{0,12},{1,13},{2,14},{3,15},{4,8},{5,9},{6,10},{7,11},{8,4},{9,5},... | collective-permute-start | bytes 2912264 | tf_op jit(solution)/shard_map/ppermute | solution.py:1087
  456.3 1.9 collective-permute-start.30
  458.2 2.9 collective-permute-start.29
  461.1 15.2 %collective-permute-done.31 = f16[1,1264,384]{2,1,0:T(8,128)(2,1)} collective-permute-done((f16[1,1264,384]{2,1,0:T(8,128)(2,1)}, f16[1,1264,384]{2,1,0:T(8,128)(2,1)}, u32[]{:S(2)}, u32[]{:S(2)}) %collective-permute-start.31) | collective-permute-done | bytes 970784 | tf_op jit(solution)/shard_map/ppermute | solution.py:1087
  478.2 40.0 %collective-permute-done.30 = f16[1,1264,384]{2,1,0:T(8,128)(2,1)} collective-permute-done((f16[1,1264,384]{2,1,0:T(8,128)(2,1)}, f16[1,1264,384]{2,1,0:T(8,128)(2,1)}, u32[]{:S(2)}, u32[]{:S(2)}) %collective-permute-start.30) | collective-permute-done | bytes 970784 | tf_op jit(solution)/shard_map/ppermute | solution.py:1087
  522.1 3.5 multiply_reduce_fusion
  525.6 1.5 place_shares.1
  527.1 1.8 select_convert_fusion.9
  528.9 5.8 all-to-all-start
  538.4 1.5 collective-permute-start.36
  540.6 1.9 collective-permute-done.36
  544.0 2.0 collective-permute-start.32
  546.7 2.4 collective-permute-start.38
  551.2 5.1 collective-permute-start.39
  556.5 2.4 collective-permute-done.39
  559.9 1.5 collective-permute-start.35
  562.0 2.3 collective-permute-done.35
  569.7 1.8 copy.42
  571.5 48.9 %soap_first.1 = (f32[5,384,384]{2,1,0:T(8,128)}, f32[5,384,384]{2,1,0:T(8,128)}, f32[5,384,384]{2,1,0:T(8,128)}, f32[5,384,384]{2,1,0:T(8,128)}, f32[5,384,384]{...) custom-call(s32[5]{0:T(128)} %get-tuple-element.215.flag, f32[1]{0:T(128)} %bitcast.38.factor, ...), custom_call_target="tpu_custom_call" | custom-call | tf_op jit(solution)/shard_map/soap_first/pallas_call | solution.py:964
  620.4 3.2 convert_element_type.320
  628.5 67.6 %soap_factor.1.q_ref = f32[5,2,384,384]{3,2,1,0:T(8,128)} custom-call(s32[5]{0:T(128)} %get-tuple-element.215.flag, f32[5,2,384,384]{3,2,1,0:T(8,128)} %get-tuple-element.176.base_ref, f32[5,2,384,384]{3,2,1,0:T(8,128)} %get-tuple-element.177.gram_ref), custom_call_target="tpu_custom_call" | custom-call | tf_op jit(solution)/shard_map/soap_factor/pallas_call | solution.py:978
  696.2 16.0 %soap_last.1 = (f32[5,384,384]{2,1,0:T(8,128)}, f32[5,384,384]{2,1,0:T(8,128)}, f32[5,384,384]{2,1,0:T(8,128)}) custom-call(s32[5]{0:T(128)} %get-tuple-element.215.flag, f32[5,384,384]{2,1,0:T(8,128)} %bitcast.83, f32[5,384,384]{2,1,0:T(8,128)} %bitcast.85, f32[5,384,384]{2,1,0:T(8,128)} %get-tuple-element.175.m_ref, f32[5,2,384,384]{3,2,1,0:T(8,128)} %soap_factor.1.q_ref), custom_call_target="tpu_custom_call" | custom-call | tf_op jit(solution)/shard_map/soap_last/pallas_call | solution.py:1001
  712.2 2.2 select_bitcast_fusion
  (175 shorter events, 55.7 us)
Async XLA Ops:
  0.6 5.8 copy-start.29
  0.7 10.2 %copy-start.25 = (s32[2,4]{1,0:T(2,128)S(1)}, s32[2,4]{1,0:T(2,128)}, u32[]{:S(2)}) copy-start(s32[2,4]{1,0:T(2,128)} %param.22) | copy-start | bytes 100
  2.7 42.7 %copy-start.1 = (bf16[5,384,384]{2,1,0:T(8,128)(2,1)}, bf16[5,384,384]{2,1,0:T(8,128)(2,1)S(1)}, u32[]{:S(2)}) copy-start(bf16[5,384,384]{2,1,0:T(8,128)(2,1)S(1)} %bitcast_convert_fusion.refs_0_) | copy-start | bytes 4423684
  2.7 12.5 %copy-start.27 = (s32[2,4,36]{2,1,0:T(4,128)S(1)}, s32[2,4,36]{2,1,0:T(4,128)}, u32[]{:S(2)}) copy-start(s32[2,4,36]{2,1,0:T(4,128)} %param.21) | copy-start | bytes 3460
  2.7 12.6 %copy-start.26 = (s32[2,128]{1,0:T(2,128)S(1)}, s32[2,128]{1,0:T(2,128)}, u32[]{:S(2)}) copy-start(s32[2,128]{1,0:T(2,128)} %param.19) | copy-start | bytes 3076
  2.7 34.1 %collective-permute-start.6 = (bf16[5,384,384]{2,1,0:T(8,128)(2,1)S(1)}, bf16[5,384,384]{2,1,0:T(8,128)(2,1)S(1)}, u32[]{:S(2)}, u32[]{:S(2)}) collective-permute-start(bf16[5,384,384]{2,1,0:T(8,128)(2,1)S(1)} %bitcast_convert_fusion.refs_0_), channel_id=1, source_target_pairs={{0,1},{1,0},{2,3},{3,2},{4,5},{5,4},{6,7},{7,6},{8,9},{9,8},{10,11... | collective-permute-start | bytes 4423688 | tf_op jit(solution)/shard_map/ppermute | solution.py:1087
  4.3 33.9 %collective-permute-start.7 = (bf16[5,384,384]{2,1,0:T(8,128)(2,1)S(1)}, bf16[5,384,384]{2,1,0:T(8,128)(2,1)}, u32[]{:S(2)}, u32[]{:S(2)}) collective-permute-start(bf16[5,384,384]{2,1,0:T(8,128)(2,1)S(1)} %bitcast_convert_fusion.refs_0_), channel_id=1, source_target_pairs={{0,2},{1,3},{2,0},{3,1},{4,6},{5,7},{6,4},{7,5},{8,10},{9,11},{10,... | collective-permute-start | bytes 4423688 | tf_op jit(solution)/shard_map/ppermute | solution.py:1087
  4.8 33.6 %collective-permute-start.8 = (bf16[5,384,384]{2,1,0:T(8,128)(2,1)S(1)}, bf16[5,384,384]{2,1,0:T(8,128)(2,1)}, u32[]{:S(2)}, u32[]{:S(2)}) collective-permute-start(bf16[5,384,384]{2,1,0:T(8,128)(2,1)S(1)} %bitcast_convert_fusion.refs_0_), channel_id=1, source_target_pairs={{0,4},{1,5},{2,6},{3,7},{4,0},{5,1},{6,2},{7,3},{8,12},{9,13},{10,... | collective-permute-start | bytes 4423688 | tf_op jit(solution)/shard_map/ppermute | solution.py:1087
  15.3 7.4 %copy-start.12 = (f32[196,192]{1,0:T(8,128)S(1)}, f32[196,192]{1,0:T(8,128)}, u32[]{:S(2)}) copy-start(f32[196,192]{1,0:T(8,128)} %get-tuple-element.212) | copy-start | bytes 451588
  15.3 7.4 %copy-start.13 = (f32[196,192]{1,0:T(8,128)S(1)}, f32[196,192]{1,0:T(8,128)}, u32[]{:S(2)}) copy-start(f32[196,192]{1,0:T(8,128)} %get-tuple-element.213) | copy-start | bytes 451588
  15.3 9.1 %copy-start.14 = (bf16[2,196,768]{2,0,1:T(2,128)(2,1)S(1)}, bf16[2,196,768]{2,0,1:T(2,128)(2,1)}, u32[]{:S(2)}) copy-start(bf16[2,196,768]{2,0,1:T(2,128)(2,1)} %param.18) | copy-start | bytes 1806340
  20.0 21.1 %copy-start.17 = (f32[1,18432]{1,0:T(1,128)S(1)}, f32[1,18432]{1,0:T(1,128)}, u32[]{:S(2)}) copy-start(f32[1,18432]{1,0:T(1,128)} %param.31) | copy-start | bytes 221188
  26.5 154.5 %copy-start = (s32[68]{0:T(128)S(1)}, s32[68]{0:T(128)}, u32[]{:S(2)}) copy-start(s32[68]{0:T(128)} %slots_ref.1) | copy-start | bytes 820
  36.8 173.9 %copy-start.3 = (bf16[5,384,384]{2,1,0:T(8,128)(2,1)}, bf16[5,384,384]{2,1,0:T(8,128)(2,1)S(1)}, u32[]{:S(2)}) copy-start(bf16[5,384,384]{2,1,0:T(8,128)(2,1)S(1)} %collective-permute-done.6.refs_1_) | copy-start | bytes 4423684
  38.3 32.9 %collective-permute-start.9 = (bf16[5,384,384]{2,1,0:T(8,128)(2,1)}, bf16[5,384,384]{2,1,0:T(8,128)(2,1)}, u32[]{:S(2)}, u32[]{:S(2)}) collective-permute-start(bf16[5,384,384]{2,1,0:T(8,128)(2,1)} %collective-permute-done.8.refs_4_), channel_id=1, source_target_pairs={{0,1},{1,0},{2,3},{3,2},{4,5},{5,4},{6,7},{7,6},{8,9},{9,8},{10,11... | collective-permute-start | bytes 4423688 | tf_op jit(solution)/shard_map/ppermute | solution.py:1087
  38.7 33.0 %collective-permute-start.10 = (bf16[5,384,384]{2,1,0:T(8,128)(2,1)}, bf16[5,384,384]{2,1,0:T(8,128)(2,1)}, u32[]{:S(2)}, u32[]{:S(2)}) collective-permute-start(bf16[5,384,384]{2,1,0:T(8,128)(2,1)} %collective-permute-done.8.refs_4_), channel_id=1, source_target_pairs={{0,2},{1,3},{2,0},{3,1},{4,6},{5,7},{6,4},{7,5},{8,10},{9,11},{10,... | collective-permute-start | bytes 4423688 | tf_op jit(solution)/shard_map/ppermute | solution.py:1087
  45.4 64.5 %collective-permute-start.13 = (bf16[5,384,384]{2,1,0:T(8,128)(2,1)S(1)}, bf16[5,384,384]{2,1,0:T(8,128)(2,1)S(1)}, u32[]{:S(2)}, u32[]{:S(2)}) collective-permute-start(bf16[5,384,384]{2,1,0:T(8,128)(2,1)S(1)} %bitcast_convert_fusion.refs_0_), channel_id=1, source_target_pairs={{0,8},{1,9},{2,10},{3,11},{4,12},{5,13},{6,14},{7,15},{8,0},{9,1},... | collective-permute-start | bytes 4423688 | tf_op jit(solution)/shard_map/ppermute | solution.py:1087
  73.4 36.5 %collective-permute-start.11 = (bf16[5,384,384]{2,1,0:T(8,128)(2,1)}, bf16[5,384,384]{2,1,0:T(8,128)(2,1)S(1)}, u32[]{:S(2)}, u32[]{:S(2)}) collective-permute-start(bf16[5,384,384]{2,1,0:T(8,128)(2,1)} %collective-permute-done.7.refs_2_), channel_id=1, source_target_pairs={{0,1},{1,0},{2,3},{3,2},{4,5},{5,4},{6,7},{7,6},{8,9},{9,8},{10,11... | collective-permute-start | bytes 4423688 | tf_op jit(solution)/shard_map/ppermute | solution.py:1087
  74.7 35.2 %collective-permute-start.12 = (bf16[5,384,384]{2,1,0:T(8,128)(2,1)}, bf16[5,384,384]{2,1,0:T(8,128)(2,1)S(1)}, u32[]{:S(2)}, u32[]{:S(2)}) collective-permute-start(bf16[5,384,384]{2,1,0:T(8,128)(2,1)} %collective-permute-done.9.refs_5_), channel_id=1, source_target_pairs={{0,2},{1,3},{2,0},{3,1},{4,6},{5,7},{6,4},{7,5},{8,10},{9,11},{10,... | collective-permute-start | bytes 4423688 | tf_op jit(solution)/shard_map/ppermute | solution.py:1087
  109.9 2.2 copy-start.4
  109.9 34.7 %copy-start.5 = (bf16[5,384,384]{2,1,0:T(8,128)(2,1)}, bf16[5,384,384]{2,1,0:T(8,128)(2,1)S(1)}, u32[]{:S(2)}) copy-start(bf16[5,384,384]{2,1,0:T(8,128)(2,1)S(1)} %collective-permute-done.11.refs_3_) | copy-start | bytes 4423684
  109.9 35.7 %copy-start.6 = (bf16[5,384,384]{2,1,0:T(8,128)(2,1)}, bf16[5,384,384]{2,1,0:T(8,128)(2,1)S(1)}, u32[]{:S(2)}) copy-start(bf16[5,384,384]{2,1,0:T(8,128)(2,1)S(1)} %collective-permute-done.12.refs_7_) | copy-start | bytes 4423684
  109.9 33.2 %collective-permute-start.14 = (bf16[5,384,384]{2,1,0:T(8,128)(2,1)S(1)}, bf16[5,384,384]{2,1,0:T(8,128)(2,1)S(1)}, u32[]{:S(2)}, u32[]{:S(2)}) collective-permute-start(bf16[5,384,384]{2,1,0:T(8,128)(2,1)S(1)} %collective-permute-done.13.refs_8_), channel_id=1, source_target_pairs={{0,1},{1,0},{2,3},{3,2},{4,5},{5,4},{6,7},{7,6},{8,9},{9,8},{10,11... | collective-permute-start | bytes 4423688 | tf_op jit(solution)/shard_map/ppermute | solution.py:1087
  111.5 33.0 %collective-permute-start.15 = (bf16[5,384,384]{2,1,0:T(8,128)(2,1)S(1)}, bf16[5,384,384]{2,1,0:T(8,128)(2,1)}, u32[]{:S(2)}, u32[]{:S(2)}) collective-permute-start(bf16[5,384,384]{2,1,0:T(8,128)(2,1)S(1)} %collective-permute-done.13.refs_8_), channel_id=1, source_target_pairs={{0,2},{1,3},{2,0},{3,1},{4,6},{5,7},{6,4},{7,5},{8,10},{9,11},{10,... | collective-permute-start | bytes 4423688 | tf_op jit(solution)/shard_map/ppermute | solution.py:1087
  112.1 32.6 %collective-permute-start.16 = (bf16[5,384,384]{2,1,0:T(8,128)(2,1)S(1)}, bf16[5,384,384]{2,1,0:T(8,128)(2,1)S(1)}, u32[]{:S(2)}, u32[]{:S(2)}) collective-permute-start(bf16[5,384,384]{2,1,0:T(8,128)(2,1)S(1)} %collective-permute-done.13.refs_8_), channel_id=1, source_target_pairs={{0,4},{1,5},{2,6},{3,7},{4,0},{5,1},{6,2},{7,3},{8,12},{9,13},{10,... | collective-permute-start | bytes 4423688 | tf_op jit(solution)/shard_map/ppermute | solution.py:1087
  143.1 67.6 %copy-start.7 = (bf16[5,384,384]{2,1,0:T(8,128)(2,1)}, bf16[5,384,384]{2,1,0:T(8,128)(2,1)S(1)}, u32[]{:S(2)}) copy-start(bf16[5,384,384]{2,1,0:T(8,128)(2,1)S(1)} %collective-permute-done.14.refs_9_) | copy-start | bytes 4423684
  144.6 2.0 copy-start.8
  144.6 32.1 %collective-permute-start.17 = (bf16[5,384,384]{2,1,0:T(8,128)(2,1)S(1)}, bf16[5,384,384]{2,1,0:T(8,128)(2,1)}, u32[]{:S(2)}, u32[]{:S(2)}) collective-permute-start(bf16[5,384,384]{2,1,0:T(8,128)(2,1)S(1)} %collective-permute-done.16.refs_12_), channel_id=1, source_target_pairs={{0,1},{1,0},{2,3},{3,2},{4,5},{5,4},{6,7},{7,6},{8,9},{9,8},{10,11... | collective-permute-start | bytes 4423688 | tf_op jit(solution)/shard_map/ppermute | solution.py:1087
  145.6 32.1 %collective-permute-start.18 = (bf16[5,384,384]{2,1,0:T(8,128)(2,1)S(1)}, bf16[5,384,384]{2,1,0:T(8,128)(2,1)S(1)}, u32[]{:S(2)}, u32[]{:S(2)}) collective-permute-start(bf16[5,384,384]{2,1,0:T(8,128)(2,1)S(1)} %collective-permute-done.16.refs_12_), channel_id=1, source_target_pairs={{0,2},{1,3},{2,0},{3,1},{4,6},{5,7},{6,4},{7,5},{8,10},{9,11},{10,... | collective-permute-start | bytes 4423688 | tf_op jit(solution)/shard_map/ppermute | solution.py:1087
  177.7 1.1 copy-start.9
  178.8 31.6 %collective-permute-start.19 = (bf16[5,384,384]{2,1,0:T(8,128)(2,1)}, bf16[5,384,384]{2,1,0:T(8,128)(2,1)}, u32[]{:S(2)}, u32[]{:S(2)}) collective-permute-start(bf16[5,384,384]{2,1,0:T(8,128)(2,1)} %collective-permute-done.15.refs_10_), channel_id=1, source_target_pairs={{0,1},{1,0},{2,3},{3,2},{4,5},{5,4},{6,7},{7,6},{8,9},{9,8},{10,11... | collective-permute-start | bytes 4423688 | tf_op jit(solution)/shard_map/ppermute | solution.py:1087
  179.5 31.2 %collective-permute-start.20 = (bf16[5,384,384]{2,1,0:T(8,128)(2,1)}, bf16[5,384,384]{2,1,0:T(8,128)(2,1)}, u32[]{:S(2)}, u32[]{:S(2)}) collective-permute-start(bf16[5,384,384]{2,1,0:T(8,128)(2,1)} %collective-permute-done.17.refs_13_), channel_id=1, source_target_pairs={{0,2},{1,3},{2,0},{3,1},{4,6},{5,7},{6,4},{7,5},{8,10},{9,11},{10,... | collective-permute-start | bytes 4423688 | tf_op jit(solution)/shard_map/ppermute | solution.py:1087
  235.6 3.5 collective-permute-start.21
  248.0 52.9 %collective-permute-start.22 = (bf16[256,768]{1,0:T(8,128)(2,1)}, bf16[256,768]{1,0:T(8,128)(2,1)S(1)}, u32[]{:S(2)}, u32[]{:S(2)}) collective-permute-start(bf16[256,768]{1,0:T(8,128)(2,1)} %get-tuple-element.129), channel_id=1, source_target_pairs={{16,0},{17,1},{18,2},{19,3},{20,4},{21,5},{22,6},{23,7},{24,8},{25... | collective-permute-start | bytes 1179656 | tf_op jit(solution)/shard_map/ppermute | solution.py:51
  335.4 44.5 %collective-permute-start.23 = (f16[4,784,384]{2,1,0:T(8,128)(2,1)}, f16[4,784,384]{2,1,0:T(8,128)(2,1)S(1)}, u32[]{:S(2)}, u32[]{:S(2)}) collective-permute-start(f16[4,784,384]{2,1,0:T(8,128)(2,1)} %get-tuple-element.154), channel_id=1, source_target_pairs={{0,1},{1,0},{2,3},{3,2},{4,5},{5,4},{6,7},{7,6},{8,9},{9,8},{10,11... | collective-permute-start | bytes 7225352 | tf_op jit(solution)/shard_map/ppermute | solution.py:1087
  338.8 57.4 %collective-permute-start.24 = (f16[4,784,384]{2,1,0:T(8,128)(2,1)}, f16[4,784,384]{2,1,0:T(8,128)(2,1)}, u32[]{:S(2)}, u32[]{:S(2)}) collective-permute-start(f16[4,784,384]{2,1,0:T(8,128)(2,1)} %get-tuple-element.155), channel_id=1, source_target_pairs={{0,2},{1,3},{2,0},{3,1},{4,6},{5,7},{6,4},{7,5},{8,10},{9,11},{10,... | collective-permute-start | bytes 7225352 | tf_op jit(solution)/shard_map/ppermute | solution.py:1087
  340.7 55.5 %collective-permute-start.25 = (f16[4,784,384]{2,1,0:T(8,128)(2,1)}, f16[4,784,384]{2,1,0:T(8,128)(2,1)}, u32[]{:S(2)}, u32[]{:S(2)}) collective-permute-start(f16[4,784,384]{2,1,0:T(8,128)(2,1)} %get-tuple-element.156), channel_id=1, source_target_pairs={{0,3},{1,2},{2,1},{3,0},{4,7},{5,6},{6,5},{7,4},{8,11},{9,10},{10,... | collective-permute-start | bytes 7225352 | tf_op jit(solution)/shard_map/ppermute | solution.py:1087
  396.1 23.1 %collective-permute-start.28 = (f16[4,496,384]{2,1,0:T(8,128)(2,1)}, f16[4,496,384]{2,1,0:T(8,128)(2,1)}, u32[]{:S(2)}, u32[]{:S(2)}) collective-permute-start(f16[4,496,384]{2,1,0:T(8,128)(2,1)} %get-tuple-element.163), channel_id=1, source_target_pairs={{0,3},{1,2},{2,1},{3,0},{4,7},{5,6},{6,5},{7,4},{8,11},{9,10},{10,... | collective-permute-start | bytes 4571144 | tf_op jit(solution)/shard_map/ppermute | solution.py:1087
  398.9 36.5 %collective-permute-start.27 = (f16[4,496,384]{2,1,0:T(8,128)(2,1)}, f16[4,496,384]{2,1,0:T(8,128)(2,1)}, u32[]{:S(2)}, u32[]{:S(2)}) collective-permute-start(f16[4,496,384]{2,1,0:T(8,128)(2,1)} %get-tuple-element.162), channel_id=1, source_target_pairs={{0,2},{1,3},{2,0},{3,1},{4,6},{5,7},{6,4},{7,5},{8,10},{9,11},{10,... | collective-permute-start | bytes 4571144 | tf_op jit(solution)/shard_map/ppermute | solution.py:1087
  402.0 35.3 %collective-permute-start.26 = (f16[4,496,384]{2,1,0:T(8,128)(2,1)}, f16[4,496,384]{2,1,0:T(8,128)(2,1)}, u32[]{:S(2)}, u32[]{:S(2)}) collective-permute-start(f16[4,496,384]{2,1,0:T(8,128)(2,1)} %get-tuple-element.161), channel_id=1, source_target_pairs={{0,1},{1,0},{2,3},{3,2},{4,5},{5,4},{6,7},{7,6},{8,9},{9,8},{10,11... | collective-permute-start | bytes 4571144 | tf_op jit(solution)/shard_map/ppermute | solution.py:1087
  440.0 4.5 copy-start.2
  447.3 29.0 %collective-permute-start.31 = (f16[1,1264,384]{2,1,0:T(8,128)(2,1)}, f16[1,1264,384]{2,1,0:T(8,128)(2,1)}, u32[]{:S(2)}, u32[]{:S(2)}) collective-permute-start(f16[1,1264,384]{2,1,0:T(8,128)(2,1)} %get-tuple-element.196), channel_id=1, source_target_pairs={{0,12},{1,13},{2,14},{3,15},{4,8},{5,9},{6,10},{7,11},{8,4},{9,5},... | collective-permute-start | bytes 2912264 | tf_op jit(solution)/shard_map/ppermute | solution.py:1087
  456.3 61.9 %collective-permute-start.30 = (f16[1,1264,384]{2,1,0:T(8,128)(2,1)}, f16[1,1264,384]{2,1,0:T(8,128)(2,1)}, u32[]{:S(2)}, u32[]{:S(2)}) collective-permute-start(f16[1,1264,384]{2,1,0:T(8,128)(2,1)} %get-tuple-element.195), channel_id=1, source_target_pairs={{0,8},{1,9},{2,10},{3,11},{4,12},{5,13},{6,14},{7,15},{8,0},{9,1},... | collective-permute-start | bytes 2912264 | tf_op jit(solution)/shard_map/ppermute | solution.py:1087
  458.2 61.8 %collective-permute-start.29 = (f16[1,1264,384]{2,1,0:T(8,128)(2,1)}, f16[1,1264,384]{2,1,0:T(8,128)(2,1)}, u32[]{:S(2)}, u32[]{:S(2)}) collective-permute-start(f16[1,1264,384]{2,1,0:T(8,128)(2,1)} %get-tuple-element.194), channel_id=1, source_target_pairs={{0,4},{1,5},{2,6},{3,7},{4,0},{5,1},{6,2},{7,3},{8,12},{9,13},{10,... | collective-permute-start | bytes 2912264 | tf_op jit(solution)/shard_map/ppermute | solution.py:1087
  528.9 7.1 copy-start.28
  528.9 8.4 %copy-start.23 = (f32[1,6912]{1,0:T(1,128)S(1)}, f32[1,6912]{1,0:T(1,128)}, u32[]{:S(2)}) copy-start(f32[1,6912]{1,0:T(1,128)} %get-tuple-element.171) | copy-start | bytes 82948
  528.9 8.6 %copy-start.24 = (f32[1,11520]{1,0:T(1,128)S(1)}, f32[1,11520]{1,0:T(1,128)}, u32[]{:S(2)}) copy-start(f32[1,11520]{1,0:T(1,128)} %get-tuple-element.170) | copy-start | bytes 138244
  528.9 40.1 %all-to-all-start = ((f16[16,136,384]{2,1,0:T(8,128)(2,1)}), f16[16,136,384]{2,1,0:T(8,128)(2,1)S(1)}, u32[]{:S(2)}, u32[]{:S(2)}) async-start(f16[16,136,384]{2,1,0:T(8,128)(2,1)} %select_convert_fusion.9), calls=%async_computation | async-start | bytes 3342336 | tf_op jit(solution)/shard_map/all_to_all | solution.py:1307
  538.4 4.2 collective-permute-start.36
  542.5 4.2 collective-permute-start.37
  544.0 5.1 collective-permute-start.32
  546.7 4.5 collective-permute-start.38
  549.1 7.2 %collective-permute-start.33 = (f32[128]{0:T(128)S(1)}, f32[128]{0:T(128)S(1)}, u32[]{:S(2)}, u32[]{:S(2)}) collective-permute-start(f32[128]{0:T(128)S(1)} %broadcast_add_fusion), channel_id=1, source_target_pairs={{0,2},{1,3},{2,0},{3,1},{4,6},{5,7},{6,4},{7,5},{8,10},{9,11},{10,... | collective-permute-start | bytes 1544 | tf_op jit(solution)/shard_map/ppermute | solution.py:1087
  551.2 7.8 %collective-permute-start.39 = (f32[11648]{0:T(1024)S(1)}, f32[11648]{0:T(1024)S(1)}, u32[]{:S(2)}, u32[]{:S(2)}) collective-permute-start(f32[11648]{0:T(1024)S(1)} %add.252), channel_id=1, source_target_pairs={{0,8},{1,9},{2,10},{3,11},{4,12},{5,13},{6,14},{7,15},{8,0},{9,1},... | collective-permute-start | bytes 139784 | tf_op jit(solution)/shard_map/ppermute | solution.py:1087
  556.3 3.5 collective-permute-start.34
  559.9 4.4 collective-permute-start.35
  565.1 1.1 collective-permute-start.40
  620.4 4.6 copy-start.18
  620.4 4.6 copy-start.21
  620.4 4.6 copy-start.22
  623.6 88.6 %collective-permute-start.41 = (bf16[5,384,384]{2,1,0:T(8,128)(2,1)}, bf16[5,384,384]{2,1,0:T(8,128)(2,1)S(1)}, u32[]{:S(2)}, u32[]{:S(2)}) collective-permute-start(bf16[5,384,384]{2,1,0:T(8,128)(2,1)} %convert_element_type.320), channel_id=1, source_target_pairs={{0,16},{1,17},{2,18},{3,19},{4,20},{5,21},{6,22},{7,23},{8,24},{9,... | collective-permute-start | bytes 4423688 | tf_op jit(solution)/shard_map/ppermute | solution.py:51
  625.7 2.1 collective-permute-start.42
  696.2 16.1 %copy-start.10 = (f32[1,5,384,384]{3,2,1,0:T(8,128)S(1)}, f32[1,5,384,384]{3,2,1,0:T(8,128)}, u32[]{:S(2)}) copy-start(f32[1,5,384,384]{3,2,1,0:T(8,128)} %param.24) | copy-start | bytes 8847364
  696.2 16.1 %copy-start.11 = (f32[5,384,384]{2,1,0:T(8,128)S(1)}, f32[5,384,384]{2,1,0:T(8,128)}, u32[]{:S(2)}) copy-start(f32[5,384,384]{2,1,0:T(8,128)} %get-tuple-element.174) | copy-start | bytes 8847364
  (2 other events, 1.5 us)

commit v2 on v1

--- a/solution.py
+++ b/solution.py
@@ -160,12 +160,16 @@
         for index, (stat, target, basis, form) in enumerate(
             ((e_ref, e_out, left, "nt"), (f_ref, f_out, right, "tn"))
         ):
-            fresh = BETA_STATS * stat[0] + (1.0 - BETA_STATS) * mul6(grad, grad, form)
+            fresh = BETA_STATS * stat[0] + (1.0 - BETA_STATS) * mul3(grad, grad, form)
             target[0] = fresh
             moved = mul6(parts_of(fresh, 3), basis)
             base_out[0, index] = moved
             pieces = parts_of(moved, 3)
-            gram_out[0, index] = mul6(pieces, pieces, "tn")
+            edge = moved.shape[-1]
+            for start in range(0, edge, 128):
+                rows = [piece[:, start : start + 128] for piece in pieces]
+                upper = [piece[:, start:] for piece in pieces]
+                gram_out[0, index, start : start + 128, start:] = mul6(rows, upper, "tn")
 
 def factor_kernel(flag, base_ref, gram_ref, q_out, base, gram, inverse):
     blocks, edge = base_ref.shape[0], base_ref.shape[-1]
@@ -183,14 +187,19 @@
         def block(b, carry):
             @pl.when(flag[b] != 0)
             def run():
-                for side in range(2):
-                    inv = parts_of(inverse[b, side], 3)
-                    q = mul6(parts_of(base[b, side, :, spot], 3), inv, "nt")
-                    q_out[b, side, :, spot] = q
-                    if k + 1 < count:
-                        p = parts_of(mul6(inv, parts_of(gram[b, side, spot, rest], 3)), 3)
-                        gram[b, side, rest, rest] = gram[b, side, rest, rest] - mul6(p, p, "tn")
-                        base[b, side, :, rest] = base[b, side, :, rest] - mul6(parts_of(q, 3), p)
+                sides = range(2)
+                inv = [parts_of(inverse[b, side], 3) for side in sides]
+                q = [mul6(parts_of(base[b, side, :, spot], 3), inv[side], "nt") for side in sides]
+                for side in sides:
+                    q_out[b, side, :, spot] = q[side]
+                if k + 1 < count:
+                    tops = [mul6(inv[side], parts_of(gram[b, side, spot, rest], 3)) for side in sides]
+                    p = [parts_of(top, 3) for top in tops]
+                    minus = [mul6(p[side], p[side], "tn") for side in sides]
+                    moved = [mul6(parts_of(q[side], 3), p[side]) for side in sides]
+                    for side in sides:
+                        gram[b, side, rest, rest] = gram[b, side, rest, rest] - minus[side]
+                        base[b, side, :, rest] = base[b, side, :, rest] - moved[side]
             return carry
 
         lax.fori_loop(0, blocks, block, 0)
@@ -375,25 +384,38 @@
     return raised * (1.0 / jnp.sum(raised, -1, keepdims=True))
 
 
+def head_jobs(q_ref, k_ref, v_ref, p, span, factors):
+    jobs = []
+    for g in range(span):
+        lanes = pl.ds(pl.multiple_of(128 * (span * p + g), 128), 128)
+        for i in range(q_ref.shape[0]):
+            q, k, v = q_ref[i, :, lanes], k_ref[i, :, lanes], v_ref[i, :, lanes]
+            for h in range(len(factors)):
+                jobs.append((i, lanes, h, q, k, v))
+    return jobs
+
+
 def attend(q_ref, k_ref, v_ref, valid_ref, out_ref, heads):
     images, rows, width = q_ref.shape
     keys = k_ref.shape[1]
     masks = head_masks(rows, heads, width)
     factors = as_factors(masks)
+    span = 1 if width // 128 % 2 else 2
 
     def group(p, carry):
-        lanes = pl.ds(pl.multiple_of(128 * p, 128), 128)
-        for i in range(images):
-            q, k, v = q_ref[i, :, lanes], k_ref[i, :, lanes], v_ref[i, :, lanes]
-            allowed = jnp.broadcast_to(valid_ref[i], (rows, keys)) > 0.0
-            result = jnp.zeros((rows, 128), f32)
-            for mask, factor in zip(masks, factors):
-                probs = soft(mm(q * factor, k, RIGHT_T), allowed)
-                result = jnp.where(mask, mm(probs.astype(bf), v), result)
-            out_ref[i, :, lanes] = result.astype(bf)
+        allowed = [jnp.broadcast_to(valid_ref[i], (rows, keys)) > 0.0 for i in range(images)]
+        jobs = head_jobs(q_ref, k_ref, v_ref, p, span, factors)
+        scores = [mm(q * factors[h], k, RIGHT_T) for _, _, h, q, k, _ in jobs]
+        probs = [soft(s, allowed[job[0]]).astype(bf) for s, job in zip(scores, jobs)]
+        parts = [mm(probs[n], job[5]) for n, job in enumerate(jobs)]
+        for n in range(0, len(jobs), len(masks)):
+            result = parts[n]
+            for h in range(1, len(masks)):
+                result = jnp.where(masks[h], parts[n + h], result)
+            out_ref[jobs[n][0], :, jobs[n][1]] = result.astype(bf)
         return carry
 
-    lax.fori_loop(0, width // 128, group, 0)
+    lax.fori_loop(0, width // 128 // span, group, 0)
 
 
 def attend_back(q_ref, k_ref, v_ref, valid_ref, go_ref, dq_ref, dk_ref, dv_ref, heads):
@@ -403,30 +425,34 @@
     key_masks = head_masks(keys, heads, width)
     factors = as_factors(masks)
     scale = 1.0 / math.sqrt(width // heads)
+    span = 1 if width // 128 % 2 else 2
 
     def group(p, carry):
-        lanes = pl.ds(pl.multiple_of(128 * p, 128), 128)
-        for i in range(images):
-            q, k, v = q_ref[i, :, lanes], k_ref[i, :, lanes], v_ref[i, :, lanes]
-            go = go_ref[i, :, lanes]
-            allowed = jnp.broadcast_to(valid_ref[i], (rows, keys)) > 0.0
-            dq = jnp.zeros((rows, 128), f32)
-            dk = jnp.zeros((keys, 128), f32)
-            dv = jnp.zeros((keys, 128), f32)
-            for mask, key_mask, factor in zip(masks, key_masks, factors):
-                probs = soft(mm(q * factor, k, RIGHT_T), allowed)
-                dv = jnp.where(key_mask, mm(probs.astype(bf), go, LEFT_T), dv)
-                dprobs = mm(go * factor, v, RIGHT_T)
-                dscores = probs * (dprobs - jnp.sum(dprobs * probs, -1, keepdims=True))
-                low = dscores.astype(bf)
-                dq = jnp.where(mask, mm(low, k) * scale, dq)
-                dk = jnp.where(key_mask, mm(low, q, LEFT_T), dk)
-            dq_ref[i, :, lanes] = dq
+        allowed = [jnp.broadcast_to(valid_ref[i], (rows, keys)) > 0.0 for i in range(images)]
+        jobs = head_jobs(q_ref, k_ref, v_ref, p, span, factors)
+        grads = [go_ref[job[0], :, job[1]] for job in jobs]
+        scores = [mm(q * factors[h], k, RIGHT_T) for _, _, h, q, k, _ in jobs]
+        dprobs = [mm(go * factors[job[2]], job[5], RIGHT_T) for go, job in zip(grads, jobs)]
+        probs = [soft(s, allowed[job[0]]) for s, job in zip(scores, jobs)]
+        lows = [
+            (a * (da - jnp.sum(da * a, -1, keepdims=True))).astype(bf) for a, da in zip(probs, dprobs)
+        ]
+        dvs = [mm(a.astype(bf), go, LEFT_T) for a, go in zip(probs, grads)]
+        dqs = [mm(low, job[4]) for low, job in zip(lows, jobs)]
+        dks = [mm(low, job[3], LEFT_T) for low, job in zip(lows, jobs)]
+        for n in range(0, len(jobs), len(masks)):
+            dq, dk, dv = dqs[n], dks[n], dvs[n]
+            for h in range(1, len(masks)):
+                dq = jnp.where(masks[h], dqs[n + h], dq)
+                dk = jnp.where(key_masks[h], dks[n + h], dk)
+                dv = jnp.where(key_masks[h], dvs[n + h], dv)
+            i, lanes = jobs[n][:2]
+            dq_ref[i, :, lanes] = dq * scale
             dk_ref[i, :, lanes] = dk
             dv_ref[i, :, lanes] = dv
         return carry
 
-    lax.fori_loop(0, width // 128, group, 0)
+    lax.fori_loop(0, width // 128 // span, group, 0)
 
 
 def split_rows(ref, value):
@@ -439,7 +465,7 @@
     return jnp.concatenate([ref[i] for i in range(ref.shape[0])], 0)
 
 
-STRIP = 384
+STRIP = 768
 
 
 def feed_forward(normed, mid, up, down, vec, pre_ref, acc_ref):
@@ -1046,9 +1072,14 @@
     (((5, 0), (6, 1), (8, 3)), (1, 2, 4)),
     (((3, 0), (7, 1)), (5, 6)),
     (((9, 0), (10, 1), (12, 2)), (3, 7, 8)),
-    (((13, 0), (14, 1)), (9, 10, 12)),
-    (((11, 0), (15, 1)), (13, 14)),
+    (((11, 0), (14, 1), (13, 2)), (9, 10, 12)),
 )
+LAST = 15
+
+
+def thirds(slot_count):
+    size = -(-slot_count // 3)
+    return size, [(start, min(start + size, slot_count)) for start in range(0, slot_count, size)]
 
 
 def gather_pieces(own, extra):
@@ -1066,7 +1097,12 @@
         source = dict(zip(names, values))
         for piece, bit in moves:
             held[piece] = both.swap(source[piece ^ (1 << bit)], bit)
-    return [held[piece] for piece in range(both.ranks)], extra
+    names = [LAST ^ 1, LAST ^ 2, LAST ^ 4]
+    source = lax.optimization_barrier([held[name] for name in names])
+    ends = [
+        both.swap(source[bit][low:high], bit) for bit, (low, high) in enumerate(thirds(own.shape[0])[1])
+    ]
+    return [held[piece] for piece in range(LAST)] + ends, extra
 
 
 class Exchange:
@@ -1228,7 +1264,11 @@
         places = jnp.concatenate([jnp.zeros_like(slot_of), slot_of] + place)
     else:
         sources = jnp.bitwise_xor(slot_of // slot_count, owner_index)
-        places = jnp.concatenate([sources, slot_of % slot_count] + place)
+        indices = slot_of % slot_count
+        size, _ = thirds(slot_count)
+        is_last = sources == LAST
+        sources = jnp.where(is_last, LAST + indices // size, sources)
+        places = jnp.concatenate([sources, jnp.where(is_last, indices % size, indices)] + place)
     (
         pixel_rows, enc_pos_ctx, ctx_keys, enc_vec_now, pixel_all, pos_all, pixel_tgt, enc_pos_tgt,
         all_valid, pred_pos_ctx, pred_pos_tgt, joined_valid, tgt_mask, pred_vec_now,

time: 721 us -> 663 us (0.920)
  Pallas kernels: 219 us -> 186 us
  waiting for transfers between devices: 310 us -> 278 us
    ppermute x4, waiting for transfers between devices: 52.5 us -> 32.5 us  [from_behind(): return lax.ppermute(shard, axis, pairs)]
    pallas_call x5, Pallas kernels: 84.5 us -> 65.4 us  [call_kernel(): pl.pallas_call(guarded, grid_spec=pltpu.PrefetchScalarGridSpec(num_scalar...]
    ppermute x32 -> x34, waiting for transfers between devices: 257 us -> 245 us  [trade(): return lax.ppermute(value, ('section', 'dp'), pairs)]
    pallas_call x1, Pallas kernels: 48.9 us -> 40.2 us  [soap_first(): pl.pallas_call(first_kernel, grid_spec=pltpu.PrefetchScalarGridSpec(num_s...]
    ppermute x32 -> x34, starting transfers between devices: 63.4 us -> 64 us  [trade(): return lax.ppermute(value, ('section', 'dp'), pairs)]
  transfers between devices with their start and end apart: 38 -> 40, of which waited for: 27 -> 29; matrix products, arithmetic and copies ran while one was open for 8% -> 9% of each run, Pallas kernels for 16% -> 15%
where the time goes in v2:
time: 663 us; the launch traced here: 653 us
  waiting for transfers between devices  278 us (42%)
  Pallas kernels  186 us (28%)
  starting transfers between devices  75.3 us (11%)
  other arithmetic  57.9 us (9%)
  local copies, waits for them, and re-layouts  27.8 us (4%)
  between operations  17.7 us (3%)
  matrix products  11.2 us (2%)
    ppermute x34, waiting for transfers between devices, trade(): return lax.ppermute(value, ('section', 'dp'), pairs)  245 us
    pallas_call x5, Pallas kernels, call_kernel(): pl.pallas_call(guarded, grid_spec=pltpu.PrefetchScalarGridSpec(num_scalar...  65.4 us
    ppermute x34, starting transfers between devices, trade(): return lax.ppermute(value, ('section', 'dp'), pairs)  64 us
    pallas_call x1, Pallas kernels, soap_factor(): pl.pallas_call(factor_kernel, grid_spec=pltpu.PrefetchScalarGridSpec(num_...  62 us
    pallas_call x1, Pallas kernels, soap_first(): pl.pallas_call(first_kernel, grid_spec=pltpu.PrefetchScalarGridSpec(num_s...  40.2 us
    ppermute x4, waiting for transfers between devices, from_behind(): return lax.ppermute(shard, axis, pairs)  32.5 us
    convert_element_type x4, other arithmetic, pack(): return marked.astype(WIRE)  19.3 us
    pallas_call x1, Pallas kernels, soap_last(): pl.pallas_call(last_kernel, grid_spec=pltpu.PrefetchScalarGridSpec(num_sc...  16.7 us
  transfers between devices with their start and end apart: 40, of which 29 were waited for; matrix products, arithmetic and copies ran while one was open for 9% of the time, Pallas kernels for 15%

profile of v2, /device:TPU:4, one launch (start us, length us, event | category | flops | bytes accessed | tf_op | source)
XLA Modules:
  0.0 653.5 jit_solution(5780933809892010148)
XLA Ops:
  0.7 2.0 bitcast_convert_fusion.refs_0_
  2.7 1.6 collective-permute-start.6
  4.8 1.6 collective-permute-start.8
  7.1 2.2 multiply_sine_fusion.1
  11.1 2.1 fusion.50
  13.2 2.0 copy.38
  15.2 2.4 fusion.26
  17.6 2.4 fusion.25
  20.0 2.7 fusion.23
  22.7 1.6 fusion.21
  26.4 10.4 %collective-permute-done.6.refs_1_ = bf16[5,384,384]{2,1,0:T(8,128)(2,1)S(1)} collective-permute-done((bf16[5,384,384]{2,1,0:T(8,128)(2,1)S(1)}, bf16[5,384,384]{2,1,0:T(8,128)(2,1)S(1)}, u32[]{:S(2)}, u32[]{:S(2)}) %collective-permute-start.6) | collective-permute-done | bytes 1474592 | tf_op jit(solution)/shard_map/ppermute | solution.py:1123
  38.7 1.7 collective-permute-start.10
  41.7 2.0 pad.26.clone
  45.4 2.6 collective-permute-start.13
  48.0 23.3 %collective-permute-done.9.refs_5_ = bf16[5,384,384]{2,1,0:T(8,128)(2,1)} collective-permute-done((bf16[5,384,384]{2,1,0:T(8,128)(2,1)}, bf16[5,384,384]{2,1,0:T(8,128)(2,1)}, u32[]{:S(2)}, u32[]{:S(2)}) %collective-permute-start.9) | collective-permute-done | bytes 1474592 | tf_op jit(solution)/shard_map/ppermute | solution.py:1123
  76.2 33.7 %collective-permute-done.13.refs_8_ = bf16[5,384,384]{2,1,0:T(8,128)(2,1)S(1)} collective-permute-done((bf16[5,384,384]{2,1,0:T(8,128)(2,1)S(1)}, bf16[5,384,384]{2,1,0:T(8,128)(2,1)S(1)}, u32[]{:S(2)}, u32[]{:S(2)}) %collective-permute-start.13) | collective-permute-done | bytes 1474592 | tf_op jit(solution)/shard_map/ppermute | solution.py:1123
  109.9 1.6 collective-permute-start.14
  112.7 30.4 %collective-permute-done.14.refs_9_ = bf16[5,384,384]{2,1,0:T(8,128)(2,1)S(1)} collective-permute-done((bf16[5,384,384]{2,1,0:T(8,128)(2,1)S(1)}, bf16[5,384,384]{2,1,0:T(8,128)(2,1)S(1)}, u32[]{:S(2)}, u32[]{:S(2)}) %collective-permute-start.14) | collective-permute-done | bytes 1474592 | tf_op jit(solution)/shard_map/ppermute | solution.py:1123
  145.3 1.7 collective-permute-start.18
  148.4 28.3 %collective-permute-done.17.refs_11_ = bf16[5,384,384]{2,1,0:T(8,128)(2,1)S(1)} collective-permute-done((bf16[5,384,384]{2,1,0:T(8,128)(2,1)S(1)}, bf16[5,384,384]{2,1,0:T(8,128)(2,1)S(1)}, u32[]{:S(2)}, u32[]{:S(2)}) %collective-permute-start.17) | collective-permute-done | bytes 1474592 | tf_op jit(solution)/shard_map/ppermute | solution.py:1123
  186.0 5.7 collective-permute-done.22.refs_17_
  192.8 2.1 collective-permute-done.21.refs_16_
  195.0 16.8 %encoder_forward.1 = (bf16[256,768]{1,0:T(8,128)(2,1)}, f32[256,768]{1,0:T(8,128)}, bf16[2,128,768]{2,1,0:T(8,128)(2,1)}, bf16[2,128,768]{2,1,0:T(8,128)(2,1)}, ...) custom-call(s32[138]{0:T(256)} %pad_add_fusion.places_ref, ...), custom_call_target="tpu_custom_call" | custom-call | bytes 75000000 | tf_op jit(solution)/shard_map/encoder_forward/pallas_call | solution.py:849
  213.9 1.7 target_forward.1.refs_22_
  216.3 7.1 %predictor_step.1 = (bf16[256,768]{1,0:T(8,128)(2,1)}, f32[4,400,384]{2,1,0:T(8,128)}, f32[4,400,384]{2,1,0:T(8,128)S(1)}, f32[4,400,384]{2,1,0:T(8,128)}, f32[4...) custom-call(s32[138]{0:T(256)} %pad_add_fusion.places_ref, ...), custom_call_target="tpu_custom_call" | custom-call | bytes 150000000 | tf_op jit(solution)/shard_map/predictor_step/pallas_call | solution.py:849
  224.8 31.6 %collective-permute-done.24.refs_18_ = bf16[256,768]{1,0:T(8,128)(2,1)S(1)} collective-permute-done((bf16[256,768]{1,0:T(8,128)(2,1)}, bf16[256,768]{1,0:T(8,128)(2,1)S(1)}, u32[]{:S(2)}, u32[]{:S(2)}) %collective-permute-start.24) | collective-permute-done | bytes 393248 | tf_op jit(solution)/shard_map/ppermute | solution.py:51
  257.2 22.4 %feed_backward.1 = (f32[4,784,384]{2,1,0:T(8,128)}, f32[4,784,384]{2,1,0:T(8,128)}, f32[4,784,384]{2,1,0:T(8,128)}, f32[4,784,384]{2,1,0:T(8,128)}, f32[256,768]...) custom-call(s32[138]{0:T(256)} %pad_add_fusion.places_ref, bf16[5,384,384]{2,1,0:T(8,128)(2,1)} %copy-done.1, ...), custom_call_target="tpu_custom_call" | custom-call | bytes 75000000 | tf_op jit(solution)/shard_map/feed_backward/pallas_call | solution.py:849
  281.7 8.1 %select_convert_fusion.6 = (f16[4,784,384]{2,1,0:T(8,128)(2,1)}, f16[4,784,384]{2,1,0:T(8,128)(2,1)}, f16[4,784,384]{2,1,0:T(8,128)(2,1)}) fusion(f32[4,784,384]{2,1,0:T(8,128)} %get-tuple-element.151, f32[]{:T(128)S(6)} %floor.18, f32[]{:T(128)S(6)} %exp2.213, pred[784]{0:T(1024)(128)(4,1)S(1)} %iota_compare_fusion.10, ...), kind=kLoop, calls=%fused_computation.21 | loop fusion | flops 10838016 | bytes 21676824 | tf_op jit(solution)/shard_map/convert_element_type | solution.py:1138
  289.7 2.4 collective-permute-start.25
  292.2 3.1 collective-permute-start.26
  295.3 3.7 collective-permute-start.27
  299.0 17.4 %attention_backward.1 = (f32[4,496,384]{2,1,0:T(8,128)}, f32[4,496,384]{2,1,0:T(8,128)}, f32[4,496,384]{2,1,0:T(8,128)}, f32[4,496,384]{2,1,0:T(8,128)}, f32[1,11520]{1,0:T(1,128)}, /*index=5*/f32[1,384]{1,0:T(1,128)}) custom-call(s32[138]{0:T(256)} %pad_add_fusion.places_ref, bf16[5,384,384]{2,1,0:T(8,128)(2,1)} %copy-done.1, ...), custom_call_target="tpu_custom_call" | custom-call | bytes 75000000 | tf_op jit(solution)/shard_map/attention_backward/pallas_call | solution.py:849
  318.4 6.6 %select_convert_fusion.10 = (f16[4,496,384]{2,1,0:T(8,128)(2,1)}, f16[4,496,384]{2,1,0:T(8,128)(2,1)}, f16[4,496,384]{2,1,0:T(8,128)(2,1)}) fusion(f32[4,496,384]{2,1,0:T(8,128)} %get-tuple-element.166, f32[]{:T(128)S(6)} %floor.19, f32[]{:T(128)S(6)} %exp2.215, pred[496]{0:T(512)(128)(4,1)S(1)} %iota_compare_fusion.12, ...), kind=kLoop, calls=%fused_computation.25 | loop fusion | flops 6856704 | bytes 13713912 | tf_op jit(solution)/shard_map/convert_element_type | solution.py:1138
  325.0 24.5 %collective-permute-done.26 = f16[4,784,384]{2,1,0:T(8,128)(2,1)} collective-permute-done((f16[4,784,384]{2,1,0:T(8,128)(2,1)}, f16[4,784,384]{2,1,0:T(8,128)(2,1)}, u32[]{:S(2)}, u32[]{:S(2)}) %collective-permute-start.26) | collective-permute-done | bytes 2408480 | tf_op jit(solution)/shard_map/ppermute | solution.py:1123
  349.6 4.0 collective-permute-start.30
  353.6 2.8 collective-permute-start.29
  356.3 2.6 collective-permute-start.28
  364.6 7.8 %multiply_add_fusion.1 = f32[4,784,384]{2,1,0:T(8,128)} fusion(f16[4,784,384]{2,1,0:T(8,128)(2,1)} %collective-permute-done.27, f16[4,784,384]{2,1,0:T(8,128)(2,1)} %collective-permute-done.26, f32[4,784,384]{2,1,0:T(8,128)} %get-tuple-element.170, f16[4,784,384]{2,1,0:T(8,128)(2,1)S(1)} %collective-permute-done.25, f32[]{:T(128)} %bitcast.27, f32[]{:T(128)} %bitcast.26, ...), kind=kLoop, calls=%fused_computation.20 | loop fusion | flops 10838016 | bytes 16859148 | tf_op jit(solution)/shard_map/add | solution.py:1171
  374.5 14.4 %collective-permute-done.29 = f16[4,496,384]{2,1,0:T(8,128)(2,1)} collective-permute-done((f16[4,496,384]{2,1,0:T(8,128)(2,1)}, f16[4,496,384]{2,1,0:T(8,128)(2,1)}, u32[]{:S(2)}, u32[]{:S(2)}) %collective-permute-start.29) | collective-permute-done | bytes 1523744 | tf_op jit(solution)/shard_map/ppermute | solution.py:1123
  393.4 4.2 fusion.4
  397.9 2.8 fusion.12
  400.8 7.0 %collective-permute-start.33 = (f16[1,1264,384]{2,1,0:T(8,128)(2,1)}, f16[1,1264,384]{2,1,0:T(8,128)(2,1)}, u32[]{:S(2)}, u32[]{:S(2)}) collective-permute-start(f16[1,1264,384]{2,1,0:T(8,128)(2,1)} %get-tuple-element.204), channel_id=1, source_target_pairs={{0,12},{1,13},{2,14},{3,15},{4,8},{5,9},{6,10},{7,11},{8,4},{9,5},... | collective-permute-start | bytes 2912264 | tf_op jit(solution)/shard_map/ppermute | solution.py:1123
  407.8 1.9 collective-permute-start.32
  409.7 2.5 collective-permute-start.31
  412.2 14.6 %collective-permute-done.33 = f16[1,1264,384]{2,1,0:T(8,128)(2,1)} collective-permute-done((f16[1,1264,384]{2,1,0:T(8,128)(2,1)}, f16[1,1264,384]{2,1,0:T(8,128)(2,1)}, u32[]{:S(2)}, u32[]{:S(2)}) %collective-permute-start.33) | collective-permute-done | bytes 970784 | tf_op jit(solution)/shard_map/ppermute | solution.py:1123
  428.7 40.5 %collective-permute-done.32 = f16[1,1264,384]{2,1,0:T(8,128)(2,1)} collective-permute-done((f16[1,1264,384]{2,1,0:T(8,128)(2,1)}, f16[1,1264,384]{2,1,0:T(8,128)(2,1)}, u32[]{:S(2)}, u32[]{:S(2)}) %collective-permute-start.32) | collective-permute-done | bytes 970784 | tf_op jit(solution)/shard_map/ppermute | solution.py:1123
  473.1 3.5 multiply_reduce_fusion
  476.6 1.5 place_shares.1
  478.1 1.8 select_convert_fusion.9
  479.9 6.0 all-to-all-start
  489.5 1.5 collective-permute-start.38
  491.8 1.9 collective-permute-done.38
  495.2 2.0 collective-permute-start.34
  497.9 2.4 collective-permute-start.40
  502.4 5.1 collective-permute-start.41
  507.7 2.4 collective-permute-done.41
  511.0 1.5 collective-permute-start.37
  513.2 2.3 collective-permute-done.37
  520.9 1.8 copy.42
  522.7 40.2 %soap_first.1 = (f32[5,384,384]{2,1,0:T(8,128)}, f32[5,384,384]{2,1,0:T(8,128)}, f32[5,384,384]{2,1,0:T(8,128)}, f32[5,384,384]{2,1,0:T(8,128)}, f32[5,384,384]{...) custom-call(s32[5]{0:T(128)} %get-tuple-element.223.flag, f32[1]{0:T(128)} %bitcast.38.factor, ...), custom_call_target="tpu_custom_call" | custom-call | tf_op jit(solution)/shard_map/soap_first/pallas_call | solution.py:990
  562.9 3.2 convert_element_type.320
  571.0 62.0 %soap_factor.1.q_ref = f32[5,2,384,384]{3,2,1,0:T(8,128)} custom-call(s32[5]{0:T(128)} %get-tuple-element.223.flag, f32[5,2,384,384]{3,2,1,0:T(8,128)} %get-tuple-element.182.base_ref, f32[5,2,384,384]{3,2,1,0:T(8,128)} %get-tuple-element.183.gram_ref), custom_call_target="tpu_custom_call" | custom-call | tf_op jit(solution)/shard_map/soap_factor/pallas_call | solution.py:1004
  633.1 16.7 %soap_last.1 = (f32[5,384,384]{2,1,0:T(8,128)}, f32[5,384,384]{2,1,0:T(8,128)}, f32[5,384,384]{2,1,0:T(8,128)}) custom-call(s32[5]{0:T(128)} %get-tuple-element.223.flag, f32[5,384,384]{2,1,0:T(8,128)} %bitcast.83, f32[5,384,384]{2,1,0:T(8,128)} %bitcast.85, f32[5,384,384]{2,1,0:T(8,128)} %get-tuple-element.181.m_ref, f32[5,2,384,384]{3,2,1,0:T(8,128)} %soap_factor.1.q_ref), custom_call_target="tpu_custom_call" | custom-call | tf_op jit(solution)/shard_map/soap_last/pallas_call | solution.py:1027
  649.7 2.2 select_bitcast_fusion
  (193 shorter events, 63.6 us)
Async XLA Ops:
  0.6 5.8 copy-start.34
  0.7 10.1 %copy-start.30 = (s32[2,4]{1,0:T(2,128)S(1)}, s32[2,4]{1,0:T(2,128)}, u32[]{:S(2)}) copy-start(s32[2,4]{1,0:T(2,128)} %param.22) | copy-start | bytes 100
  2.7 42.7 %copy-start.1 = (bf16[5,384,384]{2,1,0:T(8,128)(2,1)}, bf16[5,384,384]{2,1,0:T(8,128)(2,1)S(1)}, u32[]{:S(2)}) copy-start(bf16[5,384,384]{2,1,0:T(8,128)(2,1)S(1)} %bitcast_convert_fusion.refs_0_) | copy-start | bytes 4423684
  2.7 12.4 %copy-start.32 = (s32[2,4,36]{2,1,0:T(4,128)S(1)}, s32[2,4,36]{2,1,0:T(4,128)}, u32[]{:S(2)}) copy-start(s32[2,4,36]{2,1,0:T(4,128)} %param.21) | copy-start | bytes 3460
  2.7 12.5 %copy-start.31 = (s32[2,128]{1,0:T(2,128)S(1)}, s32[2,128]{1,0:T(2,128)}, u32[]{:S(2)}) copy-start(s32[2,128]{1,0:T(2,128)} %param.19) | copy-start | bytes 3076
  2.7 34.1 %collective-permute-start.6 = (bf16[5,384,384]{2,1,0:T(8,128)(2,1)S(1)}, bf16[5,384,384]{2,1,0:T(8,128)(2,1)S(1)}, u32[]{:S(2)}, u32[]{:S(2)}) collective-permute-start(bf16[5,384,384]{2,1,0:T(8,128)(2,1)S(1)} %bitcast_convert_fusion.refs_0_), channel_id=1, source_target_pairs={{0,1},{1,0},{2,3},{3,2},{4,5},{5,4},{6,7},{7,6},{8,9},{9,8},{10,11... | collective-permute-start | bytes 4423688 | tf_op jit(solution)/shard_map/ppermute | solution.py:1123
  4.3 33.9 %collective-permute-start.7 = (bf16[5,384,384]{2,1,0:T(8,128)(2,1)S(1)}, bf16[5,384,384]{2,1,0:T(8,128)(2,1)}, u32[]{:S(2)}, u32[]{:S(2)}) collective-permute-start(bf16[5,384,384]{2,1,0:T(8,128)(2,1)S(1)} %bitcast_convert_fusion.refs_0_), channel_id=1, source_target_pairs={{0,2},{1,3},{2,0},{3,1},{4,6},{5,7},{6,4},{7,5},{8,10},{9,11},{10,... | collective-permute-start | bytes 4423688 | tf_op jit(solution)/shard_map/ppermute | solution.py:1123
  4.8 33.6 %collective-permute-start.8 = (bf16[5,384,384]{2,1,0:T(8,128)(2,1)S(1)}, bf16[5,384,384]{2,1,0:T(8,128)(2,1)}, u32[]{:S(2)}, u32[]{:S(2)}) collective-permute-start(bf16[5,384,384]{2,1,0:T(8,128)(2,1)S(1)} %bitcast_convert_fusion.refs_0_), channel_id=1, source_target_pairs={{0,4},{1,5},{2,6},{3,7},{4,0},{5,1},{6,2},{7,3},{8,12},{9,13},{10,... | collective-permute-start | bytes 4423688 | tf_op jit(solution)/shard_map/ppermute | solution.py:1123
  15.2 7.5 %copy-start.17 = (f32[196,192]{1,0:T(8,128)S(1)}, f32[196,192]{1,0:T(8,128)}, u32[]{:S(2)}) copy-start(f32[196,192]{1,0:T(8,128)} %get-tuple-element.220) | copy-start | bytes 451588
  15.2 7.5 %copy-start.18 = (f32[196,192]{1,0:T(8,128)S(1)}, f32[196,192]{1,0:T(8,128)}, u32[]{:S(2)}) copy-start(f32[196,192]{1,0:T(8,128)} %get-tuple-element.221) | copy-start | bytes 451588
  15.2 9.1 %copy-start.19 = (bf16[2,196,768]{2,0,1:T(2,128)(2,1)S(1)}, bf16[2,196,768]{2,0,1:T(2,128)(2,1)}, u32[]{:S(2)}) copy-start(bf16[2,196,768]{2,0,1:T(2,128)(2,1)} %param.18) | copy-start | bytes 1806340
  20.0 21.1 %copy-start.22 = (f32[1,18432]{1,0:T(1,128)S(1)}, f32[1,18432]{1,0:T(1,128)}, u32[]{:S(2)}) copy-start(f32[1,18432]{1,0:T(1,128)} %param.31) | copy-start | bytes 221188
  36.8 108.5 %copy-start.6 = (bf16[5,384,384]{2,1,0:T(8,128)(2,1)}, bf16[5,384,384]{2,1,0:T(8,128)(2,1)S(1)}, u32[]{:S(2)}) copy-start(bf16[5,384,384]{2,1,0:T(8,128)(2,1)S(1)} %collective-permute-done.6.refs_1_) | copy-start | bytes 4423684
  38.3 32.9 %collective-permute-start.9 = (bf16[5,384,384]{2,1,0:T(8,128)(2,1)}, bf16[5,384,384]{2,1,0:T(8,128)(2,1)}, u32[]{:S(2)}, u32[]{:S(2)}) collective-permute-start(bf16[5,384,384]{2,1,0:T(8,128)(2,1)} %collective-permute-done.8.refs_4_), channel_id=1, source_target_pairs={{0,1},{1,0},{2,3},{3,2},{4,5},{5,4},{6,7},{7,6},{8,9},{9,8},{10,11... | collective-permute-start | bytes 4423688 | tf_op jit(solution)/shard_map/ppermute | solution.py:1123
  38.7 33.0 %collective-permute-start.10 = (bf16[5,384,384]{2,1,0:T(8,128)(2,1)}, bf16[5,384,384]{2,1,0:T(8,128)(2,1)}, u32[]{:S(2)}, u32[]{:S(2)}) collective-permute-start(bf16[5,384,384]{2,1,0:T(8,128)(2,1)} %collective-permute-done.8.refs_4_), channel_id=1, source_target_pairs={{0,2},{1,3},{2,0},{3,1},{4,6},{5,7},{6,4},{7,5},{8,10},{9,11},{10,... | collective-permute-start | bytes 4423688 | tf_op jit(solution)/shard_map/ppermute | solution.py:1123
  44.8 139.1 %copy-start = (s32[68]{0:T(128)S(1)}, s32[68]{0:T(128)}, u32[]{:S(2)}) copy-start(s32[68]{0:T(128)} %slots_ref.1) | copy-start | bytes 820
  45.4 64.5 %collective-permute-start.13 = (bf16[5,384,384]{2,1,0:T(8,128)(2,1)S(1)}, bf16[5,384,384]{2,1,0:T(8,128)(2,1)S(1)}, u32[]{:S(2)}, u32[]{:S(2)}) collective-permute-start(bf16[5,384,384]{2,1,0:T(8,128)(2,1)S(1)} %bitcast_convert_fusion.refs_0_), channel_id=1, source_target_pairs={{0,8},{1,9},{2,10},{3,11},{4,12},{5,13},{6,14},{7,15},{8,0},{9,1},... | collective-permute-start | bytes 4423688 | tf_op jit(solution)/shard_map/ppermute | solution.py:1123
  73.4 36.5 %collective-permute-start.11 = (bf16[5,384,384]{2,1,0:T(8,128)(2,1)}, bf16[5,384,384]{2,1,0:T(8,128)(2,1)S(1)}, u32[]{:S(2)}, u32[]{:S(2)}) collective-permute-start(bf16[5,384,384]{2,1,0:T(8,128)(2,1)} %collective-permute-done.7.refs_2_), channel_id=1, source_target_pairs={{0,1},{1,0},{2,3},{3,2},{4,5},{5,4},{6,7},{7,6},{8,9},{9,8},{10,11... | collective-permute-start | bytes 4423688 | tf_op jit(solution)/shard_map/ppermute | solution.py:1123
  74.7 35.2 %collective-permute-start.12 = (bf16[5,384,384]{2,1,0:T(8,128)(2,1)}, bf16[5,384,384]{2,1,0:T(8,128)(2,1)S(1)}, u32[]{:S(2)}, u32[]{:S(2)}) collective-permute-start(bf16[5,384,384]{2,1,0:T(8,128)(2,1)} %collective-permute-done.9.refs_5_), channel_id=1, source_target_pairs={{0,2},{1,3},{2,0},{3,1},{4,6},{5,7},{6,4},{7,5},{8,10},{9,11},{10,... | collective-permute-start | bytes 4423688 | tf_op jit(solution)/shard_map/ppermute | solution.py:1123
  109.9 69.4 %copy-start.7 = (bf16[5,384,384]{2,1,0:T(8,128)(2,1)}, bf16[5,384,384]{2,1,0:T(8,128)(2,1)S(1)}, u32[]{:S(2)}) copy-start(bf16[5,384,384]{2,1,0:T(8,128)(2,1)S(1)} %collective-permute-done.13.refs_8_) | copy-start | bytes 4423684
  109.9 34.4 %copy-start.8 = (bf16[5,384,384]{2,1,0:T(8,128)(2,1)}, bf16[5,384,384]{2,1,0:T(8,128)(2,1)S(1)}, u32[]{:S(2)}) copy-start(bf16[5,384,384]{2,1,0:T(8,128)(2,1)S(1)} %collective-permute-done.11.refs_3_) | copy-start | bytes 4423684
  109.9 67.9 %copy-start.9 = (bf16[5,384,384]{2,1,0:T(8,128)(2,1)}, bf16[5,384,384]{2,1,0:T(8,128)(2,1)S(1)}, u32[]{:S(2)}) copy-start(bf16[5,384,384]{2,1,0:T(8,128)(2,1)S(1)} %collective-permute-done.12.refs_7_) | copy-start | bytes 4423684
  109.9 33.2 %collective-permute-start.14 = (bf16[5,384,384]{2,1,0:T(8,128)(2,1)S(1)}, bf16[5,384,384]{2,1,0:T(8,128)(2,1)S(1)}, u32[]{:S(2)}, u32[]{:S(2)}) collective-permute-start(bf16[5,384,384]{2,1,0:T(8,128)(2,1)S(1)} %collective-permute-done.13.refs_8_), channel_id=1, source_target_pairs={{0,1},{1,0},{2,3},{3,2},{4,5},{5,4},{6,7},{7,6},{8,9},{9,8},{10,11... | collective-permute-start | bytes 4423688 | tf_op jit(solution)/shard_map/ppermute | solution.py:1123
  111.5 32.8 %collective-permute-start.15 = (bf16[5,384,384]{2,1,0:T(8,128)(2,1)S(1)}, bf16[5,384,384]{2,1,0:T(8,128)(2,1)S(1)}, u32[]{:S(2)}, u32[]{:S(2)}) collective-permute-start(bf16[5,384,384]{2,1,0:T(8,128)(2,1)S(1)} %collective-permute-done.13.refs_8_), channel_id=1, source_target_pairs={{0,2},{1,3},{2,0},{3,1},{4,6},{5,7},{6,4},{7,5},{8,10},{9,11},{10,... | collective-permute-start | bytes 4423688 | tf_op jit(solution)/shard_map/ppermute | solution.py:1123
  112.1 32.6 %collective-permute-start.16 = (bf16[5,384,384]{2,1,0:T(8,128)(2,1)S(1)}, bf16[5,384,384]{2,1,0:T(8,128)(2,1)S(1)}, u32[]{:S(2)}, u32[]{:S(2)}) collective-permute-start(bf16[5,384,384]{2,1,0:T(8,128)(2,1)S(1)} %collective-permute-done.13.refs_8_), channel_id=1, source_target_pairs={{0,4},{1,5},{2,6},{3,7},{4,0},{5,1},{6,2},{7,3},{8,12},{9,13},{10,... | collective-permute-start | bytes 4423688 | tf_op jit(solution)/shard_map/ppermute | solution.py:1123
  143.1 34.7 %copy-start.10 = (bf16[5,384,384]{2,1,0:T(8,128)(2,1)}, bf16[5,384,384]{2,1,0:T(8,128)(2,1)S(1)}, u32[]{:S(2)}) copy-start(bf16[5,384,384]{2,1,0:T(8,128)(2,1)S(1)} %collective-permute-done.14.refs_9_) | copy-start | bytes 4423684
  144.3 33.5 %copy-start.11 = (bf16[5,384,384]{2,1,0:T(8,128)(2,1)}, bf16[5,384,384]{2,1,0:T(8,128)(2,1)S(1)}, u32[]{:S(2)}) copy-start(bf16[5,384,384]{2,1,0:T(8,128)(2,1)S(1)} %collective-permute-done.15.refs_10_) | copy-start | bytes 4423684
  144.6 33.2 %copy-start.12 = (bf16[5,384,384]{2,1,0:T(8,128)(2,1)}, bf16[5,384,384]{2,1,0:T(8,128)(2,1)S(1)}, u32[]{:S(2)}) copy-start(bf16[5,384,384]{2,1,0:T(8,128)(2,1)S(1)} %collective-permute-done.16.refs_12_) | copy-start | bytes 4423684
  144.6 32.0 %collective-permute-start.17 = (bf16[5,384,384]{2,1,0:T(8,128)(2,1)S(1)}, bf16[5,384,384]{2,1,0:T(8,128)(2,1)S(1)}, u32[]{:S(2)}, u32[]{:S(2)}) collective-permute-start(bf16[5,384,384]{2,1,0:T(8,128)(2,1)S(1)} %collective-permute-done.15.refs_10_), channel_id=1, source_target_pairs={{0,1},{1,0},{2,3},{3,2},{4,5},{5,4},{6,7},{7,6},{8,9},{9,8},{10,11... | collective-permute-start | bytes 4423688 | tf_op jit(solution)/shard_map/ppermute | solution.py:1123
  145.3 32.5 %collective-permute-start.18 = (bf16[5,384,384]{2,1,0:T(8,128)(2,1)S(1)}, bf16[5,384,384]{2,1,0:T(8,128)(2,1)S(1)}, u32[]{:S(2)}, u32[]{:S(2)}) collective-permute-start(bf16[5,384,384]{2,1,0:T(8,128)(2,1)S(1)} %collective-permute-done.14.refs_9_), channel_id=1, source_target_pairs={{0,4},{1,5},{2,6},{3,7},{4,0},{5,1},{6,2},{7,3},{8,12},{9,13},{10,... | collective-permute-start | bytes 4423688 | tf_op jit(solution)/shard_map/ppermute | solution.py:1123
  147.1 32.2 %collective-permute-start.19 = (bf16[5,384,384]{2,1,0:T(8,128)(2,1)S(1)}, bf16[5,384,384]{2,1,0:T(8,128)(2,1)S(1)}, u32[]{:S(2)}, u32[]{:S(2)}) collective-permute-start(bf16[5,384,384]{2,1,0:T(8,128)(2,1)S(1)} %collective-permute-done.16.refs_12_), channel_id=1, source_target_pairs={{0,2},{1,3},{2,0},{3,1},{4,6},{5,7},{6,4},{7,5},{8,10},{9,11},{10,... | collective-permute-start | bytes 4423688 | tf_op jit(solution)/shard_map/ppermute | solution.py:1123
  177.8 17.1 %copy-start.3 = (bf16[5,384,384]{2,1,0:T(8,128)(2,1)}, bf16[5,384,384]{2,1,0:T(8,128)(2,1)S(1)}, u32[]{:S(2)}) copy-start(bf16[5,384,384]{2,1,0:T(8,128)(2,1)S(1)} %collective-permute-done.18.refs_13_) | copy-start | bytes 4423684
  179.3 15.7 %copy-start.4 = (bf16[5,384,384]{2,1,0:T(8,128)(2,1)}, bf16[5,384,384]{2,1,0:T(8,128)(2,1)S(1)}, u32[]{:S(2)}) copy-start(bf16[5,384,384]{2,1,0:T(8,128)(2,1)S(1)} %collective-permute-done.19.refs_14_) | copy-start | bytes 4423684
  180.2 12.5 %collective-permute-start.20 = (bf16[2,384,384]{2,1,0:T(8,128)(2,1)}, bf16[2,384,384]{2,1,0:T(8,128)(2,1)S(1)}, u32[]{:S(2)}, u32[]{:S(2)}) collective-permute-start(bf16[2,384,384]{2,1,0:T(8,128)(2,1)} %slice.111), channel_id=1, source_target_pairs={{0,1},{1,0},{2,3},{3,2},{4,5},{5,4},{6,7},{7,6},{8,9},{9,8},{10,11... | collective-permute-start | bytes 1769480 | tf_op jit(solution)/shard_map/ppermute | solution.py:1123
  182.5 12.4 %collective-permute-start.21 = (bf16[2,384,384]{2,1,0:T(8,128)(2,1)}, bf16[2,384,384]{2,1,0:T(8,128)(2,1)}, u32[]{:S(2)}, u32[]{:S(2)}) collective-permute-start(bf16[2,384,384]{2,1,0:T(8,128)(2,1)} %slice.112), channel_id=1, source_target_pairs={{0,2},{1,3},{2,0},{3,1},{4,6},{5,7},{6,4},{7,5},{8,10},{9,11},{10,... | collective-permute-start | bytes 1769480 | tf_op jit(solution)/shard_map/ppermute | solution.py:1123
  184.9 6.8 %collective-permute-start.22 = (bf16[1,384,384]{2,1,0:T(8,128)(2,1)S(1)}, bf16[1,384,384]{2,1,0:T(8,128)(2,1)S(1)}, u32[]{:S(2)}, u32[]{:S(2)}) collective-permute-start(bf16[1,384,384]{2,1,0:T(8,128)(2,1)S(1)} %slice.113), channel_id=1, source_target_pairs={{0,4},{1,5},{2,6},{3,7},{4,0},{5,1},{6,2},{7,3},{8,12},{9,13},{10,... | collective-permute-start | bytes 884744 | tf_op jit(solution)/shard_map/ppermute | solution.py:1123
  211.7 3.8 collective-permute-start.23
  223.5 32.9 %collective-permute-start.24 = (bf16[256,768]{1,0:T(8,128)(2,1)}, bf16[256,768]{1,0:T(8,128)(2,1)S(1)}, u32[]{:S(2)}, u32[]{:S(2)}) collective-permute-start(bf16[256,768]{1,0:T(8,128)(2,1)} %get-tuple-element.135), channel_id=1, source_target_pairs={{16,0},{17,1},{18,2},{19,3},{20,4},{21,5},{22,6},{23,7},{24,8},{25... | collective-permute-start | bytes 1179656 | tf_op jit(solution)/shard_map/ppermute | solution.py:51
  289.7 35.3 %collective-permute-start.25 = (f16[4,784,384]{2,1,0:T(8,128)(2,1)}, f16[4,784,384]{2,1,0:T(8,128)(2,1)S(1)}, u32[]{:S(2)}, u32[]{:S(2)}) collective-permute-start(f16[4,784,384]{2,1,0:T(8,128)(2,1)} %get-tuple-element.160), channel_id=1, source_target_pairs={{0,1},{1,0},{2,3},{3,2},{4,5},{5,4},{6,7},{7,6},{8,9},{9,8},{10,11... | collective-permute-start | bytes 7225352 | tf_op jit(solution)/shard_map/ppermute | solution.py:1123
  292.2 57.4 %collective-permute-start.26 = (f16[4,784,384]{2,1,0:T(8,128)(2,1)}, f16[4,784,384]{2,1,0:T(8,128)(2,1)}, u32[]{:S(2)}, u32[]{:S(2)}) collective-permute-start(f16[4,784,384]{2,1,0:T(8,128)(2,1)} %get-tuple-element.161), channel_id=1, source_target_pairs={{0,2},{1,3},{2,0},{3,1},{4,6},{5,7},{6,4},{7,5},{8,10},{9,11},{10,... | collective-permute-start | bytes 7225352 | tf_op jit(solution)/shard_map/ppermute | solution.py:1123
  295.3 54.3 %collective-permute-start.27 = (f16[4,784,384]{2,1,0:T(8,128)(2,1)}, f16[4,784,384]{2,1,0:T(8,128)(2,1)}, u32[]{:S(2)}, u32[]{:S(2)}) collective-permute-start(f16[4,784,384]{2,1,0:T(8,128)(2,1)} %get-tuple-element.162), channel_id=1, source_target_pairs={{0,3},{1,2},{2,1},{3,0},{4,7},{5,6},{6,5},{7,4},{8,11},{9,10},{10,... | collective-permute-start | bytes 7225352 | tf_op jit(solution)/shard_map/ppermute | solution.py:1123
  349.6 23.1 %collective-permute-start.30 = (f16[4,496,384]{2,1,0:T(8,128)(2,1)}, f16[4,496,384]{2,1,0:T(8,128)(2,1)}, u32[]{:S(2)}, u32[]{:S(2)}) collective-permute-start(f16[4,496,384]{2,1,0:T(8,128)(2,1)} %get-tuple-element.169), channel_id=1, source_target_pairs={{0,3},{1,2},{2,1},{3,0},{4,7},{5,6},{6,5},{7,4},{8,11},{9,10},{10,... | collective-permute-start | bytes 4571144 | tf_op jit(solution)/shard_map/ppermute | solution.py:1123
  353.6 35.3 %collective-permute-start.29 = (f16[4,496,384]{2,1,0:T(8,128)(2,1)}, f16[4,496,384]{2,1,0:T(8,128)(2,1)}, u32[]{:S(2)}, u32[]{:S(2)}) collective-permute-start(f16[4,496,384]{2,1,0:T(8,128)(2,1)} %get-tuple-element.168), channel_id=1, source_target_pairs={{0,2},{1,3},{2,0},{3,1},{4,6},{5,7},{6,4},{7,5},{8,10},{9,11},{10,... | collective-permute-start | bytes 4571144 | tf_op jit(solution)/shard_map/ppermute | solution.py:1123
  356.3 34.4 %collective-permute-start.28 = (f16[4,496,384]{2,1,0:T(8,128)(2,1)}, f16[4,496,384]{2,1,0:T(8,128)(2,1)}, u32[]{:S(2)}, u32[]{:S(2)}) collective-permute-start(f16[4,496,384]{2,1,0:T(8,128)(2,1)} %get-tuple-element.167), channel_id=1, source_target_pairs={{0,1},{1,0},{2,3},{3,2},{4,5},{5,4},{6,7},{7,6},{8,9},{9,8},{10,11... | collective-permute-start | bytes 4571144 | tf_op jit(solution)/shard_map/ppermute | solution.py:1123
  400.8 26.1 %collective-permute-start.33 = (f16[1,1264,384]{2,1,0:T(8,128)(2,1)}, f16[1,1264,384]{2,1,0:T(8,128)(2,1)}, u32[]{:S(2)}, u32[]{:S(2)}) collective-permute-start(f16[1,1264,384]{2,1,0:T(8,128)(2,1)} %get-tuple-element.204), channel_id=1, source_target_pairs={{0,12},{1,13},{2,14},{3,15},{4,8},{5,9},{6,10},{7,11},{8,4},{9,5},... | collective-permute-start | bytes 2912264 | tf_op jit(solution)/shard_map/ppermute | solution.py:1123
  407.8 61.5 %collective-permute-start.32 = (f16[1,1264,384]{2,1,0:T(8,128)(2,1)}, f16[1,1264,384]{2,1,0:T(8,128)(2,1)}, u32[]{:S(2)}, u32[]{:S(2)}) collective-permute-start(f16[1,1264,384]{2,1,0:T(8,128)(2,1)} %get-tuple-element.203), channel_id=1, source_target_pairs={{0,8},{1,9},{2,10},{3,11},{4,12},{5,13},{6,14},{7,15},{8,0},{9,1},... | collective-permute-start | bytes 2912264 | tf_op jit(solution)/shard_map/ppermute | solution.py:1123
  409.7 61.4 %collective-permute-start.31 = (f16[1,1264,384]{2,1,0:T(8,128)(2,1)}, f16[1,1264,384]{2,1,0:T(8,128)(2,1)}, u32[]{:S(2)}, u32[]{:S(2)}) collective-permute-start(f16[1,1264,384]{2,1,0:T(8,128)(2,1)} %get-tuple-element.202), channel_id=1, source_target_pairs={{0,4},{1,5},{2,6},{3,7},{4,0},{5,1},{6,2},{7,3},{8,12},{9,13},{10,... | collective-permute-start | bytes 2912264 | tf_op jit(solution)/shard_map/ppermute | solution.py:1123
  479.9 7.3 %copy-start.33 = (f32[1,768]{1,0:T(1,128)S(1)}, f32[1,768]{1,0:T(1,128)}, u32[]{:S(2)}) copy-start(f32[1,768]{1,0:T(1,128)} %get-tuple-element.178) | copy-start | bytes 9220
  479.9 8.6 %copy-start.28 = (f32[1,6912]{1,0:T(1,128)S(1)}, f32[1,6912]{1,0:T(1,128)}, u32[]{:S(2)}) copy-start(f32[1,6912]{1,0:T(1,128)} %get-tuple-element.177) | copy-start | bytes 82948
  479.9 8.7 %copy-start.29 = (f32[1,11520]{1,0:T(1,128)S(1)}, f32[1,11520]{1,0:T(1,128)}, u32[]{:S(2)}) copy-start(f32[1,11520]{1,0:T(1,128)} %get-tuple-element.176) | copy-start | bytes 138244
  479.9 40.2 %all-to-all-start = ((f16[16,136,384]{2,1,0:T(8,128)(2,1)}), f16[16,136,384]{2,1,0:T(8,128)(2,1)S(1)}, u32[]{:S(2)}, u32[]{:S(2)}) async-start(f16[16,136,384]{2,1,0:T(8,128)(2,1)} %select_convert_fusion.9), calls=%async_computation | async-start | bytes 3342336 | tf_op jit(solution)/shard_map/all_to_all | solution.py:1347
  489.5 4.2 collective-permute-start.38
  493.7 4.2 collective-permute-start.39
  495.2 5.1 collective-permute-start.34
  497.9 4.5 collective-permute-start.40
  500.3 7.2 %collective-permute-start.35 = (f32[128]{0:T(128)S(1)}, f32[128]{0:T(128)S(1)}, u32[]{:S(2)}, u32[]{:S(2)}) collective-permute-start(f32[128]{0:T(128)S(1)} %broadcast_add_fusion), channel_id=1, source_target_pairs={{0,2},{1,3},{2,0},{3,1},{4,6},{5,7},{6,4},{7,5},{8,10},{9,11},{10,... | collective-permute-start | bytes 1544 | tf_op jit(solution)/shard_map/ppermute | solution.py:1123
  502.4 7.8 %collective-permute-start.41 = (f32[11648]{0:T(1024)S(1)}, f32[11648]{0:T(1024)S(1)}, u32[]{:S(2)}, u32[]{:S(2)}) collective-permute-start(f32[11648]{0:T(1024)S(1)} %add.262), channel_id=1, source_target_pairs={{0,8},{1,9},{2,10},{3,11},{4,12},{5,13},{6,14},{7,15},{8,0},{9,1},... | collective-permute-start | bytes 139784 | tf_op jit(solution)/shard_map/ppermute | solution.py:1123
  507.5 3.5 collective-permute-start.36
  511.0 4.4 collective-permute-start.37
  516.3 1.1 collective-permute-start.42
  566.1 83.6 %collective-permute-start.43 = (bf16[5,384,384]{2,1,0:T(8,128)(2,1)}, bf16[5,384,384]{2,1,0:T(8,128)(2,1)S(1)}, u32[]{:S(2)}, u32[]{:S(2)}) collective-permute-start(bf16[5,384,384]{2,1,0:T(8,128)(2,1)} %convert_element_type.320), channel_id=1, source_target_pairs={{0,16},{1,17},{2,18},{3,19},{4,20},{5,21},{6,22},{7,23},{8,24},{9,... | collective-permute-start | bytes 4423688 | tf_op jit(solution)/shard_map/ppermute | solution.py:51
  568.2 2.1 collective-permute-start.44
  633.0 16.7 %copy-start.13 = (f32[1,5,384,384]{3,2,1,0:T(8,128)S(1)}, f32[1,5,384,384]{3,2,1,0:T(8,128)}, u32[]{:S(2)}) copy-start(f32[1,5,384,384]{3,2,1,0:T(8,128)} %param.24) | copy-start | bytes 8847364
  633.1 16.7 %copy-start.15 = (f32[5,384,384]{2,1,0:T(8,128)S(1)}, f32[5,384,384]{2,1,0:T(8,128)}, u32[]{:S(2)}) copy-start(f32[5,384,384]{2,1,0:T(8,128)} %get-tuple-element.180) | copy-start | bytes 8847364
  (9 other events, 26.5 us)

commit v3 on v2

--- a/solution.py
+++ b/solution.py
@@ -1317,8 +1317,10 @@
     rest_arrived = send_packed(ahead, lows, 0)
     feed_shares, feed_bound = add_pieces(feed_pieces[0], feed_arrived, feed_bound)
     rest_shares, rest_bound = add_pieces(rest_pieces[0], rest_arrived, rest_bound)
-    enc_shares = jnp.concatenate([rest_shares[:, :-MARKS], feed_shares], 1)
-    enc_sum, enc_bound = finish_sum(ahead, enc_shares, jnp.maximum(rest_bound, feed_bound))
+    feed_sum, feed_bound = finish_sum(ahead, feed_shares, feed_bound)
+    rest_sum, rest_bound = finish_sum(ahead, rest_shares, rest_bound)
+    enc_sum = jnp.concatenate([rest_sum, feed_sum], 0)
+    enc_bound = jnp.maximum(rest_bound, feed_bound)
     cut_at = 6 * D
     enc_vec = jnp.concatenate([rest_vec[:, :cut_at], feed_vec[:, cut_at:]], 1)
     depth = edge // ranks

time: 663 us -> 623 us (0.940)
  the two profiles are of different devices: /device:TPU:4 before, /device:TPU:2 now
where the time goes in v3:
time: 623 us; the launch traced here: 611 us
  waiting for transfers between devices  220 us (35%)
  Pallas kernels  185 us (30%)
  starting transfers between devices  85.3 us (14%)
  other arithmetic  57.2 us (9%)
  local copies, waits for them, and re-layouts  32.7 us (5%)
  between operations  19.9 us (3%)
  matrix products  11.2 us (2%)
    ppermute x37, waiting for transfers between devices, trade(): return lax.ppermute(value, ('section', 'dp'), pairs)  187 us
    ppermute x37, starting transfers between devices, trade(): return lax.ppermute(value, ('section', 'dp'), pairs)  68.7 us
    pallas_call x5, Pallas kernels, call_kernel(): pl.pallas_call(guarded, grid_spec=pltpu.PrefetchScalarGridSpec(num_scalar...  65 us
    pallas_call x1, Pallas kernels, soap_factor(): pl.pallas_call(factor_kernel, grid_spec=pltpu.PrefetchScalarGridSpec(num_...  62 us
    pallas_call x1, Pallas kernels, soap_first(): pl.pallas_call(first_kernel, grid_spec=pltpu.PrefetchScalarGridSpec(num_s...  40.2 us
    ppermute x4, waiting for transfers between devices, from_behind(): return lax.ppermute(shard, axis, pairs)  32.4 us
    convert_element_type x5, other arithmetic, pack(): return marked.astype(WIRE)  19.4 us
    pallas_call x1, Pallas kernels, soap_last(): pl.pallas_call(last_kernel, grid_spec=pltpu.PrefetchScalarGridSpec(num_sc...  16.7 us
  transfers between devices with their start and end apart: 43, of which 28 were waited for; matrix products, arithmetic and copies ran while one was open for 12% of the time, Pallas kernels for 16%

profile of v3, /device:TPU:2, one launch (start us, length us, event | category | flops | bytes accessed | tf_op | source)
XLA Modules:
  0.0 611.3 jit_solution(11387488856750104505)
XLA Ops:
  0.7 2.0 bitcast_convert_fusion.refs_0_
  2.8 2.0 collective-permute-start.7
  4.8 1.6 collective-permute-start.8
  7.2 2.2 multiply_sine_fusion.1
  11.2 2.1 fusion.38
  13.3 2.0 copy.38
  15.3 2.4 fusion.14
  17.7 2.3 fusion.13
  20.1 2.7 fusion.11
  22.8 1.6 fusion.9
  26.6 10.2 %collective-permute-done.6.refs_1_ = bf16[5,384,384]{2,1,0:T(8,128)(2,1)S(1)} collective-permute-done((bf16[5,384,384]{2,1,0:T(8,128)(2,1)S(1)}, bf16[5,384,384]{2,1,0:T(8,128)(2,1)S(1)}, u32[]{:S(2)}, u32[]{:S(2)}) %collective-permute-start.6) | collective-permute-done | bytes 1474592 | tf_op jit(solution)/shard_map/ppermute | solution.py:1123
  41.7 2.0 pad.26.clone
  45.4 2.6 collective-permute-start.13
  48.0 23.3 %collective-permute-done.9.refs_5_ = bf16[5,384,384]{2,1,0:T(8,128)(2,1)} collective-permute-done((bf16[5,384,384]{2,1,0:T(8,128)(2,1)}, bf16[5,384,384]{2,1,0:T(8,128)(2,1)}, u32[]{:S(2)}, u32[]{:S(2)}) %collective-permute-start.9) | collective-permute-done | bytes 1474592 | tf_op jit(solution)/shard_map/ppermute | solution.py:1123
  75.4 34.5 %collective-permute-done.13.refs_8_ = bf16[5,384,384]{2,1,0:T(8,128)(2,1)S(1)} collective-permute-done((bf16[5,384,384]{2,1,0:T(8,128)(2,1)S(1)}, bf16[5,384,384]{2,1,0:T(8,128)(2,1)S(1)}, u32[]{:S(2)}, u32[]{:S(2)}) %collective-permute-start.13) | collective-permute-done | bytes 1474592 | tf_op jit(solution)/shard_map/ppermute | solution.py:1123
  112.7 30.5 %collective-permute-done.14.refs_9_ = bf16[5,384,384]{2,1,0:T(8,128)(2,1)S(1)} collective-permute-done((bf16[5,384,384]{2,1,0:T(8,128)(2,1)S(1)}, bf16[5,384,384]{2,1,0:T(8,128)(2,1)S(1)}, u32[]{:S(2)}, u32[]{:S(2)}) %collective-permute-start.14) | collective-permute-done | bytes 1474592 | tf_op jit(solution)/shard_map/ppermute | solution.py:1123
  146.1 1.7 collective-permute-start.18
  148.4 28.2 %collective-permute-done.17.refs_11_ = bf16[5,384,384]{2,1,0:T(8,128)(2,1)S(1)} collective-permute-done((bf16[5,384,384]{2,1,0:T(8,128)(2,1)S(1)}, bf16[5,384,384]{2,1,0:T(8,128)(2,1)S(1)}, u32[]{:S(2)}, u32[]{:S(2)}) %collective-permute-start.17) | collective-permute-done | bytes 1474592 | tf_op jit(solution)/shard_map/ppermute | solution.py:1123
  176.6 1.9 collective-permute-done.18.refs_13_
  186.0 5.0 collective-permute-done.22.refs_17_
  191.0 2.5 collective-permute-done.20.refs_15_
  194.8 16.8 %encoder_forward.1 = (bf16[256,768]{1,0:T(8,128)(2,1)}, f32[256,768]{1,0:T(8,128)}, bf16[2,128,768]{2,1,0:T(8,128)(2,1)}, bf16[2,128,768]{2,1,0:T(8,128)(2,1)}, ...) custom-call(s32[138]{0:T(256)} %pad_add_fusion.places_ref, ...), custom_call_target="tpu_custom_call" | custom-call | bytes 75000000 | tf_op jit(solution)/shard_map/encoder_forward/pallas_call | solution.py:849
  213.7 1.6 target_forward.1.refs_22_
  216.1 7.1 %predictor_step.1 = (bf16[256,768]{1,0:T(8,128)(2,1)}, f32[4,400,384]{2,1,0:T(8,128)}, f32[4,400,384]{2,1,0:T(8,128)S(1)}, f32[4,400,384]{2,1,0:T(8,128)}, f32[4...) custom-call(s32[138]{0:T(256)} %pad_add_fusion.places_ref, ...), custom_call_target="tpu_custom_call" | custom-call | bytes 150000000 | tf_op jit(solution)/shard_map/predictor_step/pallas_call | solution.py:849
  224.6 31.6 %collective-permute-done.24.refs_18_ = bf16[256,768]{1,0:T(8,128)(2,1)S(1)} collective-permute-done((bf16[256,768]{1,0:T(8,128)(2,1)}, bf16[256,768]{1,0:T(8,128)(2,1)S(1)}, u32[]{:S(2)}, u32[]{:S(2)}) %collective-permute-start.24) | collective-permute-done | bytes 393248 | tf_op jit(solution)/shard_map/ppermute | solution.py:51
  257.0 22.2 %feed_backward.1 = (f32[4,784,384]{2,1,0:T(8,128)}, f32[4,784,384]{2,1,0:T(8,128)}, f32[4,784,384]{2,1,0:T(8,128)}, f32[4,784,384]{2,1,0:T(8,128)}, f32[256,768]...) custom-call(s32[138]{0:T(256)} %pad_add_fusion.places_ref, bf16[5,384,384]{2,1,0:T(8,128)(2,1)} %copy-done.1, ...), custom_call_target="tpu_custom_call" | custom-call | bytes 75000000 | tf_op jit(solution)/shard_map/feed_backward/pallas_call | solution.py:849
  281.2 8.1 %select_convert_fusion.6 = (f16[4,784,384]{2,1,0:T(8,128)(2,1)}, f16[4,784,384]{2,1,0:T(8,128)(2,1)}, f16[4,784,384]{2,1,0:T(8,128)(2,1)}) fusion(f32[4,784,384]{2,1,0:T(8,128)} %get-tuple-element.151, f32[]{:T(128)S(6)} %floor.20, f32[]{:T(128)S(6)} %exp2.253, pred[784]{0:T(1024)(128)(4,1)S(1)} %iota_compare_fusion.9, ...), kind=kLoop, calls=%fused_computation.13 | loop fusion | flops 10838016 | bytes 21676824 | tf_op jit(solution)/shard_map/convert_element_type | solution.py:1138
  289.3 3.4 collective-permute-start.25
  292.6 2.7 collective-permute-start.26
  295.4 3.1 collective-permute-start.27
  298.5 17.3 %attention_backward.1 = (f32[4,496,384]{2,1,0:T(8,128)}, f32[4,496,384]{2,1,0:T(8,128)}, f32[4,496,384]{2,1,0:T(8,128)}, f32[4,496,384]{2,1,0:T(8,128)}, f32[1,11520]{1,0:T(1,128)}, /*index=5*/f32[1,384]{1,0:T(1,128)}) custom-call(s32[138]{0:T(256)} %pad_add_fusion.places_ref, bf16[5,384,384]{2,1,0:T(8,128)(2,1)} %copy-done.1, ...), custom_call_target="tpu_custom_call" | custom-call | bytes 75000000 | tf_op jit(solution)/shard_map/attention_backward/pallas_call | solution.py:849
  317.8 6.6 %select_convert_fusion.10 = (f16[4,496,384]{2,1,0:T(8,128)(2,1)}, f16[4,496,384]{2,1,0:T(8,128)(2,1)}, f16[4,496,384]{2,1,0:T(8,128)(2,1)}) fusion(f32[4,496,384]{2,1,0:T(8,128)} %get-tuple-element.166, f32[]{:T(128)S(6)} %floor.21, f32[]{:T(128)S(6)} %exp2.255, pred[496]{0:T(512)(128)(4,1)S(1)} %iota_compare_fusion.11, ...), kind=kLoop, calls=%fused_computation.18 | loop fusion | flops 6856704 | bytes 13713912 | tf_op jit(solution)/shard_map/convert_element_type | solution.py:1138
  324.4 25.6 %collective-permute-done.26 = f16[4,784,384]{2,1,0:T(8,128)(2,1)} collective-permute-done((f16[4,784,384]{2,1,0:T(8,128)(2,1)}, f16[4,784,384]{2,1,0:T(8,128)(2,1)}, u32[]{:S(2)}, u32[]{:S(2)}) %collective-permute-start.26) | collective-permute-done | bytes 2408480 | tf_op jit(solution)/shard_map/ppermute | solution.py:1123
  350.0 2.7 collective-permute-start.30
  352.8 3.1 collective-permute-start.29
  355.9 3.8 collective-permute-start.28
  365.4 5.6 multiply_add_fusion.1
  371.0 1.7 select_convert_fusion.15
  372.7 1.6 copy-done.13
  374.3 6.0 collective-permute-start.36
  380.3 1.9 collective-permute-start.35
  382.3 2.5 collective-permute-start.34
  386.6 2.7 collective-permute-done.29
  393.1 3.2 multiply_add_fusion.2
  398.3 6.0 collective-permute-start.33
  404.3 1.9 collective-permute-start.32
  406.3 2.5 collective-permute-start.31
  410.7 5.1 collective-permute-done.35
  419.5 3.1 fusion.5
  428.5 1.5 fusion.8
  432.7 1.8 select_convert_fusion.9
  434.5 11.3 %all-to-all-start = ((f16[16,136,384]{2,1,0:T(8,128)(2,1)}), f16[16,136,384]{2,1,0:T(8,128)(2,1)S(1)}, u32[]{:S(2)}, u32[]{:S(2)}) async-start(f16[16,136,384]{2,1,0:T(8,128)(2,1)} %select_convert_fusion.9), calls=%async_computation | async-start | bytes 3342336 | tf_op jit(solution)/shard_map/all_to_all | solution.py:1349
  450.3 3.3 collective-permute-done.41
  457.9 1.5 collective-permute-start.43
  462.0 3.4 collective-permute-start.44
  466.8 2.2 collective-permute-done.44
  469.0 1.6 collective-permute-start.40
  471.3 2.2 collective-permute-done.40
  478.9 1.8 copy.42
  480.7 40.2 %soap_first.1 = (f32[5,384,384]{2,1,0:T(8,128)}, f32[5,384,384]{2,1,0:T(8,128)}, f32[5,384,384]{2,1,0:T(8,128)}, f32[5,384,384]{2,1,0:T(8,128)}, f32[5,384,384]{...) custom-call(s32[5]{0:T(128)} %get-tuple-element.226.flag, f32[1]{0:T(128)} %bitcast.43.factor, ...), custom_call_target="tpu_custom_call" | custom-call | tf_op jit(solution)/shard_map/soap_first/pallas_call | solution.py:990
  520.9 3.2 convert_element_type.365
  529.1 62.0 %soap_factor.1.q_ref = f32[5,2,384,384]{3,2,1,0:T(8,128)} custom-call(s32[5]{0:T(128)} %get-tuple-element.226.flag, f32[5,2,384,384]{3,2,1,0:T(8,128)} %get-tuple-element.182.base_ref, f32[5,2,384,384]{3,2,1,0:T(8,128)} %get-tuple-element.183.gram_ref), custom_call_target="tpu_custom_call" | custom-call | tf_op jit(solution)/shard_map/soap_factor/pallas_call | solution.py:1004
  591.1 16.7 %soap_last.1 = (f32[5,384,384]{2,1,0:T(8,128)}, f32[5,384,384]{2,1,0:T(8,128)}, f32[5,384,384]{2,1,0:T(8,128)}) custom-call(s32[5]{0:T(128)} %get-tuple-element.226.flag, f32[5,384,384]{2,1,0:T(8,128)} %bitcast.90, f32[5,384,384]{2,1,0:T(8,128)} %bitcast.92, f32[5,384,384]{2,1,0:T(8,128)} %get-tuple-element.181.m_ref, f32[5,2,384,384]{3,2,1,0:T(8,128)} %soap_factor.1.q_ref), custom_call_target="tpu_custom_call" | custom-call | tf_op jit(solution)/shard_map/soap_last/pallas_call | solution.py:1027
  607.8 2.2 select_bitcast_fusion
  (212 shorter events, 73.8 us)
Async XLA Ops:
  2.7 42.7 %copy-start.1 = (bf16[5,384,384]{2,1,0:T(8,128)(2,1)}, bf16[5,384,384]{2,1,0:T(8,128)(2,1)S(1)}, u32[]{:S(2)}) copy-start(bf16[5,384,384]{2,1,0:T(8,128)(2,1)S(1)} %bitcast_convert_fusion.refs_0_) | copy-start | bytes 4423684
  2.7 12.5 %copy-start.36 = (s32[2,4,36]{2,1,0:T(4,128)S(1)}, s32[2,4,36]{2,1,0:T(4,128)}, u32[]{:S(2)}) copy-start(s32[2,4,36]{2,1,0:T(4,128)} %param.21) | copy-start | bytes 3460
  2.7 12.6 %copy-start.35 = (s32[2,128]{1,0:T(2,128)S(1)}, s32[2,128]{1,0:T(2,128)}, u32[]{:S(2)}) copy-start(s32[2,128]{1,0:T(2,128)} %param.19) | copy-start | bytes 3076
  2.7 34.1 %collective-permute-start.6 = (bf16[5,384,384]{2,1,0:T(8,128)(2,1)S(1)}, bf16[5,384,384]{2,1,0:T(8,128)(2,1)S(1)}, u32[]{:S(2)}, u32[]{:S(2)}) collective-permute-start(bf16[5,384,384]{2,1,0:T(8,128)(2,1)S(1)} %bitcast_convert_fusion.refs_0_), channel_id=1, source_target_pairs={{0,1},{1,0},{2,3},{3,2},{4,5},{5,4},{6,7},{7,6},{8,9},{9,8},{10,11... | collective-permute-start | bytes 4423688 | tf_op jit(solution)/shard_map/ppermute | solution.py:1123
  2.8 34.2 %collective-permute-start.7 = (bf16[5,384,384]{2,1,0:T(8,128)(2,1)S(1)}, bf16[5,384,384]{2,1,0:T(8,128)(2,1)}, u32[]{:S(2)}, u32[]{:S(2)}) collective-permute-start(bf16[5,384,384]{2,1,0:T(8,128)(2,1)S(1)} %bitcast_convert_fusion.refs_0_), channel_id=1, source_target_pairs={{0,2},{1,3},{2,0},{3,1},{4,6},{5,7},{6,4},{7,5},{8,10},{9,11},{10,... | collective-permute-start | bytes 4423688 | tf_op jit(solution)/shard_map/ppermute | solution.py:1123
  4.8 33.6 %collective-permute-start.8 = (bf16[5,384,384]{2,1,0:T(8,128)(2,1)S(1)}, bf16[5,384,384]{2,1,0:T(8,128)(2,1)}, u32[]{:S(2)}, u32[]{:S(2)}) collective-permute-start(bf16[5,384,384]{2,1,0:T(8,128)(2,1)S(1)} %bitcast_convert_fusion.refs_0_), channel_id=1, source_target_pairs={{0,4},{1,5},{2,6},{3,7},{4,0},{5,1},{6,2},{7,3},{8,12},{9,13},{10,... | collective-permute-start | bytes 4423688 | tf_op jit(solution)/shard_map/ppermute | solution.py:1123
  20.1 21.0 %copy-start.26 = (f32[1,18432]{1,0:T(1,128)S(1)}, f32[1,18432]{1,0:T(1,128)}, u32[]{:S(2)}) copy-start(f32[1,18432]{1,0:T(1,128)} %param.31) | copy-start | bytes 221188
  36.8 109.3 %copy-start.5 = (bf16[5,384,384]{2,1,0:T(8,128)(2,1)}, bf16[5,384,384]{2,1,0:T(8,128)(2,1)S(1)}, u32[]{:S(2)}) copy-start(bf16[5,384,384]{2,1,0:T(8,128)(2,1)S(1)} %collective-permute-done.6.refs_1_) | copy-start | bytes 4423684
  38.4 32.9 %collective-permute-start.9 = (bf16[5,384,384]{2,1,0:T(8,128)(2,1)}, bf16[5,384,384]{2,1,0:T(8,128)(2,1)}, u32[]{:S(2)}, u32[]{:S(2)}) collective-permute-start(bf16[5,384,384]{2,1,0:T(8,128)(2,1)} %collective-permute-done.8.refs_4_), channel_id=1, source_target_pairs={{0,1},{1,0},{2,3},{3,2},{4,5},{5,4},{6,7},{7,6},{8,9},{9,8},{10,11... | collective-permute-start | bytes 4423688 | tf_op jit(solution)/shard_map/ppermute | solution.py:1123
  39.9 32.6 %collective-permute-start.10 = (bf16[5,384,384]{2,1,0:T(8,128)(2,1)}, bf16[5,384,384]{2,1,0:T(8,128)(2,1)}, u32[]{:S(2)}, u32[]{:S(2)}) collective-permute-start(bf16[5,384,384]{2,1,0:T(8,128)(2,1)} %collective-permute-done.8.refs_4_), channel_id=1, source_target_pairs={{0,2},{1,3},{2,0},{3,1},{4,6},{5,7},{6,4},{7,5},{8,10},{9,11},{10,... | collective-permute-start | bytes 4423688 | tf_op jit(solution)/shard_map/ppermute | solution.py:1123
  44.8 138.5 %copy-start = (s32[68]{0:T(128)S(1)}, s32[68]{0:T(128)}, u32[]{:S(2)}) copy-start(s32[68]{0:T(128)} %slots_ref.1) | copy-start | bytes 820
  45.4 64.6 %collective-permute-start.13 = (bf16[5,384,384]{2,1,0:T(8,128)(2,1)S(1)}, bf16[5,384,384]{2,1,0:T(8,128)(2,1)S(1)}, u32[]{:S(2)}, u32[]{:S(2)}) collective-permute-start(bf16[5,384,384]{2,1,0:T(8,128)(2,1)S(1)} %bitcast_convert_fusion.refs_0_), channel_id=1, source_target_pairs={{0,8},{1,9},{2,10},{3,11},{4,12},{5,13},{6,14},{7,15},{8,0},{9,1},... | collective-permute-start | bytes 4423688 | tf_op jit(solution)/shard_map/ppermute | solution.py:1123
  74.2 35.8 %collective-permute-start.11 = (bf16[5,384,384]{2,1,0:T(8,128)(2,1)}, bf16[5,384,384]{2,1,0:T(8,128)(2,1)S(1)}, u32[]{:S(2)}, u32[]{:S(2)}) collective-permute-start(bf16[5,384,384]{2,1,0:T(8,128)(2,1)} %collective-permute-done.7.refs_2_), channel_id=1, source_target_pairs={{0,1},{1,0},{2,3},{3,2},{4,5},{5,4},{6,7},{7,6},{8,9},{9,8},{10,11... | collective-permute-start | bytes 4423688 | tf_op jit(solution)/shard_map/ppermute | solution.py:1123
  74.7 35.2 %collective-permute-start.12 = (bf16[5,384,384]{2,1,0:T(8,128)(2,1)}, bf16[5,384,384]{2,1,0:T(8,128)(2,1)S(1)}, u32[]{:S(2)}, u32[]{:S(2)}) collective-permute-start(bf16[5,384,384]{2,1,0:T(8,128)(2,1)} %collective-permute-done.9.refs_5_), channel_id=1, source_target_pairs={{0,2},{1,3},{2,0},{3,1},{4,6},{5,7},{6,4},{7,5},{8,10},{9,11},{10,... | collective-permute-start | bytes 4423688 | tf_op jit(solution)/shard_map/ppermute | solution.py:1123
  110.0 70.1 %copy-start.6 = (bf16[5,384,384]{2,1,0:T(8,128)(2,1)}, bf16[5,384,384]{2,1,0:T(8,128)(2,1)S(1)}, u32[]{:S(2)}) copy-start(bf16[5,384,384]{2,1,0:T(8,128)(2,1)S(1)} %collective-permute-done.13.refs_8_) | copy-start | bytes 4423684
  110.0 33.6 %copy-start.7 = (bf16[5,384,384]{2,1,0:T(8,128)(2,1)}, bf16[5,384,384]{2,1,0:T(8,128)(2,1)S(1)}, u32[]{:S(2)}) copy-start(bf16[5,384,384]{2,1,0:T(8,128)(2,1)S(1)} %collective-permute-done.11.refs_3_) | copy-start | bytes 4423684
  110.0 68.6 %copy-start.8 = (bf16[5,384,384]{2,1,0:T(8,128)(2,1)}, bf16[5,384,384]{2,1,0:T(8,128)(2,1)S(1)}, u32[]{:S(2)}) copy-start(bf16[5,384,384]{2,1,0:T(8,128)(2,1)S(1)} %collective-permute-done.12.refs_7_) | copy-start | bytes 4423684
  110.0 33.2 %collective-permute-start.14 = (bf16[5,384,384]{2,1,0:T(8,128)(2,1)S(1)}, bf16[5,384,384]{2,1,0:T(8,128)(2,1)S(1)}, u32[]{:S(2)}, u32[]{:S(2)}) collective-permute-start(bf16[5,384,384]{2,1,0:T(8,128)(2,1)S(1)} %collective-permute-done.13.refs_8_), channel_id=1, source_target_pairs={{0,1},{1,0},{2,3},{3,2},{4,5},{5,4},{6,7},{7,6},{8,9},{9,8},{10,11... | collective-permute-start | bytes 4423688 | tf_op jit(solution)/shard_map/ppermute | solution.py:1123
  110.7 32.8 %collective-permute-start.15 = (bf16[5,384,384]{2,1,0:T(8,128)(2,1)S(1)}, bf16[5,384,384]{2,1,0:T(8,128)(2,1)S(1)}, u32[]{:S(2)}, u32[]{:S(2)}) collective-permute-start(bf16[5,384,384]{2,1,0:T(8,128)(2,1)S(1)} %collective-permute-done.13.refs_8_), channel_id=1, source_target_pairs={{0,2},{1,3},{2,0},{3,1},{4,6},{5,7},{6,4},{7,5},{8,10},{9,11},{10,... | collective-permute-start | bytes 4423688 | tf_op jit(solution)/shard_map/ppermute | solution.py:1123
  112.0 32.6 %collective-permute-start.16 = (bf16[5,384,384]{2,1,0:T(8,128)(2,1)S(1)}, bf16[5,384,384]{2,1,0:T(8,128)(2,1)S(1)}, u32[]{:S(2)}, u32[]{:S(2)}) collective-permute-start(bf16[5,384,384]{2,1,0:T(8,128)(2,1)S(1)} %collective-permute-done.13.refs_8_), channel_id=1, source_target_pairs={{0,4},{1,5},{2,6},{3,7},{4,0},{5,1},{6,2},{7,3},{8,12},{9,13},{10,... | collective-permute-start | bytes 4423688 | tf_op jit(solution)/shard_map/ppermute | solution.py:1123
  143.2 35.4 %copy-start.9 = (bf16[5,384,384]{2,1,0:T(8,128)(2,1)}, bf16[5,384,384]{2,1,0:T(8,128)(2,1)S(1)}, u32[]{:S(2)}) copy-start(bf16[5,384,384]{2,1,0:T(8,128)(2,1)S(1)} %collective-permute-done.14.refs_9_) | copy-start | bytes 4423684
  143.6 35.0 %copy-start.10 = (bf16[5,384,384]{2,1,0:T(8,128)(2,1)}, bf16[5,384,384]{2,1,0:T(8,128)(2,1)S(1)}, u32[]{:S(2)}) copy-start(bf16[5,384,384]{2,1,0:T(8,128)(2,1)S(1)} %collective-permute-done.15.refs_10_) | copy-start | bytes 4423684
  144.6 34.0 %copy-start.11 = (bf16[5,384,384]{2,1,0:T(8,128)(2,1)}, bf16[5,384,384]{2,1,0:T(8,128)(2,1)S(1)}, u32[]{:S(2)}) copy-start(bf16[5,384,384]{2,1,0:T(8,128)(2,1)S(1)} %collective-permute-done.16.refs_12_) | copy-start | bytes 4423684
  144.6 32.0 %collective-permute-start.17 = (bf16[5,384,384]{2,1,0:T(8,128)(2,1)S(1)}, bf16[5,384,384]{2,1,0:T(8,128)(2,1)S(1)}, u32[]{:S(2)}, u32[]{:S(2)}) collective-permute-start(bf16[5,384,384]{2,1,0:T(8,128)(2,1)S(1)} %collective-permute-done.15.refs_10_), channel_id=1, source_target_pairs={{0,1},{1,0},{2,3},{3,2},{4,5},{5,4},{6,7},{7,6},{8,9},{9,8},{10,11... | collective-permute-start | bytes 4423688 | tf_op jit(solution)/shard_map/ppermute | solution.py:1123
  146.1 32.4 %collective-permute-start.18 = (bf16[5,384,384]{2,1,0:T(8,128)(2,1)S(1)}, bf16[5,384,384]{2,1,0:T(8,128)(2,1)S(1)}, u32[]{:S(2)}, u32[]{:S(2)}) collective-permute-start(bf16[5,384,384]{2,1,0:T(8,128)(2,1)S(1)} %collective-permute-done.14.refs_9_), channel_id=1, source_target_pairs={{0,4},{1,5},{2,6},{3,7},{4,0},{5,1},{6,2},{7,3},{8,12},{9,13},{10,... | collective-permute-start | bytes 4423688 | tf_op jit(solution)/shard_map/ppermute | solution.py:1123
  147.9 32.2 %collective-permute-start.19 = (bf16[5,384,384]{2,1,0:T(8,128)(2,1)S(1)}, bf16[5,384,384]{2,1,0:T(8,128)(2,1)S(1)}, u32[]{:S(2)}, u32[]{:S(2)}) collective-permute-start(bf16[5,384,384]{2,1,0:T(8,128)(2,1)S(1)} %collective-permute-done.16.refs_12_), channel_id=1, source_target_pairs={{0,2},{1,3},{2,0},{3,1},{4,6},{5,7},{6,4},{7,5},{8,10},{9,11},{10,... | collective-permute-start | bytes 4423688 | tf_op jit(solution)/shard_map/ppermute | solution.py:1123
  178.6 16.2 %copy-start.2 = (bf16[5,384,384]{2,1,0:T(8,128)(2,1)}, bf16[5,384,384]{2,1,0:T(8,128)(2,1)S(1)}, u32[]{:S(2)}) copy-start(bf16[5,384,384]{2,1,0:T(8,128)(2,1)S(1)} %collective-permute-done.18.refs_13_) | copy-start | bytes 4423684
  180.0 14.8 %copy-start.3 = (bf16[5,384,384]{2,1,0:T(8,128)(2,1)}, bf16[5,384,384]{2,1,0:T(8,128)(2,1)S(1)}, u32[]{:S(2)}) copy-start(bf16[5,384,384]{2,1,0:T(8,128)(2,1)S(1)} %collective-permute-done.19.refs_14_) | copy-start | bytes 4423684
  181.0 12.5 %collective-permute-start.20 = (bf16[2,384,384]{2,1,0:T(8,128)(2,1)}, bf16[2,384,384]{2,1,0:T(8,128)(2,1)S(1)}, u32[]{:S(2)}, u32[]{:S(2)}) collective-permute-start(bf16[2,384,384]{2,1,0:T(8,128)(2,1)} %slice.120), channel_id=1, source_target_pairs={{0,1},{1,0},{2,3},{3,2},{4,5},{5,4},{6,7},{7,6},{8,9},{9,8},{10,11... | collective-permute-start | bytes 1769480 | tf_op jit(solution)/shard_map/ppermute | solution.py:1123
  182.4 12.3 %collective-permute-start.21 = (bf16[2,384,384]{2,1,0:T(8,128)(2,1)}, bf16[2,384,384]{2,1,0:T(8,128)(2,1)}, u32[]{:S(2)}, u32[]{:S(2)}) collective-permute-start(bf16[2,384,384]{2,1,0:T(8,128)(2,1)} %slice.121), channel_id=1, source_target_pairs={{0,2},{1,3},{2,0},{3,1},{4,6},{5,7},{6,4},{7,5},{8,10},{9,11},{10,... | collective-permute-start | bytes 1769480 | tf_op jit(solution)/shard_map/ppermute | solution.py:1123
  184.2 6.8 %collective-permute-start.22 = (bf16[1,384,384]{2,1,0:T(8,128)(2,1)S(1)}, bf16[1,384,384]{2,1,0:T(8,128)(2,1)S(1)}, u32[]{:S(2)}, u32[]{:S(2)}) collective-permute-start(bf16[1,384,384]{2,1,0:T(8,128)(2,1)S(1)} %slice.122), channel_id=1, source_target_pairs={{0,4},{1,5},{2,6},{3,7},{4,0},{5,1},{6,2},{7,3},{8,12},{9,13},{10,... | collective-permute-start | bytes 884744 | tf_op jit(solution)/shard_map/ppermute | solution.py:1123
  211.6 3.8 collective-permute-start.23
  223.2 32.9 %collective-permute-start.24 = (bf16[256,768]{1,0:T(8,128)(2,1)}, bf16[256,768]{1,0:T(8,128)(2,1)S(1)}, u32[]{:S(2)}, u32[]{:S(2)}) collective-permute-start(bf16[256,768]{1,0:T(8,128)(2,1)} %get-tuple-element.135), channel_id=1, source_target_pairs={{16,0},{17,1},{18,2},{19,3},{20,4},{21,5},{22,6},{23,7},{24,8},{25... | collective-permute-start | bytes 1179656 | tf_op jit(solution)/shard_map/ppermute | solution.py:51
  256.9 22.2 %copy-start.17 = (f32[384,384]{1,0:T(8,128)}, f32[384,384]{1,0:T(8,128)S(1)}, u32[]{:S(2)}) copy-start(f32[384,384]{1,0:T(8,128)S(1)} %get-tuple-element.174) | copy-start | bytes 1769476
  289.3 35.2 %collective-permute-start.25 = (f16[4,784,384]{2,1,0:T(8,128)(2,1)}, f16[4,784,384]{2,1,0:T(8,128)(2,1)S(1)}, u32[]{:S(2)}, u32[]{:S(2)}) collective-permute-start(f16[4,784,384]{2,1,0:T(8,128)(2,1)} %get-tuple-element.160), channel_id=1, source_target_pairs={{0,1},{1,0},{2,3},{3,2},{4,5},{5,4},{6,7},{7,6},{8,9},{9,8},{10,11... | collective-permute-start | bytes 7225352 | tf_op jit(solution)/shard_map/ppermute | solution.py:1123
  292.6 57.4 %collective-permute-start.26 = (f16[4,784,384]{2,1,0:T(8,128)(2,1)}, f16[4,784,384]{2,1,0:T(8,128)(2,1)}, u32[]{:S(2)}, u32[]{:S(2)}) collective-permute-start(f16[4,784,384]{2,1,0:T(8,128)(2,1)} %get-tuple-element.161), channel_id=1, source_target_pairs={{0,2},{1,3},{2,0},{3,1},{4,6},{5,7},{6,4},{7,5},{8,10},{9,11},{10,... | collective-permute-start | bytes 7225352 | tf_op jit(solution)/shard_map/ppermute | solution.py:1123
  295.4 54.6 %collective-permute-start.27 = (f16[4,784,384]{2,1,0:T(8,128)(2,1)}, f16[4,784,384]{2,1,0:T(8,128)(2,1)}, u32[]{:S(2)}, u32[]{:S(2)}) collective-permute-start(f16[4,784,384]{2,1,0:T(8,128)(2,1)} %get-tuple-element.162), channel_id=1, source_target_pairs={{0,3},{1,2},{2,1},{3,0},{4,7},{5,6},{6,5},{7,4},{8,11},{9,10},{10,... | collective-permute-start | bytes 7225352 | tf_op jit(solution)/shard_map/ppermute | solution.py:1123
  350.0 32.2 %collective-permute-start.30 = (f16[4,496,384]{2,1,0:T(8,128)(2,1)}, f16[4,496,384]{2,1,0:T(8,128)(2,1)}, u32[]{:S(2)}, u32[]{:S(2)}) collective-permute-start(f16[4,496,384]{2,1,0:T(8,128)(2,1)} %get-tuple-element.169), channel_id=1, source_target_pairs={{0,3},{1,2},{2,1},{3,0},{4,7},{5,6},{6,5},{7,4},{8,11},{9,10},{10,... | collective-permute-start | bytes 4571144 | tf_op jit(solution)/shard_map/ppermute | solution.py:1123
  352.8 36.6 %collective-permute-start.29 = (f16[4,496,384]{2,1,0:T(8,128)(2,1)}, f16[4,496,384]{2,1,0:T(8,128)(2,1)}, u32[]{:S(2)}, u32[]{:S(2)}) collective-permute-start(f16[4,496,384]{2,1,0:T(8,128)(2,1)} %get-tuple-element.168), channel_id=1, source_target_pairs={{0,2},{1,3},{2,0},{3,1},{4,6},{5,7},{6,4},{7,5},{8,10},{9,11},{10,... | collective-permute-start | bytes 4571144 | tf_op jit(solution)/shard_map/ppermute | solution.py:1123
  355.9 35.4 %collective-permute-start.28 = (f16[4,496,384]{2,1,0:T(8,128)(2,1)}, f16[4,496,384]{2,1,0:T(8,128)(2,1)}, u32[]{:S(2)}, u32[]{:S(2)}) collective-permute-start(f16[4,496,384]{2,1,0:T(8,128)(2,1)} %get-tuple-element.167), channel_id=1, source_target_pairs={{0,1},{1,0},{2,3},{3,2},{4,5},{5,4},{6,7},{7,6},{8,9},{9,8},{10,11... | collective-permute-start | bytes 4571144 | tf_op jit(solution)/shard_map/ppermute | solution.py:1123
  371.0 22.1 %copy-start.22 = (f32[4,496,384]{2,1,0:T(8,128)S(1)}, f32[4,496,384]{2,1,0:T(8,128)}, u32[]{:S(2)}) copy-start(f32[4,496,384]{2,1,0:T(8,128)} %get-tuple-element.159) | copy-start | bytes 9142276
  374.3 32.0 %collective-permute-start.36 = (f16[1,784,384]{2,1,0:T(8,128)(2,1)}, f16[1,784,384]{2,1,0:T(8,128)(2,1)}, u32[]{:S(2)}, u32[]{:S(2)}) collective-permute-start(f16[1,784,384]{2,1,0:T(8,128)(2,1)} %get-tuple-element.201), channel_id=1, source_target_pairs={{0,12},{1,13},{2,14},{3,15},{4,8},{5,9},{6,10},{7,11},{8,4},{9,5},... | collective-permute-start | bytes 1806344 | tf_op jit(solution)/shard_map/ppermute | solution.py:1123
  380.3 35.4 %collective-permute-start.35 = (f16[1,784,384]{2,1,0:T(8,128)(2,1)}, f16[1,784,384]{2,1,0:T(8,128)(2,1)}, u32[]{:S(2)}, u32[]{:S(2)}) collective-permute-start(f16[1,784,384]{2,1,0:T(8,128)(2,1)} %get-tuple-element.202), channel_id=1, source_target_pairs={{0,8},{1,9},{2,10},{3,11},{4,12},{5,13},{6,14},{7,15},{8,0},{9,1},... | collective-permute-start | bytes 1806344 | tf_op jit(solution)/shard_map/ppermute | solution.py:1123
  382.3 35.4 %collective-permute-start.34 = (f16[1,784,384]{2,1,0:T(8,128)(2,1)}, f16[1,784,384]{2,1,0:T(8,128)(2,1)}, u32[]{:S(2)}, u32[]{:S(2)}) collective-permute-start(f16[1,784,384]{2,1,0:T(8,128)(2,1)} %get-tuple-element.200), channel_id=1, source_target_pairs={{0,4},{1,5},{2,6},{3,7},{4,0},{5,1},{6,2},{7,3},{8,12},{9,13},{10,... | collective-permute-start | bytes 1806344 | tf_op jit(solution)/shard_map/ppermute | solution.py:1123
  398.3 24.4 %collective-permute-start.33 = (f16[1,496,384]{2,1,0:T(8,128)(2,1)}, f16[1,496,384]{2,1,0:T(8,128)(2,1)}, u32[]{:S(2)}, u32[]{:S(2)}) collective-permute-start(f16[1,496,384]{2,1,0:T(8,128)(2,1)} %get-tuple-element.204), channel_id=1, source_target_pairs={{0,12},{1,13},{2,14},{3,15},{4,8},{5,9},{6,10},{7,11},{8,4},{9,5},... | collective-permute-start | bytes 1142792 | tf_op jit(solution)/shard_map/ppermute | solution.py:1123
  404.3 20.2 %collective-permute-start.32 = (f16[1,496,384]{2,1,0:T(8,128)(2,1)}, f16[1,496,384]{2,1,0:T(8,128)(2,1)}, u32[]{:S(2)}, u32[]{:S(2)}) collective-permute-start(f16[1,496,384]{2,1,0:T(8,128)(2,1)} %get-tuple-element.205), channel_id=1, source_target_pairs={{0,8},{1,9},{2,10},{3,11},{4,12},{5,13},{6,14},{7,15},{8,0},{9,1},... | collective-permute-start | bytes 1142792 | tf_op jit(solution)/shard_map/ppermute | solution.py:1123
  406.3 20.2 %collective-permute-start.31 = (f16[1,496,384]{2,1,0:T(8,128)(2,1)S(1)}, f16[1,496,384]{2,1,0:T(8,128)(2,1)}, u32[]{:S(2)}, u32[]{:S(2)}) collective-permute-start(f16[1,496,384]{2,1,0:T(8,128)(2,1)S(1)} %get-tuple-element.203), channel_id=1, source_target_pairs={{0,4},{1,5},{2,6},{3,7},{4,0},{5,1},{6,2},{7,3},{8,12},{9,13},{10,... | collective-permute-start | bytes 1142792 | tf_op jit(solution)/shard_map/ppermute | solution.py:1123
  434.5 12.6 %copy-start.37 = (f32[1,768]{1,0:T(1,128)S(1)}, f32[1,768]{1,0:T(1,128)}, u32[]{:S(2)}) copy-start(f32[1,768]{1,0:T(1,128)} %get-tuple-element.178) | copy-start | bytes 9220
  434.5 13.9 %copy-start.32 = (f32[1,6912]{1,0:T(1,128)S(1)}, f32[1,6912]{1,0:T(1,128)}, u32[]{:S(2)}) copy-start(f32[1,6912]{1,0:T(1,128)} %get-tuple-element.177) | copy-start | bytes 82948
  434.5 14.1 %copy-start.33 = (f32[1,11520]{1,0:T(1,128)S(1)}, f32[1,11520]{1,0:T(1,128)}, u32[]{:S(2)}) copy-start(f32[1,11520]{1,0:T(1,128)} %get-tuple-element.176) | copy-start | bytes 138244
  434.5 43.6 %all-to-all-start = ((f16[16,136,384]{2,1,0:T(8,128)(2,1)}), f16[16,136,384]{2,1,0:T(8,128)(2,1)S(1)}, u32[]{:S(2)}, u32[]{:S(2)}) async-start(f16[16,136,384]{2,1,0:T(8,128)(2,1)} %select_convert_fusion.9), calls=%async_computation | async-start | bytes 3342336 | tf_op jit(solution)/shard_map/all_to_all | solution.py:1349
  449.5 4.2 collective-permute-start.41
  453.6 4.2 collective-permute-start.42
  456.5 3.7 collective-permute-start.37
  457.9 4.2 collective-permute-start.43
  460.1 5.3 collective-permute-start.38
  462.0 6.9 %collective-permute-start.44 = (f32[11648]{0:T(1024)S(1)}, f32[11648]{0:T(1024)S(1)}, u32[]{:S(2)}, u32[]{:S(2)}) collective-permute-start(f32[11648]{0:T(1024)S(1)} %add.288), channel_id=1, source_target_pairs={{0,8},{1,9},{2,10},{3,11},{4,12},{5,13},{6,14},{7,15},{8,0},{9,1},... | collective-permute-start | bytes 139784 | tf_op jit(solution)/shard_map/ppermute | solution.py:1123
  465.5 3.5 collective-permute-start.39
  469.0 4.4 collective-permute-start.40
  474.2 1.1 collective-permute-start.45
  524.1 83.6 %collective-permute-start.46 = (bf16[5,384,384]{2,1,0:T(8,128)(2,1)}, bf16[5,384,384]{2,1,0:T(8,128)(2,1)S(1)}, u32[]{:S(2)}, u32[]{:S(2)}) collective-permute-start(bf16[5,384,384]{2,1,0:T(8,128)(2,1)} %convert_element_type.365), channel_id=1, source_target_pairs={{0,16},{1,17},{2,18},{3,19},{4,20},{5,21},{6,22},{7,23},{8,24},{9,... | collective-permute-start | bytes 4423688 | tf_op jit(solution)/shard_map/ppermute | solution.py:51
  526.3 2.1 collective-permute-start.47
  591.1 16.7 %copy-start.12 = (f32[1,5,384,384]{3,2,1,0:T(8,128)S(1)}, f32[1,5,384,384]{3,2,1,0:T(8,128)}, u32[]{:S(2)}) copy-start(f32[1,5,384,384]{3,2,1,0:T(8,128)} %param.24) | copy-start | bytes 8847364
  591.1 16.7 %copy-start.15 = (f32[5,384,384]{2,1,0:T(8,128)S(1)}, f32[5,384,384]{2,1,0:T(8,128)}, u32[]{:S(2)}) copy-start(f32[5,384,384]{2,1,0:T(8,128)} %get-tuple-element.180) | copy-start | bytes 8847364
  (16 other events, 68.4 us)

commit v4 on v3

--- a/solution.py
+++ b/solution.py
@@ -356,10 +356,12 @@
     return groups
 
 
-def start_all(groups):
+def start_all(groups, loads):
     for group in groups:
         for copy in group:
             copy.start()
+    for copy in loads:
+        copy.wait()
 
 
 def wait_group(group):
@@ -400,7 +402,7 @@
     keys = k_ref.shape[1]
     masks = head_masks(rows, heads, width)
     factors = as_factors(masks)
-    span = 1 if width // 128 % 2 else 2
+    span = 3 if width // 128 % 3 == 0 else 1
 
     def group(p, carry):
         allowed = [jnp.broadcast_to(valid_ref[i], (rows, keys)) > 0.0 for i in range(images)]
@@ -425,7 +427,7 @@
     key_masks = head_masks(keys, heads, width)
     factors = as_factors(masks)
     scale = 1.0 / math.sqrt(width // heads)
-    span = 1 if width // 128 % 2 else 2
+    span = 3 if width // 128 % 3 == 0 else 1
 
     def group(p, carry):
         allowed = [jnp.broadcast_to(valid_ref[i], (rows, keys)) > 0.0 for i in range(images)]
@@ -484,13 +486,14 @@
 
 
 def encoder_kernel(
-    slots, table, rows_ref, pos_ref, valid_ref, vec_ref,
+    loads, slots, table, rows_ref, pos_ref, valid_ref, vec_ref,
     z_out, e_out, q_out, k_out, v_out, att_out, mid_out, pre_out, hid_out,
     wp, wqkv, wo, w1, w2, acc, sems,
 ):
     vec = Vec(vec_ref, enc_lengths())
     groups = load_blocks(table, slots, sems, 0, enc_shapes(), (wp, wqkv, wo, w1, w2))
-    start_all(groups)
+    start_all((), loads)
+    start_all(groups, ())
     wait_group(groups[0])
     e = mm(rows_ref[...], wp[...]) + vec[0] + pos_ref[...]
     e_out[...] = e
@@ -512,12 +515,13 @@
 
 
 def target_kernel(
-    slots, table, all_ref, pos_all_ref, some_ref, pos_some_ref, valid_ref, vec_ref,
+    loads, slots, table, all_ref, pos_all_ref, some_ref, pos_some_ref, valid_ref, vec_ref,
     out_ref, wp, wqkv, wo, w1, w2, q, k, v, att, acc, sems,
 ):
     vec = Vec(vec_ref, enc_lengths())
     groups = load_blocks(table, slots, sems, 0, enc_shapes(), (wp, wqkv, wo, w1, w2))
-    start_all(groups)
+    start_all((), loads)
+    start_all(groups, ())
     wait_group(groups[0])
     e = mm(all_ref[...], wp[...]) + vec[0] + pos_all_ref[...]
     normed = norm(e, vec[1], vec[2]).astype(bf)
@@ -577,7 +581,7 @@
 
 
 def predictor_kernel(
-    depth, slots, table, z_ref, pos_c_ref, pos_t_ref, valid_ref, tgt_ref, tmask_ref, vec_ref,
+    depth, loads, slots, table, z_ref, pos_c_ref, pos_t_ref, valid_ref, tgt_ref, tmask_ref, vec_ref,
     dz_out, out_0, out_1, out_2, out_3, vec_out, loss_out, top_out,
     win, wqkv, wo, w1, w2, wout, q, k, v, att, go, dq, dk, dv, pre_ref, act_ref, dpre_ref, acc, stage, sems, flow_sems,
 ):
@@ -586,7 +590,7 @@
     flow = Flow((out_0, out_1, out_2, out_3), stage, depth, slots[2 * (NBE + NBP) + 1])
     images = z_ref.shape[0] // LC
     groups = load_blocks(table, slots, sems, NBE, pred_shapes(), (win, wqkv, wo, w1, w2, wout))
-    start_all(groups)
+    start_all(groups, loads)
     for group in groups:
         wait_group(group)
     firsts = offsets([h * b // (edge * edge) for h, b in pred_shapes()])
@@ -722,14 +726,14 @@
 
 
 def feed_back_kernel(
-    depth, slots, table, dz_ref, mid_ref, pre_ref, hid_ref, vec_ref,
+    depth, loads, slots, table, dz_ref, mid_ref, pre_ref, hid_ref, vec_ref,
     out_0, out_1, out_2, out_3, dmid_out, vec_out, top_out,
     w1, w2, act_t, dpre_ref, x_t, low_ref, acc, stage, sems, out_sems,
 ):
     vec, grads = Vec(vec_ref, enc_lengths()), Vec(vec_out, enc_lengths())
     flow = Flow((out_0, out_1, out_2, out_3), None, depth, slots[2 * (NBE + NBP) + 1])
     groups = load_blocks(table, slots, sems, 0, enc_shapes(), (None, None, None, w1, w2))
-    start_all(groups)
+    start_all(groups, loads)
     top_out[...] = jnp.zeros_like(top_out)
     hid = hid_ref[...]
     dy, grads[10], grads[11] = norm_back(hid, vec[10], dz_ref[...].astype(f32))
@@ -763,14 +767,14 @@
 
 
 def attention_back_kernel(
-    depth, slots, table, dmid_ref, rows_ref, e_ref, q, k, v, att_ref, valid_ref, vec_ref,
+    depth, loads, slots, table, dmid_ref, rows_ref, e_ref, q, k, v, att_ref, valid_ref, vec_ref,
     out_0, out_1, out_2, out_3, vec_out, top_out,
     wqkv, wo, go, dq, dk, dv, x_t, dqkv, stage, sems, out_sems,
 ):
     vec, grads = Vec(vec_ref, enc_lengths()), Vec(vec_out, enc_lengths())
     flow = Flow((out_0, out_1, out_2, out_3), None, depth, slots[2 * (NBE + NBP) + 1])
     groups = load_blocks(table, slots, sems, 0, enc_shapes(), (None, wqkv, wo, None, None))
-    start_all(groups[::-1])
+    start_all(groups[::-1], loads)
     top_out[...] = jnp.zeros_like(top_out)
     store = Store(top_out, out_sems)
     dmid = dmid_ref[...]
@@ -838,9 +842,7 @@
                     pltpu.make_async_copy(mine[n_in + place], results[i], sems.at[n_in + place])
                 )
                 results[i] = mine[n_in + place]
-            for copy in loads:
-                copy.wait()
-            body(places_ref, sources, *mine[:n_in], *results, *rest)
+            body(loads, places_ref, sources, *mine[:n_in], *results, *rest)
             for copy in stores:
                 copy.start()
             for copy in stores:

time: 623 us -> 614 us (0.986)
  the two profiles are of different devices: /device:TPU:2 before, /device:TPU:4 now
where the time goes in v4:
time: 614 us; the launch traced here: 607 us
  waiting for transfers between devices  200 us (33%)
  Pallas kernels  194 us (32%)
  starting transfers between devices  91.7 us (15%)
  other arithmetic  57.2 us (9%)
  local copies, waits for them, and re-layouts  32.7 us (5%)
  between operations  19.8 us (3%)
  matrix products  11.2 us (2%)
    ppermute x37, waiting for transfers between devices, trade(): return lax.ppermute(value, ('section', 'dp'), pairs)  182 us
    ppermute x37, starting transfers between devices, trade(): return lax.ppermute(value, ('section', 'dp'), pairs)  75.3 us
    pallas_call x5, Pallas kernels, call_kernel(): pl.pallas_call(guarded, grid_spec=pltpu.PrefetchScalarGridSpec(num_scalar...  69.9 us
    pallas_call x1, Pallas kernels, soap_factor(): pl.pallas_call(factor_kernel, grid_spec=pltpu.PrefetchScalarGridSpec(num_...  64.9 us
    pallas_call x1, Pallas kernels, soap_first(): pl.pallas_call(first_kernel, grid_spec=pltpu.PrefetchScalarGridSpec(num_s...  41.8 us
    convert_element_type x5, other arithmetic, pack(): return marked.astype(WIRE)  19.4 us
    ppermute x4, waiting for transfers between devices, from_behind(): return lax.ppermute(shard, axis, pairs)  17.5 us
    pallas_call x1, Pallas kernels, soap_last(): pl.pallas_call(last_kernel, grid_spec=pltpu.PrefetchScalarGridSpec(num_sc...  16 us
  transfers between devices with their start and end apart: 43, of which 27 were waited for; matrix products, arithmetic and copies ran while one was open for 12% of the time, Pallas kernels for 16%

profile of v4, /device:TPU:4, one launch (start us, length us, event | category | flops | bytes accessed | tf_op | source)
XLA Modules:
  0.0 607.1 jit_solution(968343810394751776)
XLA Ops:
  0.7 2.0 bitcast_convert_fusion.refs_0_
  2.7 1.6 collective-permute-start.6
  4.8 1.6 collective-permute-start.8
  7.1 2.2 multiply_sine_fusion.1
  11.2 2.1 fusion.38
  13.2 2.0 copy.38
  15.3 2.4 fusion.14
  17.7 2.3 fusion.13
  20.0 2.7 fusion.11
  22.7 1.6 fusion.9
  26.5 10.3 %collective-permute-done.6.refs_1_ = bf16[5,384,384]{2,1,0:T(8,128)(2,1)S(1)} collective-permute-done((bf16[5,384,384]{2,1,0:T(8,128)(2,1)S(1)}, bf16[5,384,384]{2,1,0:T(8,128)(2,1)S(1)}, u32[]{:S(2)}, u32[]{:S(2)}) %collective-permute-start.6) | collective-permute-done | bytes 1474592 | tf_op jit(solution)/shard_map/ppermute | solution.py:1125
  38.7 1.7 collective-permute-start.10
  41.7 2.0 pad.26.clone
  45.4 2.6 collective-permute-start.13
  48.0 23.3 %collective-permute-done.9.refs_5_ = bf16[5,384,384]{2,1,0:T(8,128)(2,1)} collective-permute-done((bf16[5,384,384]{2,1,0:T(8,128)(2,1)}, bf16[5,384,384]{2,1,0:T(8,128)(2,1)}, u32[]{:S(2)}, u32[]{:S(2)}) %collective-permute-start.9) | collective-permute-done | bytes 1474592 | tf_op jit(solution)/shard_map/ppermute | solution.py:1125
  76.2 33.7 %collective-permute-done.13.refs_8_ = bf16[5,384,384]{2,1,0:T(8,128)(2,1)S(1)} collective-permute-done((bf16[5,384,384]{2,1,0:T(8,128)(2,1)S(1)}, bf16[5,384,384]{2,1,0:T(8,128)(2,1)S(1)}, u32[]{:S(2)}, u32[]{:S(2)}) %collective-permute-start.13) | collective-permute-done | bytes 1474592 | tf_op jit(solution)/shard_map/ppermute | solution.py:1125
  109.9 1.6 collective-permute-start.14
  112.7 30.4 %collective-permute-done.14.refs_9_ = bf16[5,384,384]{2,1,0:T(8,128)(2,1)S(1)} collective-permute-done((bf16[5,384,384]{2,1,0:T(8,128)(2,1)S(1)}, bf16[5,384,384]{2,1,0:T(8,128)(2,1)S(1)}, u32[]{:S(2)}, u32[]{:S(2)}) %collective-permute-start.14) | collective-permute-done | bytes 1474592 | tf_op jit(solution)/shard_map/ppermute | solution.py:1125
  145.3 1.7 collective-permute-start.18
  148.4 28.3 %collective-permute-done.17.refs_11_ = bf16[5,384,384]{2,1,0:T(8,128)(2,1)S(1)} collective-permute-done((bf16[5,384,384]{2,1,0:T(8,128)(2,1)S(1)}, bf16[5,384,384]{2,1,0:T(8,128)(2,1)S(1)}, u32[]{:S(2)}, u32[]{:S(2)}) %collective-permute-start.17) | collective-permute-done | bytes 1474592 | tf_op jit(solution)/shard_map/ppermute | solution.py:1125
  186.0 5.7 collective-permute-done.22.refs_17_
  192.8 2.2 collective-permute-done.21.refs_16_
  195.0 16.8 %encoder_forward.1 = (bf16[256,768]{1,0:T(8,128)(2,1)}, f32[256,768]{1,0:T(8,128)}, bf16[2,128,768]{2,1,0:T(8,128)(2,1)}, bf16[2,128,768]{2,1,0:T(8,128)(2,1)}, ...) custom-call(s32[138]{0:T(256)} %pad_add_fusion.places_ref, ...), custom_call_target="tpu_custom_call" | custom-call | bytes 75000000 | tf_op jit(solution)/shard_map/encoder_forward/pallas_call | solution.py:851
  216.1 13.4 %predictor_step.1 = (bf16[256,768]{1,0:T(8,128)(2,1)}, f32[4,400,384]{2,1,0:T(8,128)}, f32[4,400,384]{2,1,0:T(8,128)S(1)}, f32[4,400,384]{2,1,0:T(8,128)}, f32[4...) custom-call(s32[138]{0:T(256)} %pad_add_fusion.places_ref, ...), custom_call_target="tpu_custom_call" | custom-call | bytes 150000000 | tf_op jit(solution)/shard_map/predictor_step/pallas_call | solution.py:851
  230.8 16.7 %collective-permute-done.24.refs_18_ = bf16[256,768]{1,0:T(8,128)(2,1)S(1)} collective-permute-done((bf16[256,768]{1,0:T(8,128)(2,1)}, bf16[256,768]{1,0:T(8,128)(2,1)S(1)}, u32[]{:S(2)}, u32[]{:S(2)}) %collective-permute-start.24) | collective-permute-done | bytes 393248 | tf_op jit(solution)/shard_map/ppermute | solution.py:51
  248.3 21.8 %feed_backward.1 = (f32[4,784,384]{2,1,0:T(8,128)}, f32[4,784,384]{2,1,0:T(8,128)}, f32[4,784,384]{2,1,0:T(8,128)}, f32[4,784,384]{2,1,0:T(8,128)}, f32[256,768]...) custom-call(s32[138]{0:T(256)} %pad_add_fusion.places_ref, bf16[5,384,384]{2,1,0:T(8,128)(2,1)} %copy-done.1, ...), custom_call_target="tpu_custom_call" | custom-call | bytes 75000000 | tf_op jit(solution)/shard_map/feed_backward/pallas_call | solution.py:851
  272.3 8.1 %select_convert_fusion.6 = (f16[4,784,384]{2,1,0:T(8,128)(2,1)}, f16[4,784,384]{2,1,0:T(8,128)(2,1)}, f16[4,784,384]{2,1,0:T(8,128)(2,1)}) fusion(f32[4,784,384]{2,1,0:T(8,128)} %get-tuple-element.151, f32[]{:T(128)S(6)} %floor.20, f32[]{:T(128)S(6)} %exp2.253, pred[784]{0:T(1024)(128)(4,1)S(1)} %iota_compare_fusion.9, ...), kind=kLoop, calls=%fused_computation.13 | loop fusion | flops 10838016 | bytes 21676824 | tf_op jit(solution)/shard_map/convert_element_type | solution.py:1140
  280.3 2.4 collective-permute-start.25
  282.8 3.1 collective-permute-start.26
  285.9 3.7 collective-permute-start.27
  289.6 16.5 %attention_backward.1 = (f32[4,496,384]{2,1,0:T(8,128)}, f32[4,496,384]{2,1,0:T(8,128)}, f32[4,496,384]{2,1,0:T(8,128)}, f32[4,496,384]{2,1,0:T(8,128)}, f32[1,11520]{1,0:T(1,128)}, /*index=5*/f32[1,384]{1,0:T(1,128)}) custom-call(s32[138]{0:T(256)} %pad_add_fusion.places_ref, bf16[5,384,384]{2,1,0:T(8,128)(2,1)} %copy-done.1, ...), custom_call_target="tpu_custom_call" | custom-call | bytes 75000000 | tf_op jit(solution)/shard_map/attention_backward/pallas_call | solution.py:851
  308.1 6.6 %select_convert_fusion.10 = (f16[4,496,384]{2,1,0:T(8,128)(2,1)}, f16[4,496,384]{2,1,0:T(8,128)(2,1)}, f16[4,496,384]{2,1,0:T(8,128)(2,1)}) fusion(f32[4,496,384]{2,1,0:T(8,128)} %get-tuple-element.166, f32[]{:T(128)S(6)} %floor.21, f32[]{:T(128)S(6)} %exp2.255, pred[496]{0:T(512)(128)(4,1)S(1)} %iota_compare_fusion.11, ...), kind=kLoop, calls=%fused_computation.18 | loop fusion | flops 6856704 | bytes 13713912 | tf_op jit(solution)/shard_map/convert_element_type | solution.py:1140
  314.7 25.4 %collective-permute-done.26 = f16[4,784,384]{2,1,0:T(8,128)(2,1)} collective-permute-done((f16[4,784,384]{2,1,0:T(8,128)(2,1)}, f16[4,784,384]{2,1,0:T(8,128)(2,1)}, u32[]{:S(2)}, u32[]{:S(2)}) %collective-permute-start.26) | collective-permute-done | bytes 2408480 | tf_op jit(solution)/shard_map/ppermute | solution.py:1125
  340.2 3.9 collective-permute-start.30
  344.1 2.8 collective-permute-start.29
  346.9 2.7 collective-permute-start.28
  355.4 5.6 multiply_add_fusion.1
  361.0 1.7 select_convert_fusion.15
  362.7 1.6 copy-done.13
  364.2 7.0 %collective-permute-start.36 = (f16[1,784,384]{2,1,0:T(8,128)(2,1)}, f16[1,784,384]{2,1,0:T(8,128)(2,1)}, u32[]{:S(2)}, u32[]{:S(2)}) collective-permute-start(f16[1,784,384]{2,1,0:T(8,128)(2,1)} %get-tuple-element.201), channel_id=1, source_target_pairs={{0,12},{1,13},{2,14},{3,15},{4,8},{5,9},{6,10},{7,11},{8,4},{9,5},... | collective-permute-start | bytes 1806344 | tf_op jit(solution)/shard_map/ppermute | solution.py:1125
  371.2 1.9 collective-permute-start.35
  373.2 2.5 collective-permute-start.34
  377.5 1.9 collective-permute-done.29
  383.2 3.2 multiply_add_fusion.2
  388.4 7.0 %collective-permute-start.33 = (f16[1,496,384]{2,1,0:T(8,128)(2,1)}, f16[1,496,384]{2,1,0:T(8,128)(2,1)}, u32[]{:S(2)}, u32[]{:S(2)}) collective-permute-start(f16[1,496,384]{2,1,0:T(8,128)(2,1)} %get-tuple-element.204), channel_id=1, source_target_pairs={{0,12},{1,13},{2,14},{3,15},{4,8},{5,9},{6,10},{7,11},{8,4},{9,5},... | collective-permute-start | bytes 1142792 | tf_op jit(solution)/shard_map/ppermute | solution.py:1125
  395.4 1.9 collective-permute-start.32
  397.4 2.5 collective-permute-start.31
  401.8 4.4 collective-permute-done.35
  410.0 3.1 fusion.5
  418.9 1.5 fusion.8
  423.2 1.8 select_convert_fusion.9
  425.0 11.2 %all-to-all-start = ((f16[16,136,384]{2,1,0:T(8,128)(2,1)}), f16[16,136,384]{2,1,0:T(8,128)(2,1)S(1)}, u32[]{:S(2)}, u32[]{:S(2)}) async-start(f16[16,136,384]{2,1,0:T(8,128)(2,1)} %select_convert_fusion.9), calls=%async_computation | async-start | bytes 3342336 | tf_op jit(solution)/shard_map/all_to_all | solution.py:1351
  442.0 1.9 collective-permute-done.41
  445.3 2.1 collective-permute-start.37
  448.1 2.4 collective-permute-start.43
  452.5 4.9 collective-permute-start.44
  457.7 2.5 collective-permute-done.44
  463.2 2.3 collective-permute-done.40
  470.8 1.8 copy.42
  472.6 41.8 %soap_first.1 = (f32[5,384,384]{2,1,0:T(8,128)}, f32[5,384,384]{2,1,0:T(8,128)}, f32[5,384,384]{2,1,0:T(8,128)}, f32[5,384,384]{2,1,0:T(8,128)}, f32[5,384,384]{...) custom-call(s32[5]{0:T(128)} %get-tuple-element.226.flag, f32[1]{0:T(128)} %bitcast.43.factor, ...), custom_call_target="tpu_custom_call" | custom-call | tf_op jit(solution)/shard_map/soap_first/pallas_call | solution.py:992
  514.5 3.2 convert_element_type.365
  522.6 64.9 %soap_factor.1.q_ref = f32[5,2,384,384]{3,2,1,0:T(8,128)} custom-call(s32[5]{0:T(128)} %get-tuple-element.226.flag, f32[5,2,384,384]{3,2,1,0:T(8,128)} %get-tuple-element.182.base_ref, f32[5,2,384,384]{3,2,1,0:T(8,128)} %get-tuple-element.183.gram_ref), custom_call_target="tpu_custom_call" | custom-call | tf_op jit(solution)/shard_map/soap_factor/pallas_call | solution.py:1006
  587.6 16.0 %soap_last.1 = (f32[5,384,384]{2,1,0:T(8,128)}, f32[5,384,384]{2,1,0:T(8,128)}, f32[5,384,384]{2,1,0:T(8,128)}) custom-call(s32[5]{0:T(128)} %get-tuple-element.226.flag, f32[5,384,384]{2,1,0:T(8,128)} %bitcast.90, f32[5,384,384]{2,1,0:T(8,128)} %bitcast.92, f32[5,384,384]{2,1,0:T(8,128)} %get-tuple-element.181.m_ref, f32[5,2,384,384]{3,2,1,0:T(8,128)} %soap_factor.1.q_ref), custom_call_target="tpu_custom_call" | custom-call | tf_op jit(solution)/shard_map/soap_last/pallas_call | solution.py:1029
  603.6 2.2 select_bitcast_fusion
  (212 shorter events, 74.8 us)
Async XLA Ops:
  2.7 42.7 %copy-start.1 = (bf16[5,384,384]{2,1,0:T(8,128)(2,1)}, bf16[5,384,384]{2,1,0:T(8,128)(2,1)S(1)}, u32[]{:S(2)}) copy-start(bf16[5,384,384]{2,1,0:T(8,128)(2,1)S(1)} %bitcast_convert_fusion.refs_0_) | copy-start | bytes 4423684
  2.7 12.5 %copy-start.36 = (s32[2,4,36]{2,1,0:T(4,128)S(1)}, s32[2,4,36]{2,1,0:T(4,128)}, u32[]{:S(2)}) copy-start(s32[2,4,36]{2,1,0:T(4,128)} %param.21) | copy-start | bytes 3460
  2.7 12.6 %copy-start.35 = (s32[2,128]{1,0:T(2,128)S(1)}, s32[2,128]{1,0:T(2,128)}, u32[]{:S(2)}) copy-start(s32[2,128]{1,0:T(2,128)} %param.19) | copy-start | bytes 3076
  2.7 34.1 %collective-permute-start.6 = (bf16[5,384,384]{2,1,0:T(8,128)(2,1)S(1)}, bf16[5,384,384]{2,1,0:T(8,128)(2,1)S(1)}, u32[]{:S(2)}, u32[]{:S(2)}) collective-permute-start(bf16[5,384,384]{2,1,0:T(8,128)(2,1)S(1)} %bitcast_convert_fusion.refs_0_), channel_id=1, source_target_pairs={{0,1},{1,0},{2,3},{3,2},{4,5},{5,4},{6,7},{7,6},{8,9},{9,8},{10,11... | collective-permute-start | bytes 4423688 | tf_op jit(solution)/shard_map/ppermute | solution.py:1125
  4.3 33.9 %collective-permute-start.7 = (bf16[5,384,384]{2,1,0:T(8,128)(2,1)S(1)}, bf16[5,384,384]{2,1,0:T(8,128)(2,1)}, u32[]{:S(2)}, u32[]{:S(2)}) collective-permute-start(bf16[5,384,384]{2,1,0:T(8,128)(2,1)S(1)} %bitcast_convert_fusion.refs_0_), channel_id=1, source_target_pairs={{0,2},{1,3},{2,0},{3,1},{4,6},{5,7},{6,4},{7,5},{8,10},{9,11},{10,... | collective-permute-start | bytes 4423688 | tf_op jit(solution)/shard_map/ppermute | solution.py:1125
  4.8 33.6 %collective-permute-start.8 = (bf16[5,384,384]{2,1,0:T(8,128)(2,1)S(1)}, bf16[5,384,384]{2,1,0:T(8,128)(2,1)}, u32[]{:S(2)}, u32[]{:S(2)}) collective-permute-start(bf16[5,384,384]{2,1,0:T(8,128)(2,1)S(1)} %bitcast_convert_fusion.refs_0_), channel_id=1, source_target_pairs={{0,4},{1,5},{2,6},{3,7},{4,0},{5,1},{6,2},{7,3},{8,12},{9,13},{10,... | collective-permute-start | bytes 4423688 | tf_op jit(solution)/shard_map/ppermute | solution.py:1125
  20.0 21.0 %copy-start.26 = (f32[1,18432]{1,0:T(1,128)S(1)}, f32[1,18432]{1,0:T(1,128)}, u32[]{:S(2)}) copy-start(f32[1,18432]{1,0:T(1,128)} %param.31) | copy-start | bytes 221188
  36.8 108.5 %copy-start.5 = (bf16[5,384,384]{2,1,0:T(8,128)(2,1)}, bf16[5,384,384]{2,1,0:T(8,128)(2,1)S(1)}, u32[]{:S(2)}) copy-start(bf16[5,384,384]{2,1,0:T(8,128)(2,1)S(1)} %collective-permute-done.6.refs_1_) | copy-start | bytes 4423684
  38.3 32.9 %collective-permute-start.9 = (bf16[5,384,384]{2,1,0:T(8,128)(2,1)}, bf16[5,384,384]{2,1,0:T(8,128)(2,1)}, u32[]{:S(2)}, u32[]{:S(2)}) collective-permute-start(bf16[5,384,384]{2,1,0:T(8,128)(2,1)} %collective-permute-done.8.refs_4_), channel_id=1, source_target_pairs={{0,1},{1,0},{2,3},{3,2},{4,5},{5,4},{6,7},{7,6},{8,9},{9,8},{10,11... | collective-permute-start | bytes 4423688 | tf_op jit(solution)/shard_map/ppermute | solution.py:1125
  38.7 33.0 %collective-permute-start.10 = (bf16[5,384,384]{2,1,0:T(8,128)(2,1)}, bf16[5,384,384]{2,1,0:T(8,128)(2,1)}, u32[]{:S(2)}, u32[]{:S(2)}) collective-permute-start(bf16[5,384,384]{2,1,0:T(8,128)(2,1)} %collective-permute-done.8.refs_4_), channel_id=1, source_target_pairs={{0,2},{1,3},{2,0},{3,1},{4,6},{5,7},{6,4},{7,5},{8,10},{9,11},{10,... | collective-permute-start | bytes 4423688 | tf_op jit(solution)/shard_map/ppermute | solution.py:1125
  44.8 139.2 %copy-start = (s32[68]{0:T(128)S(1)}, s32[68]{0:T(128)}, u32[]{:S(2)}) copy-start(s32[68]{0:T(128)} %slots_ref.1) | copy-start | bytes 820
  45.4 64.5 %collective-permute-start.13 = (bf16[5,384,384]{2,1,0:T(8,128)(2,1)S(1)}, bf16[5,384,384]{2,1,0:T(8,128)(2,1)S(1)}, u32[]{:S(2)}, u32[]{:S(2)}) collective-permute-start(bf16[5,384,384]{2,1,0:T(8,128)(2,1)S(1)} %bitcast_convert_fusion.refs_0_), channel_id=1, source_target_pairs={{0,8},{1,9},{2,10},{3,11},{4,12},{5,13},{6,14},{7,15},{8,0},{9,1},... | collective-permute-start | bytes 4423688 | tf_op jit(solution)/shard_map/ppermute | solution.py:1125
  73.4 36.5 %collective-permute-start.11 = (bf16[5,384,384]{2,1,0:T(8,128)(2,1)}, bf16[5,384,384]{2,1,0:T(8,128)(2,1)S(1)}, u32[]{:S(2)}, u32[]{:S(2)}) collective-permute-start(bf16[5,384,384]{2,1,0:T(8,128)(2,1)} %collective-permute-done.7.refs_2_), channel_id=1, source_target_pairs={{0,1},{1,0},{2,3},{3,2},{4,5},{5,4},{6,7},{7,6},{8,9},{9,8},{10,11... | collective-permute-start | bytes 4423688 | tf_op jit(solution)/shard_map/ppermute | solution.py:1125
  74.7 35.1 %collective-permute-start.12 = (bf16[5,384,384]{2,1,0:T(8,128)(2,1)}, bf16[5,384,384]{2,1,0:T(8,128)(2,1)S(1)}, u32[]{:S(2)}, u32[]{:S(2)}) collective-permute-start(bf16[5,384,384]{2,1,0:T(8,128)(2,1)} %collective-permute-done.9.refs_5_), channel_id=1, source_target_pairs={{0,2},{1,3},{2,0},{3,1},{4,6},{5,7},{6,4},{7,5},{8,10},{9,11},{10,... | collective-permute-start | bytes 4423688 | tf_op jit(solution)/shard_map/ppermute | solution.py:1125
  109.9 69.4 %copy-start.6 = (bf16[5,384,384]{2,1,0:T(8,128)(2,1)}, bf16[5,384,384]{2,1,0:T(8,128)(2,1)S(1)}, u32[]{:S(2)}) copy-start(bf16[5,384,384]{2,1,0:T(8,128)(2,1)S(1)} %collective-permute-done.13.refs_8_) | copy-start | bytes 4423684
  109.9 34.4 %copy-start.7 = (bf16[5,384,384]{2,1,0:T(8,128)(2,1)}, bf16[5,384,384]{2,1,0:T(8,128)(2,1)S(1)}, u32[]{:S(2)}) copy-start(bf16[5,384,384]{2,1,0:T(8,128)(2,1)S(1)} %collective-permute-done.11.refs_3_) | copy-start | bytes 4423684
  109.9 67.9 %copy-start.8 = (bf16[5,384,384]{2,1,0:T(8,128)(2,1)}, bf16[5,384,384]{2,1,0:T(8,128)(2,1)S(1)}, u32[]{:S(2)}) copy-start(bf16[5,384,384]{2,1,0:T(8,128)(2,1)S(1)} %collective-permute-done.12.refs_7_) | copy-start | bytes 4423684
  109.9 33.2 %collective-permute-start.14 = (bf16[5,384,384]{2,1,0:T(8,128)(2,1)S(1)}, bf16[5,384,384]{2,1,0:T(8,128)(2,1)S(1)}, u32[]{:S(2)}, u32[]{:S(2)}) collective-permute-start(bf16[5,384,384]{2,1,0:T(8,128)(2,1)S(1)} %collective-permute-done.13.refs_8_), channel_id=1, source_target_pairs={{0,1},{1,0},{2,3},{3,2},{4,5},{5,4},{6,7},{7,6},{8,9},{9,8},{10,11... | collective-permute-start | bytes 4423688 | tf_op jit(solution)/shard_map/ppermute | solution.py:1125
  111.5 32.8 %collective-permute-start.15 = (bf16[5,384,384]{2,1,0:T(8,128)(2,1)S(1)}, bf16[5,384,384]{2,1,0:T(8,128)(2,1)S(1)}, u32[]{:S(2)}, u32[]{:S(2)}) collective-permute-start(bf16[5,384,384]{2,1,0:T(8,128)(2,1)S(1)} %collective-permute-done.13.refs_8_), channel_id=1, source_target_pairs={{0,2},{1,3},{2,0},{3,1},{4,6},{5,7},{6,4},{7,5},{8,10},{9,11},{10,... | collective-permute-start | bytes 4423688 | tf_op jit(solution)/shard_map/ppermute | solution.py:1125
  112.1 32.6 %collective-permute-start.16 = (bf16[5,384,384]{2,1,0:T(8,128)(2,1)S(1)}, bf16[5,384,384]{2,1,0:T(8,128)(2,1)S(1)}, u32[]{:S(2)}, u32[]{:S(2)}) collective-permute-start(bf16[5,384,384]{2,1,0:T(8,128)(2,1)S(1)} %collective-permute-done.13.refs_8_), channel_id=1, source_target_pairs={{0,4},{1,5},{2,6},{3,7},{4,0},{5,1},{6,2},{7,3},{8,12},{9,13},{10,... | collective-permute-start | bytes 4423688 | tf_op jit(solution)/shard_map/ppermute | solution.py:1125
  143.1 34.7 %copy-start.9 = (bf16[5,384,384]{2,1,0:T(8,128)(2,1)}, bf16[5,384,384]{2,1,0:T(8,128)(2,1)S(1)}, u32[]{:S(2)}) copy-start(bf16[5,384,384]{2,1,0:T(8,128)(2,1)S(1)} %collective-permute-done.14.refs_9_) | copy-start | bytes 4423684
  144.3 33.5 %copy-start.10 = (bf16[5,384,384]{2,1,0:T(8,128)(2,1)}, bf16[5,384,384]{2,1,0:T(8,128)(2,1)S(1)}, u32[]{:S(2)}) copy-start(bf16[5,384,384]{2,1,0:T(8,128)(2,1)S(1)} %collective-permute-done.15.refs_10_) | copy-start | bytes 4423684
  144.6 33.2 %copy-start.11 = (bf16[5,384,384]{2,1,0:T(8,128)(2,1)}, bf16[5,384,384]{2,1,0:T(8,128)(2,1)S(1)}, u32[]{:S(2)}) copy-start(bf16[5,384,384]{2,1,0:T(8,128)(2,1)S(1)} %collective-permute-done.16.refs_12_) | copy-start | bytes 4423684
  144.6 32.0 %collective-permute-start.17 = (bf16[5,384,384]{2,1,0:T(8,128)(2,1)S(1)}, bf16[5,384,384]{2,1,0:T(8,128)(2,1)S(1)}, u32[]{:S(2)}, u32[]{:S(2)}) collective-permute-start(bf16[5,384,384]{2,1,0:T(8,128)(2,1)S(1)} %collective-permute-done.15.refs_10_), channel_id=1, source_target_pairs={{0,1},{1,0},{2,3},{3,2},{4,5},{5,4},{6,7},{7,6},{8,9},{9,8},{10,11... | collective-permute-start | bytes 4423688 | tf_op jit(solution)/shard_map/ppermute | solution.py:1125
  145.3 32.5 %collective-permute-start.18 = (bf16[5,384,384]{2,1,0:T(8,128)(2,1)S(1)}, bf16[5,384,384]{2,1,0:T(8,128)(2,1)S(1)}, u32[]{:S(2)}, u32[]{:S(2)}) collective-permute-start(bf16[5,384,384]{2,1,0:T(8,128)(2,1)S(1)} %collective-permute-done.14.refs_9_), channel_id=1, source_target_pairs={{0,4},{1,5},{2,6},{3,7},{4,0},{5,1},{6,2},{7,3},{8,12},{9,13},{10,... | collective-permute-start | bytes 4423688 | tf_op jit(solution)/shard_map/ppermute | solution.py:1125
  147.0 32.2 %collective-permute-start.19 = (bf16[5,384,384]{2,1,0:T(8,128)(2,1)S(1)}, bf16[5,384,384]{2,1,0:T(8,128)(2,1)S(1)}, u32[]{:S(2)}, u32[]{:S(2)}) collective-permute-start(bf16[5,384,384]{2,1,0:T(8,128)(2,1)S(1)} %collective-permute-done.16.refs_12_), channel_id=1, source_target_pairs={{0,2},{1,3},{2,0},{3,1},{4,6},{5,7},{6,4},{7,5},{8,10},{9,11},{10,... | collective-permute-start | bytes 4423688 | tf_op jit(solution)/shard_map/ppermute | solution.py:1125
  177.8 17.1 %copy-start.2 = (bf16[5,384,384]{2,1,0:T(8,128)(2,1)}, bf16[5,384,384]{2,1,0:T(8,128)(2,1)S(1)}, u32[]{:S(2)}) copy-start(bf16[5,384,384]{2,1,0:T(8,128)(2,1)S(1)} %collective-permute-done.18.refs_13_) | copy-start | bytes 4423684
  179.3 15.7 %copy-start.3 = (bf16[5,384,384]{2,1,0:T(8,128)(2,1)}, bf16[5,384,384]{2,1,0:T(8,128)(2,1)S(1)}, u32[]{:S(2)}) copy-start(bf16[5,384,384]{2,1,0:T(8,128)(2,1)S(1)} %collective-permute-done.19.refs_14_) | copy-start | bytes 4423684
  180.2 12.5 %collective-permute-start.20 = (bf16[2,384,384]{2,1,0:T(8,128)(2,1)}, bf16[2,384,384]{2,1,0:T(8,128)(2,1)S(1)}, u32[]{:S(2)}, u32[]{:S(2)}) collective-permute-start(bf16[2,384,384]{2,1,0:T(8,128)(2,1)} %slice.120), channel_id=1, source_target_pairs={{0,1},{1,0},{2,3},{3,2},{4,5},{5,4},{6,7},{7,6},{8,9},{9,8},{10,11... | collective-permute-start | bytes 1769480 | tf_op jit(solution)/shard_map/ppermute | solution.py:1125
  182.6 12.4 %collective-permute-start.21 = (bf16[2,384,384]{2,1,0:T(8,128)(2,1)}, bf16[2,384,384]{2,1,0:T(8,128)(2,1)}, u32[]{:S(2)}, u32[]{:S(2)}) collective-permute-start(bf16[2,384,384]{2,1,0:T(8,128)(2,1)} %slice.121), channel_id=1, source_target_pairs={{0,2},{1,3},{2,0},{3,1},{4,6},{5,7},{6,4},{7,5},{8,10},{9,11},{10,... | collective-permute-start | bytes 1769480 | tf_op jit(solution)/shard_map/ppermute | solution.py:1125
  184.9 6.8 %collective-permute-start.22 = (bf16[1,384,384]{2,1,0:T(8,128)(2,1)S(1)}, bf16[1,384,384]{2,1,0:T(8,128)(2,1)S(1)}, u32[]{:S(2)}, u32[]{:S(2)}) collective-permute-start(bf16[1,384,384]{2,1,0:T(8,128)(2,1)S(1)} %slice.122), channel_id=1, source_target_pairs={{0,4},{1,5},{2,6},{3,7},{4,0},{5,1},{6,2},{7,3},{8,12},{9,13},{10,... | collective-permute-start | bytes 884744 | tf_op jit(solution)/shard_map/ppermute | solution.py:1125
  211.8 3.5 collective-permute-start.23
  229.5 18.0 %collective-permute-start.24 = (bf16[256,768]{1,0:T(8,128)(2,1)}, bf16[256,768]{1,0:T(8,128)(2,1)S(1)}, u32[]{:S(2)}, u32[]{:S(2)}) collective-permute-start(bf16[256,768]{1,0:T(8,128)(2,1)} %get-tuple-element.135), channel_id=1, source_target_pairs={{16,0},{17,1},{18,2},{19,3},{20,4},{21,5},{22,6},{23,7},{24,8},{25... | collective-permute-start | bytes 1179656 | tf_op jit(solution)/shard_map/ppermute | solution.py:51
  248.3 21.9 %copy-start.17 = (f32[384,384]{1,0:T(8,128)}, f32[384,384]{1,0:T(8,128)S(1)}, u32[]{:S(2)}) copy-start(f32[384,384]{1,0:T(8,128)S(1)} %get-tuple-element.174) | copy-start | bytes 1769476
  280.3 34.4 %collective-permute-start.25 = (f16[4,784,384]{2,1,0:T(8,128)(2,1)}, f16[4,784,384]{2,1,0:T(8,128)(2,1)S(1)}, u32[]{:S(2)}, u32[]{:S(2)}) collective-permute-start(f16[4,784,384]{2,1,0:T(8,128)(2,1)} %get-tuple-element.160), channel_id=1, source_target_pairs={{0,1},{1,0},{2,3},{3,2},{4,5},{5,4},{6,7},{7,6},{8,9},{9,8},{10,11... | collective-permute-start | bytes 7225352 | tf_op jit(solution)/shard_map/ppermute | solution.py:1125
  282.8 57.4 %collective-permute-start.26 = (f16[4,784,384]{2,1,0:T(8,128)(2,1)}, f16[4,784,384]{2,1,0:T(8,128)(2,1)}, u32[]{:S(2)}, u32[]{:S(2)}) collective-permute-start(f16[4,784,384]{2,1,0:T(8,128)(2,1)} %get-tuple-element.161), channel_id=1, source_target_pairs={{0,2},{1,3},{2,0},{3,1},{4,6},{5,7},{6,4},{7,5},{8,10},{9,11},{10,... | collective-permute-start | bytes 7225352 | tf_op jit(solution)/shard_map/ppermute | solution.py:1125
  285.9 54.3 %collective-permute-start.27 = (f16[4,784,384]{2,1,0:T(8,128)(2,1)}, f16[4,784,384]{2,1,0:T(8,128)(2,1)}, u32[]{:S(2)}, u32[]{:S(2)}) collective-permute-start(f16[4,784,384]{2,1,0:T(8,128)(2,1)} %get-tuple-element.162), channel_id=1, source_target_pairs={{0,3},{1,2},{2,1},{3,0},{4,7},{5,6},{6,5},{7,4},{8,11},{9,10},{10,... | collective-permute-start | bytes 7225352 | tf_op jit(solution)/shard_map/ppermute | solution.py:1125
  340.2 33.0 %collective-permute-start.30 = (f16[4,496,384]{2,1,0:T(8,128)(2,1)}, f16[4,496,384]{2,1,0:T(8,128)(2,1)}, u32[]{:S(2)}, u32[]{:S(2)}) collective-permute-start(f16[4,496,384]{2,1,0:T(8,128)(2,1)} %get-tuple-element.169), channel_id=1, source_target_pairs={{0,3},{1,2},{2,1},{3,0},{4,7},{5,6},{6,5},{7,4},{8,11},{9,10},{10,... | collective-permute-start | bytes 4571144 | tf_op jit(solution)/shard_map/ppermute | solution.py:1125
  344.1 35.4 %collective-permute-start.29 = (f16[4,496,384]{2,1,0:T(8,128)(2,1)}, f16[4,496,384]{2,1,0:T(8,128)(2,1)}, u32[]{:S(2)}, u32[]{:S(2)}) collective-permute-start(f16[4,496,384]{2,1,0:T(8,128)(2,1)} %get-tuple-element.168), channel_id=1, source_target_pairs={{0,2},{1,3},{2,0},{3,1},{4,6},{5,7},{6,4},{7,5},{8,10},{9,11},{10,... | collective-permute-start | bytes 4571144 | tf_op jit(solution)/shard_map/ppermute | solution.py:1125
  346.9 34.4 %collective-permute-start.28 = (f16[4,496,384]{2,1,0:T(8,128)(2,1)}, f16[4,496,384]{2,1,0:T(8,128)(2,1)}, u32[]{:S(2)}, u32[]{:S(2)}) collective-permute-start(f16[4,496,384]{2,1,0:T(8,128)(2,1)} %get-tuple-element.167), channel_id=1, source_target_pairs={{0,1},{1,0},{2,3},{3,2},{4,5},{5,4},{6,7},{7,6},{8,9},{9,8},{10,11... | collective-permute-start | bytes 4571144 | tf_op jit(solution)/shard_map/ppermute | solution.py:1125
  361.0 22.3 %copy-start.22 = (f32[4,496,384]{2,1,0:T(8,128)S(1)}, f32[4,496,384]{2,1,0:T(8,128)}, u32[]{:S(2)}) copy-start(f32[4,496,384]{2,1,0:T(8,128)} %get-tuple-element.159) | copy-start | bytes 9142276
  364.2 33.2 %collective-permute-start.36 = (f16[1,784,384]{2,1,0:T(8,128)(2,1)}, f16[1,784,384]{2,1,0:T(8,128)(2,1)}, u32[]{:S(2)}, u32[]{:S(2)}) collective-permute-start(f16[1,784,384]{2,1,0:T(8,128)(2,1)} %get-tuple-element.201), channel_id=1, source_target_pairs={{0,12},{1,13},{2,14},{3,15},{4,8},{5,9},{6,10},{7,11},{8,4},{9,5},... | collective-permute-start | bytes 1806344 | tf_op jit(solution)/shard_map/ppermute | solution.py:1125
  371.2 34.9 %collective-permute-start.35 = (f16[1,784,384]{2,1,0:T(8,128)(2,1)}, f16[1,784,384]{2,1,0:T(8,128)(2,1)}, u32[]{:S(2)}, u32[]{:S(2)}) collective-permute-start(f16[1,784,384]{2,1,0:T(8,128)(2,1)} %get-tuple-element.202), channel_id=1, source_target_pairs={{0,8},{1,9},{2,10},{3,11},{4,12},{5,13},{6,14},{7,15},{8,0},{9,1},... | collective-permute-start | bytes 1806344 | tf_op jit(solution)/shard_map/ppermute | solution.py:1125
  373.2 34.9 %collective-permute-start.34 = (f16[1,784,384]{2,1,0:T(8,128)(2,1)}, f16[1,784,384]{2,1,0:T(8,128)(2,1)}, u32[]{:S(2)}, u32[]{:S(2)}) collective-permute-start(f16[1,784,384]{2,1,0:T(8,128)(2,1)} %get-tuple-element.200), channel_id=1, source_target_pairs={{0,4},{1,5},{2,6},{3,7},{4,0},{5,1},{6,2},{7,3},{8,12},{9,13},{10,... | collective-permute-start | bytes 1806344 | tf_op jit(solution)/shard_map/ppermute | solution.py:1125
  388.4 24.7 %collective-permute-start.33 = (f16[1,496,384]{2,1,0:T(8,128)(2,1)}, f16[1,496,384]{2,1,0:T(8,128)(2,1)}, u32[]{:S(2)}, u32[]{:S(2)}) collective-permute-start(f16[1,496,384]{2,1,0:T(8,128)(2,1)} %get-tuple-element.204), channel_id=1, source_target_pairs={{0,12},{1,13},{2,14},{3,15},{4,8},{5,9},{6,10},{7,11},{8,4},{9,5},... | collective-permute-start | bytes 1142792 | tf_op jit(solution)/shard_map/ppermute | solution.py:1125
  395.4 19.6 %collective-permute-start.32 = (f16[1,496,384]{2,1,0:T(8,128)(2,1)}, f16[1,496,384]{2,1,0:T(8,128)(2,1)}, u32[]{:S(2)}, u32[]{:S(2)}) collective-permute-start(f16[1,496,384]{2,1,0:T(8,128)(2,1)} %get-tuple-element.205), channel_id=1, source_target_pairs={{0,8},{1,9},{2,10},{3,11},{4,12},{5,13},{6,14},{7,15},{8,0},{9,1},... | collective-permute-start | bytes 1142792 | tf_op jit(solution)/shard_map/ppermute | solution.py:1125
  397.4 19.5 %collective-permute-start.31 = (f16[1,496,384]{2,1,0:T(8,128)(2,1)S(1)}, f16[1,496,384]{2,1,0:T(8,128)(2,1)}, u32[]{:S(2)}, u32[]{:S(2)}) collective-permute-start(f16[1,496,384]{2,1,0:T(8,128)(2,1)S(1)} %get-tuple-element.203), channel_id=1, source_target_pairs={{0,4},{1,5},{2,6},{3,7},{4,0},{5,1},{6,2},{7,3},{8,12},{9,13},{10,... | collective-permute-start | bytes 1142792 | tf_op jit(solution)/shard_map/ppermute | solution.py:1125
  424.9 12.5 %copy-start.37 = (f32[1,768]{1,0:T(1,128)S(1)}, f32[1,768]{1,0:T(1,128)}, u32[]{:S(2)}) copy-start(f32[1,768]{1,0:T(1,128)} %get-tuple-element.178) | copy-start | bytes 9220
  424.9 13.8 %copy-start.32 = (f32[1,6912]{1,0:T(1,128)S(1)}, f32[1,6912]{1,0:T(1,128)}, u32[]{:S(2)}) copy-start(f32[1,6912]{1,0:T(1,128)} %get-tuple-element.177) | copy-start | bytes 82948
  424.9 13.9 %copy-start.33 = (f32[1,11520]{1,0:T(1,128)S(1)}, f32[1,11520]{1,0:T(1,128)}, u32[]{:S(2)}) copy-start(f32[1,11520]{1,0:T(1,128)} %get-tuple-element.176) | copy-start | bytes 138244
  425.0 45.2 %all-to-all-start = ((f16[16,136,384]{2,1,0:T(8,128)(2,1)}), f16[16,136,384]{2,1,0:T(8,128)(2,1)S(1)}, u32[]{:S(2)}, u32[]{:S(2)}) async-start(f16[16,136,384]{2,1,0:T(8,128)(2,1)} %select_convert_fusion.9), calls=%async_computation | async-start | bytes 3342336 | tf_op jit(solution)/shard_map/all_to_all | solution.py:1351
  439.8 4.2 collective-permute-start.41
  443.9 4.2 collective-permute-start.42
  445.3 5.1 collective-permute-start.37
  448.1 4.4 collective-permute-start.43
  450.5 7.0 %collective-permute-start.38 = (f32[128]{0:T(128)S(1)}, f32[128]{0:T(128)S(1)}, u32[]{:S(2)}, u32[]{:S(2)}) collective-permute-start(f32[128]{0:T(128)S(1)} %broadcast_add_fusion), channel_id=1, source_target_pairs={{0,2},{1,3},{2,0},{3,1},{4,6},{5,7},{6,4},{7,5},{8,10},{9,11},{10,... | collective-permute-start | bytes 1544 | tf_op jit(solution)/shard_map/ppermute | solution.py:1125
  452.5 7.7 %collective-permute-start.44 = (f32[11648]{0:T(1024)S(1)}, f32[11648]{0:T(1024)S(1)}, u32[]{:S(2)}, u32[]{:S(2)}) collective-permute-start(f32[11648]{0:T(1024)S(1)} %add.288), channel_id=1, source_target_pairs={{0,8},{1,9},{2,10},{3,11},{4,12},{5,13},{6,14},{7,15},{8,0},{9,1},... | collective-permute-start | bytes 139784 | tf_op jit(solution)/shard_map/ppermute | solution.py:1125
  457.5 3.5 collective-permute-start.39
  461.0 4.4 collective-permute-start.40
  466.2 1.1 collective-permute-start.45
  517.7 85.9 %collective-permute-start.46 = (bf16[5,384,384]{2,1,0:T(8,128)(2,1)}, bf16[5,384,384]{2,1,0:T(8,128)(2,1)S(1)}, u32[]{:S(2)}, u32[]{:S(2)}) collective-permute-start(bf16[5,384,384]{2,1,0:T(8,128)(2,1)} %convert_element_type.365), channel_id=1, source_target_pairs={{0,16},{1,17},{2,18},{3,19},{4,20},{5,21},{6,22},{7,23},{8,24},{9,... | collective-permute-start | bytes 4423688 | tf_op jit(solution)/shard_map/ppermute | solution.py:51
  519.8 2.1 collective-permute-start.47
  587.5 16.0 %copy-start.12 = (f32[1,5,384,384]{3,2,1,0:T(8,128)S(1)}, f32[1,5,384,384]{3,2,1,0:T(8,128)}, u32[]{:S(2)}) copy-start(f32[1,5,384,384]{3,2,1,0:T(8,128)} %param.24) | copy-start | bytes 8847364
  587.5 16.0 %copy-start.15 = (f32[5,384,384]{2,1,0:T(8,128)S(1)}, f32[5,384,384]{2,1,0:T(8,128)}, u32[]{:S(2)}) copy-start(f32[5,384,384]{2,1,0:T(8,128)} %get-tuple-element.180) | copy-start | bytes 8847364
  (16 other events, 67.9 us)
